TPU v7x, 32 devices: a whole 2x2x4 slice. The times are simulated.
32 devices in a mesh: leaf: 8 (over z, y), row: 4 (over x, core).
Axes of the slice: x: 2, y: 2, z: 4, core: 2. Of those that a mesh axis runs over, the one named last changes fastest.
Arguments:
- rhs_blocks: float32 [7, 1024, 256], P(None, 'leaf'), may hold values from -6 to 6
- diag_inverse: float32 [7, 1024, 1024], P(None, 'leaf', 'row'), may hold values from -0.1875 to 0.1875
- lower_blocks: float32 [6, 1024, 1024], P(None, 'leaf', 'row'), may hold values from -0.09375 to 0.09375
- update_rows: int32 [6, 1024], P(None, 'leaf'), may hold values from 512 to 895, as said below
Outputs:
- solution: float32 [7, 1024, 256], P(None, 'leaf')
Inputs may be any that keep to these rules, and one draw needn't show every extreme that they name: update_rows[s, m] = a * 128 + c names column i * 128 + c of an ancestor a of supernode s, where i = m // 128; the 128 entries of one supernode with the same i are distinct.
All inputs are finite; a program needn't handle non-finite values.
Results may differ from a plain program's by a relative error of at most 0.0001.
Values sent between devices are 32-bit elements; how exact they have to be, the bound alone decides.
No kernel may reach another device: no remote copies, remote signals or barrier semaphores. Data moves between devices by JAX's collectives and lax.ppermute only.
A program may use at most 64 MiB of HBM per device.

v0:
```python
import jax
import jax.numpy as jnp
from jax import lax
from jax.sharding import PartitionSpec as P


def local(rhs_blocks, diag_inverse, lower_blocks, update_rows):
    leaf_count = lax.axis_size("leaf")
    node_total = rhs_blocks.shape[0]
    panel_rows = rhs_blocks.shape[1]
    rhs_width = rhs_blocks.shape[2]
    level_total = (node_total + 1).bit_length() - 1
    slice_rows = diag_inverse.shape[2] // leaf_count
    current = rhs_blocks.reshape(node_total * panel_rows, rhs_width)
    stored_slices = [None] * level_total
    for depth_level in range(level_total - 1, -1, -1):
        first_node = 2**level_total - 2 ** (depth_level + 1)
        node_count = 2**depth_level
        stop_node = first_node + node_count
        diag_part = diag_inverse[first_node:stop_node]
        lower_part = lower_blocks[first_node:stop_node] if depth_level > 0 else None
        local_rhs = current[first_node * panel_rows : stop_node * panel_rows].reshape(
            node_count, panel_rows, rhs_width
        )
        partial_value = jnp.einsum(
            "scr,sct->rst", diag_part, local_rhs, precision=lax.Precision.HIGHEST
        )
        complete = lax.psum(partial_value, "leaf")
        stored = lax.dynamic_slice_in_dim(
            complete, lax.axis_index("leaf") * slice_rows, slice_rows, 0
        )
        if depth_level > 0:
            update = jnp.einsum(
                "smr,rst->smt", lower_part, complete, precision=lax.Precision.HIGHEST
            )
        stored_slices[depth_level] = stored
        if depth_level > 0:
            update = lax.psum(update, "row")
            targets = update_rows[first_node:stop_node].reshape(-1)
            current = current.at[targets].add(-update.reshape(-1, rhs_width))
    answer = jnp.zeros((node_total * panel_rows, rhs_width), jnp.float32)
    for depth_level in range(level_total):
        first_node = 2**level_total - 2 ** (depth_level + 1)
        node_count = 2**depth_level
        stop_node = first_node + node_count
        diag_part = diag_inverse[first_node:stop_node]
        residual = stored_slices[depth_level]
        if depth_level > 0:
            lower_part = lower_blocks[first_node:stop_node]
            targets = update_rows[first_node:stop_node].reshape(-1)
            known = answer[targets].reshape(node_count, panel_rows, rhs_width)
            residual = residual - lax.psum_scatter(
                jnp.einsum("smr,smt->rst", lower_part, known, precision=lax.Precision.HIGHEST),
                "leaf",
                scatter_dimension=0,
                tiled=True,
            )
        partial_value = jnp.einsum(
            "scr,rst->sct",
            diag_part,
            lax.all_gather(residual, "leaf", axis=0, tiled=True),
            precision=lax.Precision.HIGHEST,
        )
        solved = lax.psum(partial_value, "row")
        answer = answer.at[first_node * panel_rows : stop_node * panel_rows].set(
            solved.reshape(-1, rhs_width)
        )
    return answer.reshape(node_total, panel_rows, rhs_width)


def solution(mesh):
    placed = (
        P(None, "leaf", None),
        P(None, "leaf", "row"),
        P(None, "leaf", "row"),
        P(None, "leaf"),
    )
    return jax.shard_map(
        local, mesh=mesh, in_specs=placed, out_specs=P(None, "leaf", None), check_vma=False
    )
```

profile of v0, /device:TPU:0, one launch (start us, length us, event | category | flops | bytes accessed | tf_op | source)
XLA Modules:
  0.0 698.2 jit_solution(705623157416841822)
XLA Ops:
  8.0 2.0 convolution_bitcast_fusion.1
  10.1 81.5 %all-reduce.14.cloned.1.call-done = f32[256,4,256]{2,0,1:T(8,128)} async-done(((f32[256,4,256]{2,0,1:T(8,128)}), f32[256,4,256]{2,0,1:T(8,128)}) %all-reduce.14.cloned.1.call-update) | async-done | bytes 1048592 | tf_op jit(solution)/shard_map/psum | solution.py:28
  91.6 3.9 convolution_bitcast_fusion.4
  96.2 32.2 %all-reduce.16.cloned.1.call-done = f32[4,128,256]{1,2,0:T(8,128)} async-done(((f32[4,128,256]{1,2,0:T(8,128)}), f32[4,128,256]{1,2,0:T(8,128)}) %all-reduce.16.cloned.1.call-update) | async-done | bytes 524304 | tf_op jit(solution)/shard_map/psum | solution.py:38
  128.4 1.9 neg.12
  131.6 3.7 scatter_fusion
  137.4 71.9 %all-reduce.18.cloned.1.call-done = f32[256,2,256]{2,0,1:T(8,128)} async-done(((f32[256,2,256]{2,0,1:T(8,128)}), f32[256,2,256]{2,0,1:T(8,128)}) %all-reduce.18.cloned.1.call-update) | async-done | bytes 524304 | tf_op jit(solution)/shard_map/psum | solution.py:28
  209.3 2.8 convolution_bitcast_fusion.5
  212.1 31.3 %all-reduce.20.cloned.1.call-done = f32[2,128,256]{1,2,0:T(8,128)} async-done(((f32[2,128,256]{1,2,0:T(8,128)}), f32[2,128,256]{1,2,0:T(8,128)}) %all-reduce.20.cloned.1.call-update) | async-done | bytes 262160 | tf_op jit(solution)/shard_map/psum | solution.py:38
  244.6 2.3 scatter_fusion.1
  248.1 70.6 %all-reduce.22.cloned.1.call-done = f32[256,1,256]{0,2,1:T(8,128)} async-done(((f32[256,1,256]{0,2,1:T(8,128)}), f32[256,1,256]{0,2,1:T(8,128)}) %all-reduce.22.cloned.1.call-update) | async-done | bytes 262160 | tf_op jit(solution)/shard_map/psum | solution.py:28
  319.8 30.8 %all_gather.9 = f32[256,1,256]{2,1,0:T(1,128)S(1)} all-gather(f32[32,1,256]{2,1,0:T(1,128)S(1)} %copy.52), channel_id=1, replica_groups=mesh['leaf'=8,'row'=4] {'leaf'}, dimensions={0}, use_global_device_ids=true | all-gather | bytes 294912 | tf_op jit(solution)/shard_map/all_gather | solution.py:61
  352.0 30.8 %all-reduce.24.cloned.1.call-done = f32[128,256]{0,1:T(8,128)} async-done(((f32[128,256]{0,1:T(8,128)}), f32[128,256]{0,1:T(8,128)}) %all-reduce.24.cloned.1.call-update) | async-done | bytes 131088 | tf_op jit(solution)/shard_map/psum | solution.py:64
  384.1 1.7 gather_fusion
  385.7 1.6 convolution_bitcast_fusion.2
  390.3 70.6 %all-reduce.30.cloned.1.call-done = f32[256,2,256]{2,1,0:T(2,128)} async-done(((f32[256,2,256]{2,1,0:T(2,128)}), f32[256,2,256]{2,1,0:T(2,128)}) %all-reduce.30.cloned.1.call-update) | async-done | bytes 524304
  462.6 31.8 %all_gather.10 = f32[256,2,256]{2,1,0:T(2,128)S(1)} all-gather(f32[32,2,256]{2,1,0:T(2,128)S(1)} %copy.57), channel_id=1, replica_groups=mesh['leaf'=8,'row'=4] {'leaf'}, dimensions={0}, use_global_device_ids=true | all-gather | bytes 589824 | tf_op jit(solution)/shard_map/all_gather | solution.py:61
  495.8 31.2 %all-reduce.26.cloned.1.call-done = f32[256,256]{0,1:T(8,128)} async-done(((f32[256,256]{0,1:T(8,128)}), f32[256,256]{0,1:T(8,128)}) %all-reduce.26.cloned.1.call-update) | async-done | bytes 262160 | tf_op jit(solution)/shard_map/psum | solution.py:64
  528.3 1.6 gather_fusion.1
  529.8 2.1 convolution_bitcast_fusion
  533.3 78.3 %all-reduce.32.cloned.1.call-done = f32[256,4,256]{2,1,0:T(4,128)} async-done(((f32[256,4,256]{2,1,0:T(4,128)}), f32[256,4,256]{2,1,0:T(4,128)}) %all-reduce.32.cloned.1.call-update) | async-done | bytes 1048592
  614.3 39.8 %all-gather.2.cloned.1.call-done = f32[256,4,256]{2,1,0:T(4,128)} async-done(((f32[32,4,256]{2,1,0:T(4,128)}), f32[256,4,256]{2,1,0:T(4,128)}) %all-gather.2.cloned.1.call-update) | async-done | bytes 1048592 | tf_op jit(solution)/shard_map/all_gather | solution.py:61
  654.1 2.1 fusion
  657.3 32.1 %all-reduce.28.cloned.1.call-done = f32[512,256]{0,1:T(8,128)} async-done(((f32[512,256]{0,1:T(8,128)}), f32[512,256]{0,1:T(8,128)}) %all-reduce.28.cloned.1.call-update) | async-done | bytes 524304 | tf_op jit(solution)/shard_map/psum | solution.py:64
  (67 shorter events, 25.6 us)
Async XLA Ops:
  6.5 1.5 copy-start
  6.5 85.1 %all-reduce.14.cloned.1.call-start = ((), (), s32[]{:S(2)}) async-start(), calls=%async_computation | async-start | bytes 2097152 | tf_op jit(solution)/shard_map/psum | solution.py:28
  10.0 81.6 %copy-start.2 = (f32[6,128,256]{2,1,0:T(8,128)S(1)}, f32[6,128,256]{2,1,0:T(8,128)}, u32[]{:S(2)}) copy-start(f32[6,128,256]{2,1,0:T(8,128)} %param.12) | copy-start | bytes 2359300
  10.1 118.4 %all-reduce.16.cloned.1.call-start = ((), (), s32[]{:S(2)}) async-start(), calls=%async_computation.1 | async-start | bytes 1048576 | tf_op jit(solution)/shard_map/psum | solution.py:38
  95.5 0.7 slice-start
  95.5 113.7 %all-reduce.18.cloned.1.call-start = ((), (), s32[]{:S(2)}) async-start(), calls=%async_computation.2 | async-start | bytes 1048576 | tf_op jit(solution)/shard_map/psum | solution.py:28
  136.7 0.7 copy-start.3
  136.7 106.8 %all-reduce.20.cloned.1.call-start = ((), (), s32[]{:S(2)}) async-start(), calls=%async_computation.3 | async-start | bytes 524288 | tf_op jit(solution)/shard_map/psum | solution.py:38
  212.1 106.7 %all-reduce.22.cloned.1.call-start = ((), (), s32[]{:S(2)}) async-start(), calls=%async_computation.4 | async-start | bytes 524288 | tf_op jit(solution)/shard_map/psum | solution.py:28
  248.0 134.7 %all-reduce.24.cloned.1.call-start = ((), (), s32[]{:S(2)}) async-start(), calls=%async_computation.5 | async-start | bytes 262144 | tf_op jit(solution)/shard_map/psum | solution.py:64
  351.9 108.9 %all-reduce.30.cloned.1.call-start = ((), (), s32[]{:S(2)}) async-start(), calls=%async_computation.9 | async-start | bytes 1048576
  388.3 138.7 %all-reduce.26.cloned.1.call-start = ((), (), s32[]{:S(2)}) async-start(), calls=%async_computation.6 | async-start | bytes 524288 | tf_op jit(solution)/shard_map/psum | solution.py:64
  388.4 0.7 copy-start.4
  495.7 115.9 %all-reduce.32.cloned.1.call-start = ((), (), s32[]{:S(2)}) async-start(), calls=%async_computation.10 | async-start | bytes 2097152
  533.2 120.9 %copy-start.1 = (f32[7,128,256]{2,1,0:T(8,128)S(1)}, f32[7,128,256]{2,1,0:T(8,128)}, u32[]{:S(2)}) copy-start(f32[7,128,256]{2,1,0:T(8,128)} %param.11) | copy-start | bytes 2752516
  533.3 120.9 %all-gather.2.cloned.1.call-start = ((), (), s32[]{:S(2)}) async-start(), calls=%async_computation.7 | async-start | bytes 1179648 | tf_op jit(solution)/shard_map/all_gather | solution.py:61
  614.2 75.1 %all-reduce.28.cloned.1.call-start = ((), (), s32[]{:S(2)}) async-start(), calls=%async_computation.8 | async-start | bytes 1048576 | tf_op jit(solution)/shard_map/psum | solution.py:64
Sparse Core Ops, SparseCore 0:
  10.9 80.7 all-reduce.13
  95.6 32.7 all-reduce.15
  136.8 72.3 all-reduce.17
  212.2 31.2 all-reduce.19
  248.2 70.5 all-reduce.21
  352.0 30.6 all-reduce.23
  388.4 72.3 all-reduce.29
  495.8 31.1 all-reduce.25
  533.4 78.1 all-reduce.31
  614.4 39.7 all-gather.1
  657.4 31.8 all-reduce.27
where the time goes:
time: 699 us; the launch traced here: 698 us
  waiting for transfers between devices  571 us (82%)
  blocking collectives  62.6 us (9%)
  local copies, waits for them, and re-layouts  21.2 us (3%)
  matrix products  18.7 us (3%)
  between operations  14.1 us (2%)
  other arithmetic  10.6 us (2%)
    psum x3, waiting for transfers between devices, local(): complete = lax.psum(partial_value, 'leaf')  224 us
    unnamed x13, waiting for transfers between devices  149 us
    psum x3, waiting for transfers between devices, local(): solved = lax.psum(partial_value, 'row')  94.1 us
    psum x2, waiting for transfers between devices, local(): update = lax.psum(update, 'row')  63.6 us
    all_gather x2, blocking collectives, local(): lax.all_gather(residual, 'leaf', axis=0, tiled=True)  62.6 us
    all_gather x1, waiting for transfers between devices, local(): lax.all_gather(residual, 'leaf', axis=0, tiled=True)  39.8 us
  transfers between devices with their start and end apart: 11, of which 11 were waited for; matrix products, arithmetic and copies ran while one was open for 0% of the time, Pallas kernels for 0%

commit v1 on v0

v1 whole, which is shorter than its diff:
```python
import jax
import jax.numpy as jnp
from jax import lax
from jax.sharding import PartitionSpec as P

AXES = ("leaf", "row")
PRECISION = lax.Precision.HIGHEST


def dot(left, right, dims):
    return lax.dot_general(
        left, right, (dims, ((), ())), precision=PRECISION, preferred_element_type=jnp.float32
    )


def local(rhs_blocks, diag_inverse, lower_blocks, update_rows):
    leaf_count = lax.axis_size("leaf")
    row_count = lax.axis_size("row")
    node_total, panel, width = rhs_blocks.shape
    piece = diag_inverse.shape[2]
    levels = (node_total + 1).bit_length() - 1
    planes = 2 ** (levels - 1)
    inner = leaf_count // planes
    cross = row_count // 2
    half = width // 2
    group = half // planes
    first = [2**levels - 2 ** (d + 1) for d in range(levels)]
    shift = [levels - 1 - d for d in range(levels)]

    leaf_index = lax.axis_index("leaf")
    plane = leaf_index // inner
    core = lax.axis_index("row") % 2

    def move(x, plane_mask=0, inner_mask=0, cross_mask=0, core_mask=0):
        pairs = []
        for leaf in range(leaf_count):
            for row in range(row_count):
                other_leaf = leaf ^ (plane_mask * inner + inner_mask)
                other_row = row ^ (cross_mask * 2 + core_mask)
                pairs.append((leaf * row_count + row, other_leaf * row_count + other_row))
        return lax.ppermute(x, AXES, pairs)

    def inner_sum(x):
        mask = 1
        while mask < inner:
            x = x + move(x, inner_mask=mask)
            mask *= 2
        return x

    def cross_sum(x, plane_mask=0):
        parts = [
            move(x, plane_mask=plane_mask, cross_mask=m) if m or plane_mask else x
            for m in range(cross)
        ]
        while len(parts) > 1:
            parts = [parts[i] + parts[i + 1] for i in range(0, len(parts), 2)]
        return parts[0]

    def reverse(mask):
        return sum(((mask >> b) & 1) << (levels - 2 - b) for b in range(levels - 1))

    def reorder(x, mask):
        parts = [x[:, (o ^ mask) * panel : ((o ^ mask) + 1) * panel] for o in range(planes)]
        return jnp.concatenate(parts, axis=1)

    def regroup(x, mask):
        if mask == 0:
            return x
        count = x.shape[0] // group
        g = reverse(mask)
        return jnp.concatenate(
            [x[(i ^ g) * group : ((i ^ g) + 1) * group] for i in range(count)], axis=0
        )

    def pick(array, index):
        return lax.dynamic_index_in_dim(array, index, 0, keepdims=False)

    def gather_node(blocks, depth):
        parts = []
        for o in range(planes):
            node = first[depth] + ((plane ^ o) >> shift[depth])
            block = pick(blocks, node)
            parts.append(block if o == 0 else move(block, plane_mask=o))
        own = jnp.concatenate(parts, axis=0)
        return own

    def pair_core(own):
        return jnp.concatenate([own, move(own, core_mask=1)], axis=1)

    flipped = jnp.swapaxes(
        lax.dynamic_slice_in_dim(rhs_blocks, core * half, half, 2), 1, 2
    ).reshape(node_total, planes, group, panel)
    own_group = sum(((plane >> b) & 1) << (levels - 2 - b) for b in range(levels - 1))
    columns = jnp.stack(
        [lax.dynamic_index_in_dim(flipped, own_group ^ g, 1, keepdims=False) for g in range(planes)],
        axis=1,
    )
    right_parts = []
    for o in range(planes):
        g = reverse(o)
        pieces = []
        for depth in range(levels - 1, -1, -1):
            node = first[depth] + ((plane ^ o) >> shift[depth])
            mine = pick(columns, node)
            for i in range(2**depth):
                pieces.append(mine[i ^ g])
        packed = jnp.concatenate(pieces, axis=0)
        right_parts.append(packed if o == 0 else move(packed, plane_mask=o))
    right = [None] * levels
    start = 0
    for depth in range(levels - 1, -1, -1):
        size = group * 2**depth
        right[depth] = jnp.concatenate([p[start : start + size] for p in right_parts], axis=1)
        start += size

    diag = [None] * levels
    lower = [None] * levels
    for depth in range(levels - 1, -1, -1):
        diag[depth] = pair_core(gather_node(diag_inverse, depth))
        if depth > 0:
            tagged = jnp.concatenate(
                [
                    lower_blocks[first[depth] : first[depth] + 2**depth],
                    jnp.pad(
                        update_rows[first[depth] : first[depth] + 2**depth, None, :].astype(jnp.float32),
                        ((0, 0), (0, 7), (0, piece - panel)),
                    ),
                ],
                axis=1,
            )
            parts = []
            for o in range(planes):
                block = pick(tagged, (plane ^ o) >> shift[depth])
                parts.append(block if o == 0 else move(block, plane_mask=o))
            own = jnp.stack(parts)
            both = jnp.concatenate([own, move(own, core_mask=1)], axis=2)
            body = both[:, :panel]
            names = both[:, panel, :panel]
            lower[depth] = []
            for up in range(depth):
                base = (first[up] + (plane >> shift[up])) * panel
                spots = (base + jnp.arange(panel, dtype=jnp.int32)).astype(jnp.float32)
                chosen = (names[:, None, :] == spots[None, :, None]).astype(jnp.float32)
                lower[depth].append(
                    jnp.einsum("otm,omr->otr", chosen, body, precision=lax.Precision.HIGHEST).reshape(
                        planes * panel, 2 * piece
                    )
                )

    forward = [None] * levels
    pending = [None] * levels
    work = right[levels - 1]
    for depth in range(levels - 1, -1, -1):
        forward[depth] = inner_sum(dot(work, diag[depth], ((1,), (0,))))
        if depth == 0:
            break
        keep = work.shape[0] // 2
        mask = 1 << shift[depth]
        for up in range(depth - 1, -1, -1):
            update = dot(forward[depth], lower[depth][up], ((1,), (1,)))
            if pending[up] is not None:
                update = update + pending[up]
            mine, theirs = update[:keep], reorder(update[keep:], mask)
            if up == depth - 1:
                work = right[up] - (cross_sum(mine) + cross_sum(theirs, mask))
            else:
                pending[up] = mine + move(theirs, plane_mask=mask)

    answer = [None] * levels
    for depth in range(levels):
        residual = forward[depth]
        if depth > 0:
            known = sum(dot(answer[up], lower[depth][up], ((1,), (0,))) for up in range(depth))
            residual = residual - inner_sum(known)
        partial_value = dot(residual, diag[depth], ((1,), (1,)))
        if depth < levels - 1:
            mask = 1 << shift[depth + 1]
            for up in range(depth):
                answer[up] = jnp.concatenate(
                    [answer[up], move(reorder(answer[up], mask), plane_mask=mask)], axis=0
                )
            answer[depth] = jnp.concatenate(
                [cross_sum(partial_value), cross_sum(reorder(partial_value, mask), mask)], axis=0
            )
        else:
            answer[depth] = cross_sum(partial_value)

    collected = [None] * node_total
    for depth in range(levels):
        for s in range(2**depth):
            o = s << shift[depth]
            block = answer[depth][:, o * panel : (o + 1) * panel]
            if o:
                block = move(regroup(block, o), plane_mask=o)
            collected[first[depth] + s] = block
    relative = jnp.stack(collected)
    other = move(relative, core_mask=1)
    both = jnp.where(core == 0, jnp.stack([relative, other]), jnp.stack([other, relative]))
    ordered = []
    for depth in range(levels - 1, -1, -1):
        for n in range(2**depth):
            node = first[depth] + (n ^ (plane >> shift[depth]))
            mine = lax.dynamic_index_in_dim(both, node, 1, keepdims=False).reshape(
                2, planes, group, panel
            )
            ordered.append(
                jnp.concatenate(
                    [lax.dynamic_index_in_dim(mine, own_group ^ g, 1, keepdims=False) for g in range(planes)],
                    axis=1,
                ).reshape(width, panel)
            )
    return jnp.swapaxes(jnp.stack(ordered), 1, 2)


def solution(mesh):
    placed = (
        P(None, "leaf", None),
        P(None, "leaf", "row"),
        P(None, "leaf", "row"),
        P(None, "leaf"),
    )
    return jax.shard_map(
        local, mesh=mesh, in_specs=placed, out_specs=P(None, "leaf", None), check_vma=False
    )
```

time: 699 us -> 186 us (0.27)
  waiting for transfers between devices: 571 us -> 69.5 us
  starting transfers between devices: 0.42 us -> 74.5 us
  blocking collectives: 62.6 us -> 0 us
  between operations: 14.1 us -> 0.97 us
    psum x8 -> x0, waiting for transfers between devices: 382 us -> none  [the longest x3 224 us: local(): complete = lax.psum(partial_value, 'leaf')]
    unnamed x13 -> x0, waiting for transfers between devices: 149 us -> none
    ppermute x0 -> x48, starting transfers between devices: none -> 74.5 us  [move(): return lax.ppermute(x, AXES, pairs)]
    ppermute x0 -> x48, waiting for transfers between devices: none -> 69.5 us  [move(): return lax.ppermute(x, AXES, pairs)]
    all_gather x2 -> x0, blocking collectives: 62.6 us -> none  [local(): lax.all_gather(residual, 'leaf', axis=0, tiled=True)]
    all_gather x1 -> x0, waiting for transfers between devices: 39.8 us -> none  [local(): lax.all_gather(residual, 'leaf', axis=0, tiled=True)]
    dot_general x10 -> x15, matrix products: 18.7 us -> 15.3 us  [the longest x12 13.1 us: dot(): lax.dot_general(left, right, (dims, ((), ())), precision=PRECISION, prefe...]
  transfers between devices with their start and end apart: 11 -> 48, of which waited for: 11 -> 26; matrix products, arithmetic and copies ran while one was open for 0% -> 8% of each run, Pallas kernels for 0% -> 0%
where the time goes in v1:
time: 186 us; the launch traced here: 185 us
  starting transfers between devices  74.5 us (40%)
  waiting for transfers between devices  69.5 us (37%)
  local copies, waits for them, and re-layouts  20.1 us (11%)
  matrix products  15.3 us (8%)
  other arithmetic  4.91 us (3%)
    ppermute x48, starting transfers between devices, move(): return lax.ppermute(x, AXES, pairs)  74.5 us
    ppermute x48, waiting for transfers between devices, move(): return lax.ppermute(x, AXES, pairs)  69.5 us
    dot_general x12, matrix products, dot(): lax.dot_general(left, right, (dims, ((), ())), precision=PRECISION, prefe...  13.1 us
    unnamed x49, local copies, waits for them, and re-layouts  8.48 us
  transfers between devices with their start and end apart: 48, of which 26 were waited for; matrix products, arithmetic and copies ran while one was open for 8% of the time, Pallas kernels for 0%

profile of v1, /device:TPU:0, one launch (start us, length us, event | category | flops | bytes accessed | tf_op | source)
XLA Modules:
  0.0 185.3 jit_solution(13041509440393776266)
XLA Ops:
  6.5 3.0 %collective-permute-start = (f32[224,128]{1,0:T(8,128)}, f32[224,128]{1,0:T(8,128)S(1)}, u32[]{:S(2)}, u32[]{:S(2)}) collective-permute-start(f32[224,128]{1,0:T(8,128)} %get-tuple-element.35), channel_id=1, source_target_pairs={{0,8},{1,9},{2,10},{3,11},{4,12},{5,13},{6,14},{7,15},{8,0},{9,1},... | collective-permute-start | bytes 344072 | tf_op jit(solution)/shard_map/ppermute | solution.py:41
  10.7 2.6 %collective-permute-start.1 = (f32[224,128]{1,0:T(8,128)}, f32[224,128]{1,0:T(8,128)}, u32[]{:S(2)}, u32[]{:S(2)}) collective-permute-start(f32[224,128]{1,0:T(8,128)} %get-tuple-element.47), channel_id=1, source_target_pairs={{0,16},{1,17},{2,18},{3,19},{4,20},{5,21},{6,22},{7,23},{8,24},{9,... | collective-permute-start | bytes 344072 | tf_op jit(solution)/shard_map/ppermute | solution.py:41
  22.4 7.1 %collective-permute-done.2 = f32[224,128]{1,0:T(8,128)S(1)} collective-permute-done((f32[224,128]{1,0:T(8,128)}, f32[224,128]{1,0:T(8,128)S(1)}, u32[]{:S(2)}, u32[]{:S(2)}) %collective-permute-start.2) | collective-permute-done | bytes 114720 | tf_op jit(solution)/shard_map/ppermute | solution.py:41
  30.2 2.7 %collective-permute-start.10 = (f32[136,256]{1,0:T(8,128)S(1)}, f32[136,256]{1,0:T(8,128)S(1)}, u32[]{:S(2)}, u32[]{:S(2)}) collective-permute-start(f32[136,256]{1,0:T(8,128)S(1)} %get-tuple-element.25), channel_id=1, source_target_pairs={{0,24},{1,25},{2,26},{3,27},{4,28},{5,29},{6,30},{7,31},{8,16},{9,... | collective-permute-start | bytes 417800 | tf_op jit(solution)/shard_map/ppermute | solution.py:41
  32.9 7.8 %collective-permute-start.9 = (f32[136,256]{1,0:T(8,128)S(1)}, f32[136,256]{1,0:T(8,128)S(1)}, u32[]{:S(2)}, u32[]{:S(2)}) collective-permute-start(f32[136,256]{1,0:T(8,128)S(1)} %get-tuple-element.26), channel_id=1, source_target_pairs={{0,16},{1,17},{2,18},{3,19},{4,20},{5,21},{6,22},{7,23},{8,24},{9,... | collective-permute-start | bytes 417800 | tf_op jit(solution)/shard_map/ppermute | solution.py:41
  40.9 2.4 %collective-permute-start.17 = (f32[128,256]{1,0:T(8,128)}, f32[128,256]{1,0:T(8,128)S(1)}, u32[]{:S(2)}, u32[]{:S(2)}) collective-permute-start(f32[128,256]{1,0:T(8,128)} %get-tuple-element.14), channel_id=1, source_target_pairs={{0,24},{1,25},{2,26},{3,27},{4,28},{5,29},{6,30},{7,31},{8,16},{9,... | collective-permute-start | bytes 393224 | tf_op jit(solution)/shard_map/ppermute | solution.py:41
  44.2 7.6 %collective-permute-done.17 = f32[128,256]{1,0:T(8,128)S(1)} collective-permute-done((f32[128,256]{1,0:T(8,128)}, f32[128,256]{1,0:T(8,128)S(1)}, u32[]{:S(2)}, u32[]{:S(2)}) %collective-permute-start.17) | collective-permute-done | bytes 131104 | tf_op jit(solution)/shard_map/ppermute | solution.py:41
  51.8 7.8 %collective-permute-start.15 = (f32[128,256]{1,0:T(8,128)S(1)}, f32[128,256]{1,0:T(8,128)S(1)}, u32[]{:S(2)}, u32[]{:S(2)}) collective-permute-start(f32[128,256]{1,0:T(8,128)S(1)} %copy-done.6), channel_id=1, source_target_pairs={{0,8},{1,9},{2,10},{3,11},{4,12},{5,13},{6,14},{7,15},{8,0},{9,1},... | collective-permute-start | bytes 393224 | tf_op jit(solution)/shard_map/ppermute | solution.py:41
  67.4 8.0 %collective-permute-start.21 = (f32[136,256]{1,0:T(8,128)S(1)}, f32[136,256]{1,0:T(8,128)S(1)}, u32[]{:S(2)}, u32[]{:S(2)}) collective-permute-start(f32[136,256]{1,0:T(8,128)S(1)} %get-tuple-element.59), channel_id=1, source_target_pairs={{0,16},{1,17},{2,18},{3,19},{4,20},{5,21},{6,22},{7,23},{8,24},{9,... | collective-permute-start | bytes 417800 | tf_op jit(solution)/shard_map/ppermute | solution.py:41
  78.8 5.4 %collective-permute-done.21 = f32[136,256]{1,0:T(8,128)S(1)} collective-permute-done((f32[136,256]{1,0:T(8,128)S(1)}, f32[136,256]{1,0:T(8,128)S(1)}, u32[]{:S(2)}, u32[]{:S(2)}) %collective-permute-start.21) | collective-permute-done | bytes 139296 | tf_op jit(solution)/shard_map/ppermute | solution.py:41
  89.7 5.1 %collective-permute-done.7 = f32[128,512]{1,0:T(8,128)S(1)} collective-permute-done((f32[128,512]{1,0:T(8,128)S(1)}, f32[128,512]{1,0:T(8,128)S(1)}, u32[]{:S(2)}, u32[]{:S(2)}) %collective-permute-start.7) | collective-permute-done | bytes 262176 | tf_op jit(solution)/shard_map/ppermute | solution.py:41
  96.6 2.5 %collective-permute-start.13 = (f32[64,512]{1,0:T(8,128)S(1)}, f32[64,512]{1,0:T(8,128)S(1)}, u32[]{:S(2)}, u32[]{:S(2)}) collective-permute-start(f32[64,512]{1,0:T(8,128)S(1)} %pad_maximum_fusion.31), channel_id=1, source_target_pairs={{0,8},{1,9},{2,10},{3,11},{4,12},{5,13},{6,14},{7,15},{8,0},{9,1},... | collective-permute-start | bytes 393224 | tf_op jit(solution)/shard_map/ppermute | solution.py:41
  107.5 2.7 %collective-permute-done.19 = f32[64,512]{1,0:T(8,128)S(1)} collective-permute-done((f32[64,512]{1,0:T(8,128)S(1)}, f32[64,512]{1,0:T(8,128)S(1)}, u32[]{:S(2)}, u32[]{:S(2)}) %collective-permute-start.19) | collective-permute-done | bytes 131104 | tf_op jit(solution)/shard_map/ppermute | solution.py:41
  112.4 2.7 %collective-permute-start.26 = (f32[32,512]{1,0:T(8,128)S(1)}, f32[32,512]{1,0:T(8,128)S(1)}, u32[]{:S(2)}, u32[]{:S(2)}) collective-permute-start(f32[32,512]{1,0:T(8,128)S(1)} %pad_maximum_fusion.42), channel_id=1, source_target_pairs={{0,16},{1,17},{2,18},{3,19},{4,20},{5,21},{6,22},{7,23},{8,24},{9,... | collective-permute-start | bytes 196616 | tf_op jit(solution)/shard_map/ppermute | solution.py:41
  116.5 2.4 %collective-permute-done.27 = f32[32,512]{1,0:T(8,128)S(1)} collective-permute-done((f32[32,512]{1,0:T(8,128)S(1)}, f32[32,512]{1,0:T(8,128)S(1)}, u32[]{:S(2)}, u32[]{:S(2)}) %collective-permute-start.27) | collective-permute-done | bytes 65568 | tf_op jit(solution)/shard_map/ppermute | solution.py:41
  122.8 2.7 %collective-permute-done.32 = f32[32,512]{1,0:T(8,128)S(1)} collective-permute-done((f32[32,512]{1,0:T(8,128)S(1)}, f32[32,512]{1,0:T(8,128)S(1)}, u32[]{:S(2)}, u32[]{:S(2)}) %collective-permute-start.32) | collective-permute-done | bytes 65568 | tf_op jit(solution)/shard_map/ppermute | solution.py:41
  132.0 2.9 %collective-permute-done.35 = f32[32,512]{1,0:T(8,128)S(1)} collective-permute-done((f32[32,512]{1,0:T(8,128)S(1)}, f32[32,512]{1,0:T(8,128)S(1)}, u32[]{:S(2)}, u32[]{:S(2)}) %collective-permute-start.35) | collective-permute-done | bytes 65568 | tf_op jit(solution)/shard_map/ppermute | solution.py:41
  138.8 3.4 %collective-permute-done.37 = f32[64,512]{1,0:T(8,128)S(1)} collective-permute-done((f32[64,512]{1,0:T(8,128)S(1)}, f32[64,512]{1,0:T(8,128)S(1)}, u32[]{:S(2)}, u32[]{:S(2)}) %collective-permute-start.37) | collective-permute-done | bytes 131104 | tf_op jit(solution)/shard_map/ppermute | solution.py:41
  143.5 2.2 %collective-permute-start.39 = (f32[64,512]{1,0:T(8,128)S(1)}, f32[64,512]{1,0:T(8,128)S(1)}, u32[]{:S(2)}, u32[]{:S(2)}) collective-permute-start(f32[64,512]{1,0:T(8,128)S(1)} %pad_maximum_fusion.34), channel_id=1, source_target_pairs={{0,8},{1,9},{2,10},{3,11},{4,12},{5,13},{6,14},{7,15},{8,0},{9,1},... | collective-permute-start | bytes 393224 | tf_op jit(solution)/shard_map/ppermute | solution.py:41
  147.1 3.7 %collective-permute-done.38 = f32[64,512]{1,0:T(8,128)S(1)} collective-permute-done((f32[64,512]{1,0:T(8,128)S(1)}, f32[64,512]{1,0:T(8,128)S(1)}, u32[]{:S(2)}, u32[]{:S(2)}) %collective-permute-start.38) | collective-permute-done | bytes 131104 | tf_op jit(solution)/shard_map/ppermute | solution.py:41
  154.4 4.8 %collective-permute-done.41 = f32[128,512]{1,0:T(8,128)S(1)} collective-permute-done((f32[128,512]{1,0:T(8,128)S(1)}, f32[128,512]{1,0:T(8,128)S(1)}, u32[]{:S(2)}, u32[]{:S(2)}) %collective-permute-start.41) | collective-permute-done | bytes 262176 | tf_op jit(solution)/shard_map/ppermute | solution.py:41
  162.2 4.6 %collective-permute-done.42 = f32[128,512]{1,0:T(8,128)S(1)} collective-permute-done((f32[128,512]{1,0:T(8,128)S(1)}, f32[128,512]{1,0:T(8,128)S(1)}, u32[]{:S(2)}, u32[]{:S(2)}) %collective-permute-start.42) | collective-permute-done | bytes 262176 | tf_op jit(solution)/shard_map/ppermute | solution.py:41
  168.4 3.0 %collective-permute-start.45 = (f32[128,128]{1,0:T(8,128)S(1)}, f32[128,128]{1,0:T(8,128)S(1)}, u32[]{:S(2)}, u32[]{:S(2)}) collective-permute-start(f32[128,128]{1,0:T(8,128)S(1)} %pad_maximum_fusion.46), channel_id=1, source_target_pairs={{0,24},{1,25},{2,26},{3,27},{4,28},{5,29},{6,30},{7,31},{8,16},{9,... | collective-permute-start | bytes 196616 | tf_op jit(solution)/shard_map/ppermute | solution.py:41
  172.2 2.2 %collective-permute-done.45 = f32[128,128]{1,0:T(8,128)S(1)} collective-permute-done((f32[128,128]{1,0:T(8,128)S(1)}, f32[128,128]{1,0:T(8,128)S(1)}, u32[]{:S(2)}, u32[]{:S(2)}) %collective-permute-start.45) | collective-permute-done | bytes 65568 | tf_op jit(solution)/shard_map/ppermute | solution.py:41
  (258 shorter events, 85.0 us)
Async XLA Ops:
  6.5 13.3 %collective-permute-start = (f32[224,128]{1,0:T(8,128)}, f32[224,128]{1,0:T(8,128)S(1)}, u32[]{:S(2)}, u32[]{:S(2)}) collective-permute-start(f32[224,128]{1,0:T(8,128)} %get-tuple-element.35), channel_id=1, source_target_pairs={{0,8},{1,9},{2,10},{3,11},{4,12},{5,13},{6,14},{7,15},{8,0},{9,1},... | collective-permute-start | bytes 344072 | tf_op jit(solution)/shard_map/ppermute | solution.py:41
  10.7 10.1 %collective-permute-start.1 = (f32[224,128]{1,0:T(8,128)}, f32[224,128]{1,0:T(8,128)}, u32[]{:S(2)}, u32[]{:S(2)}) collective-permute-start(f32[224,128]{1,0:T(8,128)} %get-tuple-element.47), channel_id=1, source_target_pairs={{0,16},{1,17},{2,18},{3,19},{4,20},{5,21},{6,22},{7,23},{8,24},{9,... | collective-permute-start | bytes 344072 | tf_op jit(solution)/shard_map/ppermute | solution.py:41
  14.3 18.6 %collective-permute-start.28 = (f32[128,256]{1,0:T(8,128)}, f32[128,256]{1,0:T(8,128)}, u32[]{:S(2)}, u32[]{:S(2)}) collective-permute-start(f32[128,256]{1,0:T(8,128)} %get-tuple-element.13), channel_id=1, source_target_pairs={{0,8},{1,9},{2,10},{3,11},{4,12},{5,13},{6,14},{7,15},{8,0},{9,1},... | collective-permute-start | bytes 393224 | tf_op jit(solution)/shard_map/ppermute | solution.py:41
  14.8 25.9 %collective-permute-start.5 = (f32[128,256]{1,0:T(8,128)}, f32[128,256]{1,0:T(8,128)S(1)}, u32[]{:S(2)}, u32[]{:S(2)}) collective-permute-start(f32[128,256]{1,0:T(8,128)} %get-tuple-element.18), channel_id=1, source_target_pairs={{0,24},{1,25},{2,26},{3,27},{4,28},{5,29},{6,30},{7,31},{8,16},{9,... | collective-permute-start | bytes 393224 | tf_op jit(solution)/shard_map/ppermute | solution.py:41
  16.1 24.8 %collective-permute-start.4 = (f32[128,256]{1,0:T(8,128)}, f32[128,256]{1,0:T(8,128)S(1)}, u32[]{:S(2)}, u32[]{:S(2)}) collective-permute-start(f32[128,256]{1,0:T(8,128)} %get-tuple-element.19), channel_id=1, source_target_pairs={{0,16},{1,17},{2,18},{3,19},{4,20},{5,21},{6,22},{7,23},{8,24},{9,... | collective-permute-start | bytes 393224 | tf_op jit(solution)/shard_map/ppermute | solution.py:41
  19.8 9.8 %collective-permute-start.2 = (f32[224,128]{1,0:T(8,128)}, f32[224,128]{1,0:T(8,128)S(1)}, u32[]{:S(2)}, u32[]{:S(2)}) collective-permute-start(f32[224,128]{1,0:T(8,128)} %get-tuple-element.48), channel_id=1, source_target_pairs={{0,24},{1,25},{2,26},{3,27},{4,28},{5,29},{6,30},{7,31},{8,16},{9,... | collective-permute-start | bytes 344072 | tf_op jit(solution)/shard_map/ppermute | solution.py:41
  20.8 22.5 %collective-permute-start.3 = (f32[128,256]{1,0:T(8,128)}, f32[128,256]{1,0:T(8,128)S(1)}, u32[]{:S(2)}, u32[]{:S(2)}) collective-permute-start(f32[128,256]{1,0:T(8,128)} %get-tuple-element.20), channel_id=1, source_target_pairs={{0,8},{1,9},{2,10},{3,11},{4,12},{5,13},{6,14},{7,15},{8,0},{9,1},... | collective-permute-start | bytes 393224 | tf_op jit(solution)/shard_map/ppermute | solution.py:41
  30.2 29.5 %collective-permute-start.10 = (f32[136,256]{1,0:T(8,128)S(1)}, f32[136,256]{1,0:T(8,128)S(1)}, u32[]{:S(2)}, u32[]{:S(2)}) collective-permute-start(f32[136,256]{1,0:T(8,128)S(1)} %get-tuple-element.25), channel_id=1, source_target_pairs={{0,24},{1,25},{2,26},{3,27},{4,28},{5,29},{6,30},{7,31},{8,16},{9,... | collective-permute-start | bytes 417800 | tf_op jit(solution)/shard_map/ppermute | solution.py:41
  32.9 28.3 %collective-permute-start.9 = (f32[136,256]{1,0:T(8,128)S(1)}, f32[136,256]{1,0:T(8,128)S(1)}, u32[]{:S(2)}, u32[]{:S(2)}) collective-permute-start(f32[136,256]{1,0:T(8,128)S(1)} %get-tuple-element.26), channel_id=1, source_target_pairs={{0,16},{1,17},{2,18},{3,19},{4,20},{5,21},{6,22},{7,23},{8,24},{9,... | collective-permute-start | bytes 417800 | tf_op jit(solution)/shard_map/ppermute | solution.py:41
  40.7 20.6 %collective-permute-start.8 = (f32[136,256]{1,0:T(8,128)S(1)}, f32[136,256]{1,0:T(8,128)S(1)}, u32[]{:S(2)}, u32[]{:S(2)}) collective-permute-start(f32[136,256]{1,0:T(8,128)S(1)} %get-tuple-element.27), channel_id=1, source_target_pairs={{0,8},{1,9},{2,10},{3,11},{4,12},{5,13},{6,14},{7,15},{8,0},{9,1},... | collective-permute-start | bytes 417800 | tf_op jit(solution)/shard_map/ppermute | solution.py:41
  40.9 10.9 %collective-permute-start.17 = (f32[128,256]{1,0:T(8,128)}, f32[128,256]{1,0:T(8,128)S(1)}, u32[]{:S(2)}, u32[]{:S(2)}) collective-permute-start(f32[128,256]{1,0:T(8,128)} %get-tuple-element.14), channel_id=1, source_target_pairs={{0,24},{1,25},{2,26},{3,27},{4,28},{5,29},{6,30},{7,31},{8,16},{9,... | collective-permute-start | bytes 393224 | tf_op jit(solution)/shard_map/ppermute | solution.py:41
  43.3 19.7 %collective-permute-start.16 = (f32[128,256]{1,0:T(8,128)}, f32[128,256]{1,0:T(8,128)S(1)}, u32[]{:S(2)}, u32[]{:S(2)}) collective-permute-start(f32[128,256]{1,0:T(8,128)} %get-tuple-element.15), channel_id=1, source_target_pairs={{0,16},{1,17},{2,18},{3,19},{4,20},{5,21},{6,22},{7,23},{8,24},{9,... | collective-permute-start | bytes 393224 | tf_op jit(solution)/shard_map/ppermute | solution.py:41
  51.8 13.1 %collective-permute-start.15 = (f32[128,256]{1,0:T(8,128)S(1)}, f32[128,256]{1,0:T(8,128)S(1)}, u32[]{:S(2)}, u32[]{:S(2)}) collective-permute-start(f32[128,256]{1,0:T(8,128)S(1)} %copy-done.6), channel_id=1, source_target_pairs={{0,8},{1,9},{2,10},{3,11},{4,12},{5,13},{6,14},{7,15},{8,0},{9,1},... | collective-permute-start | bytes 393224 | tf_op jit(solution)/shard_map/ppermute | solution.py:41
  59.7 7.7 %collective-permute-start.30 = (f32[128,256]{1,0:T(8,128)S(1)}, f32[128,256]{1,0:T(8,128)S(1)}, u32[]{:S(2)}, u32[]{:S(2)}) collective-permute-start(f32[128,256]{1,0:T(8,128)S(1)} %copy-done.5), channel_id=1, source_target_pairs={{0,24},{1,25},{2,26},{3,27},{4,28},{5,29},{6,30},{7,31},{8,16},{9,... | collective-permute-start | bytes 393224 | tf_op jit(solution)/shard_map/ppermute | solution.py:41
  61.2 16.4 %collective-permute-start.29 = (f32[128,256]{1,0:T(8,128)S(1)}, f32[128,256]{1,0:T(8,128)S(1)}, u32[]{:S(2)}, u32[]{:S(2)}) collective-permute-start(f32[128,256]{1,0:T(8,128)S(1)} %copy-done.4), channel_id=1, source_target_pairs={{0,16},{1,17},{2,18},{3,19},{4,20},{5,21},{6,22},{7,23},{8,24},{9,... | collective-permute-start | bytes 393224 | tf_op jit(solution)/shard_map/ppermute | solution.py:41
  61.2 24.0 %collective-permute-start.6 = (f32[512,256]{1,0:T(8,128)S(1)}, f32[512,256]{1,0:T(8,128)S(1)}, u32[]{:S(2)}, u32[]{:S(2)}) collective-permute-start(f32[512,256]{1,0:T(8,128)S(1)} %pad_maximum_fusion.17), channel_id=1, source_target_pairs={{0,1},{1,0},{2,3},{3,2},{4,5},{5,4},{6,7},{7,6},{8,9},{9,8},{10,11... | collective-permute-start | bytes 1572872 | tf_op jit(solution)/shard_map/ppermute | solution.py:41
  63.0 25.2 %collective-permute-start.11 = (f32[4,136,256]{2,1,0:T(8,128)S(1)}, f32[4,136,256]{2,1,0:T(8,128)S(1)}, u32[]{:S(2)}, u32[]{:S(2)}) collective-permute-start(f32[4,136,256]{2,1,0:T(8,128)S(1)} %pad_maximum_fusion.15), channel_id=1, source_target_pairs={{0,1},{1,0},{2,3},{3,2},{4,5},{5,4},{6,7},{7,6},{8,9},{9,8},{10,11... | collective-permute-start | bytes 1671176 | tf_op jit(solution)/shard_map/ppermute | solution.py:41
  64.9 13.8 %collective-permute-start.22 = (f32[136,256]{1,0:T(8,128)S(1)}, f32[136,256]{1,0:T(8,128)S(1)}, u32[]{:S(2)}, u32[]{:S(2)}) collective-permute-start(f32[136,256]{1,0:T(8,128)S(1)} %get-tuple-element.58), channel_id=1, source_target_pairs={{0,24},{1,25},{2,26},{3,27},{4,28},{5,29},{6,30},{7,31},{8,16},{9,... | collective-permute-start | bytes 417800 | tf_op jit(solution)/shard_map/ppermute | solution.py:41
  67.4 16.7 %collective-permute-start.21 = (f32[136,256]{1,0:T(8,128)S(1)}, f32[136,256]{1,0:T(8,128)S(1)}, u32[]{:S(2)}, u32[]{:S(2)}) collective-permute-start(f32[136,256]{1,0:T(8,128)S(1)} %get-tuple-element.59), channel_id=1, source_target_pairs={{0,16},{1,17},{2,18},{3,19},{4,20},{5,21},{6,22},{7,23},{8,24},{9,... | collective-permute-start | bytes 417800 | tf_op jit(solution)/shard_map/ppermute | solution.py:41
  78.7 22.2 %collective-permute-start.18 = (f32[512,256]{1,0:T(8,128)S(1)}, f32[512,256]{1,0:T(8,128)S(1)}, u32[]{:S(2)}, u32[]{:S(2)}) collective-permute-start(f32[512,256]{1,0:T(8,128)S(1)} %pad_maximum_fusion.18), channel_id=1, source_target_pairs={{0,1},{1,0},{2,3},{3,2},{4,5},{5,4},{6,7},{7,6},{8,9},{9,8},{10,11... | collective-permute-start | bytes 1572872 | tf_op jit(solution)/shard_map/ppermute | solution.py:41
  85.1 21.6 %collective-permute-start.23 = (f32[4,136,256]{2,1,0:T(8,128)S(1)}, f32[4,136,256]{2,1,0:T(8,128)S(1)}, u32[]{:S(2)}, u32[]{:S(2)}) collective-permute-start(f32[4,136,256]{2,1,0:T(8,128)S(1)} %pad_maximum_fusion.16), channel_id=1, source_target_pairs={{0,1},{1,0},{2,3},{3,2},{4,5},{5,4},{6,7},{7,6},{8,9},{9,8},{10,11... | collective-permute-start | bytes 1671176 | tf_op jit(solution)/shard_map/ppermute | solution.py:41
  86.7 8.1 %collective-permute-start.7 = (f32[128,512]{1,0:T(8,128)S(1)}, f32[128,512]{1,0:T(8,128)S(1)}, u32[]{:S(2)}, u32[]{:S(2)}) collective-permute-start(f32[128,512]{1,0:T(8,128)S(1)} %fusion.3), channel_id=1, source_target_pairs={{0,4},{1,5},{2,6},{3,7},{4,0},{5,1},{6,2},{7,3},{8,12},{9,13},{10,... | collective-permute-start | bytes 786440 | tf_op jit(solution)/shard_map/ppermute | solution.py:41
  100.9 15.7 %collective-permute-start.31 = (f32[512,256]{1,0:T(8,128)S(1)}, f32[512,256]{1,0:T(8,128)S(1)}, u32[]{:S(2)}, u32[]{:S(2)}) collective-permute-start(f32[512,256]{1,0:T(8,128)S(1)} %pad_maximum_fusion.19), channel_id=1, source_target_pairs={{0,1},{1,0},{2,3},{3,2},{4,5},{5,4},{6,7},{7,6},{8,9},{9,8},{10,11... | collective-permute-start | bytes 1572872 | tf_op jit(solution)/shard_map/ppermute | solution.py:41
  161.2 13.3 %collective-permute-start.46 = (f32[128,128]{1,0:T(8,128)S(1)}, f32[128,128]{1,0:T(8,128)S(1)}, u32[]{:S(2)}, u32[]{:S(2)}) collective-permute-start(f32[128,128]{1,0:T(8,128)S(1)} %pad_maximum_fusion.47), channel_id=1, source_target_pairs={{0,16},{1,17},{2,18},{3,19},{4,20},{5,21},{6,22},{7,23},{8,24},{9,... | collective-permute-start | bytes 196616 | tf_op jit(solution)/shard_map/ppermute | solution.py:41
  (47 other events, 228.0 us)

commit v2 on v1

v2 whole, which is shorter than its diff:
```python
import functools

import jax
import jax.numpy as jnp
from jax import lax
from jax.experimental import pallas as pl
from jax.experimental.pallas import tpu as pltpu
from jax.sharding import PartitionSpec as P

AXES = ("leaf", "row")
PRECISION = lax.Precision.HIGHEST


def dot(left, right, dims):
    return lax.dot_general(
        left, right, (dims, ((), ())), precision=PRECISION, preferred_element_type=jnp.float32
    )


def reverse(mask, bits):
    return sum(((mask >> b) & 1) << (bits - 1 - b) for b in range(bits))


def pack_kernel(levels, first, cross, spots, rhs, own, *rest):
    planes = 2 ** (levels - 1)
    messages, flat, lined = rest[: planes - 1], rest[-2], rest[-1]
    plane, core, across, own_group = spots[0], spots[1], spots[2], spots[3]
    panel = rhs.shape[1]
    half = rhs.shape[2] // 2
    group = half // planes
    columns = pl.ds(pl.multiple_of(core * half, half), half)
    slot = start = 0
    for depth in range(levels - 1, -1, -1):
        shift = levels - 1 - depth
        for s in range(2**depth):
            node = first[depth] + ((plane >> shift) ^ s)
            flat[slot] = rhs[node, :, columns].T
            for o in range(planes):
                if o >> shift != s:
                    continue
                for i in range(2**depth):
                    picked = own_group ^ (i ^ reverse(o, levels - 1))
                    lined[o, start + i * group : start + (i + 1) * group, :] = flat[
                        slot, pl.ds(pl.multiple_of(picked * group, group), group), :
                    ]
            slot += 1
        start += group * 2**depth
    own[...] = lined[0]
    part = lined.shape[1] // cross
    for o in range(1, planes):
        messages[o - 1][...] = lined[o, pl.ds(pl.multiple_of(across * part, 8), part), :]


def finish_kernel(levels, first, spots, *refs):
    total = 2**levels - 1
    planes = 2 ** (levels - 1)
    mine, theirs_upper, theirs_last, out, flat = refs[:total], refs[-4], refs[-3], refs[-2], refs[-1]
    plane, core, own_group = spots[0], spots[1], spots[3]
    half = out.shape[2] // 2
    group = half // planes
    slot = 0
    for depth in range(levels):
        shift = levels - 1 - depth
        for s in range(2**depth):
            node = first[depth] + ((plane >> shift) ^ s)
            index = 2**depth - 1 + s
            for side in range(2):
                for g in range(planes):
                    to = pl.ds(pl.multiple_of((own_group ^ g) * group, group), group)
                    rows = slice(g * group, (g + 1) * group)
                    if side == 0:
                        value = mine[index][rows, :]
                    elif depth < levels - 1:
                        value = theirs_upper[index, rows, :]
                    else:
                        value = theirs_last[s, rows, :]
                    flat[slot, to, :] = value
                place = core if side == 0 else 1 - core
                out[node, :, pl.ds(pl.multiple_of(place * half, half), half)] = flat[slot].T
                slot += 1


def after(value, *others):
    return lax.optimization_barrier((value,) + others)[0]


def local(rhs_blocks, diag_inverse, lower_blocks, update_rows):
    leaf_count = lax.axis_size("leaf")
    row_count = lax.axis_size("row")
    node_total, panel, width = rhs_blocks.shape
    piece = diag_inverse.shape[2]
    levels = (node_total + 1).bit_length() - 1
    bits = levels - 1
    planes = 2**bits
    inner = leaf_count // planes
    cross = row_count // 2
    half = width // 2
    group = half // planes
    first = [2**levels - 2 ** (d + 1) for d in range(levels)]
    shift = [levels - 1 - d for d in range(levels)]

    plane = lax.axis_index("leaf") // inner
    core = lax.axis_index("row") % 2
    across = lax.axis_index("row") // 2
    own_group = sum(((plane >> b) & 1) << (bits - 1 - b) for b in range(bits))
    spots = jnp.stack([plane, core, across, own_group]).astype(jnp.int32)

    def move(x, plane_mask=0, inner_mask=0, cross_mask=0, core_mask=0):
        pairs = []
        for leaf in range(leaf_count):
            for row in range(row_count):
                other_leaf = leaf ^ (plane_mask * inner + inner_mask)
                other_row = row ^ (cross_mask * 2 + core_mask)
                pairs.append((leaf * row_count + row, other_leaf * row_count + other_row))
        return lax.ppermute(x, AXES, pairs)

    def inner_sum(x):
        mask = 1
        while mask < inner:
            x = x + move(x, inner_mask=mask)
            mask *= 2
        return x

    def cross_sum(x, plane_mask=0):
        parts = [
            move(x, plane_mask=plane_mask, cross_mask=m) if m or plane_mask else x
            for m in range(cross)
        ]
        while len(parts) > 1:
            parts = [parts[i] + parts[i + 1] for i in range(0, len(parts), 2)]
        return parts[0]

    def reorder(x, mask):
        g = reverse(mask, bits)
        parts = [x[:, (p ^ g) * panel : ((p ^ g) + 1) * panel] for p in range(planes)]
        return jnp.concatenate(parts, axis=1)

    def regroup(x, mask):
        g = reverse(mask, bits)
        return jnp.concatenate(
            [x[(i ^ g) * group : ((i ^ g) + 1) * group] for i in range(planes)], axis=0
        )

    def pick(array, index):
        return lax.dynamic_index_in_dim(array, index, 0, keepdims=False)

    last = levels - 1
    diag_pieces = {0: pick(diag_inverse, first[last] + plane)}
    for o in range(1, planes):
        diag_pieces[o] = move(pick(diag_inverse, first[last] + (plane ^ o)), plane_mask=o)

    lines = sum(group * 2**d for d in range(levels))
    vmem = pl.BlockSpec(memory_space=pltpu.VMEM)
    packed = pl.pallas_call(
        functools.partial(pack_kernel, levels, first, cross),
        out_shape=[jax.ShapeDtypeStruct((lines, panel), jnp.float32)]
        + [jax.ShapeDtypeStruct((lines // cross, panel), jnp.float32)] * (planes - 1),
        in_specs=[pl.BlockSpec(memory_space=pltpu.SMEM), vmem],
        out_specs=[vmem] * planes,
        scratch_shapes=[
            pltpu.VMEM((node_total, half, panel), jnp.float32),
            pltpu.VMEM((planes, lines, panel), jnp.float32),
        ],
        name="pack",
    )(spots, rhs_blocks)
    arrived = jnp.stack([move(packed[o], plane_mask=o) for o in range(1, planes)])
    sides = [arrived] + [move(arrived, cross_mask=m) for m in range(1, cross)]
    part = lines // cross
    spread = jnp.concatenate(
        [sum(jnp.where(across ^ m == j, sides[m], 0.0) for m in range(cross)) for j in range(cross)],
        axis=1,
    )
    line_blocks = [packed[0]] + [spread[o - 1] for o in range(1, planes)]
    right = [None] * levels
    start = 0
    for depth in range(levels - 1, -1, -1):
        size = group * 2**depth
        right[depth] = jnp.concatenate(
            [line_blocks[reverse(p, bits)][start : start + size] for p in range(planes)], axis=1
        )
        start += size

    def in_order(parts):
        return jnp.concatenate([parts[reverse(p, bits)] for p in range(planes)], axis=0)

    def pair_core(own):
        return jnp.concatenate([own, move(own, core_mask=1)], axis=-1)

    diag = [None] * levels
    lower = [None] * levels
    diag[last] = pair_core(in_order(diag_pieces))

    def tagged(index):
        names = pick(update_rows, index).astype(jnp.float32)[None, :]
        return jnp.concatenate(
            [pick(lower_blocks, index), jnp.pad(names, ((0, 7), (0, piece - panel)))], axis=0
        )

    gate = diag_pieces[1]
    lower_pieces = {0: tagged(first[last] + plane)}
    for o in range(1, planes):
        lower_pieces[o] = move(after(tagged(first[last] + (plane ^ o)), gate), plane_mask=o)

    def spread_rows(body, names, depth, where):
        result = []
        for up in range(depth):
            base = (first[up] + (where >> shift[up])) * panel
            spot = (base + jnp.arange(panel, dtype=jnp.int32)).astype(jnp.float32)
            chosen = (names[..., None, :] == spot[:, None]).astype(jnp.float32)
            result.append(jnp.matmul(chosen, body, precision=lax.Precision.HIGHEST))
        return result

    both = pair_core(jnp.stack([lower_pieces[reverse(p, bits)] for p in range(planes)]))
    lower[last] = [
        block.reshape(planes * panel, 2 * piece)
        for block in spread_rows(both[:, :panel], both[:, panel, :panel], last, plane)
    ]

    def gather(blocks, depth):
        held = blocks[0]
        for s in range(1, 2**depth):
            held = jnp.concatenate([held, move(blocks[s], plane_mask=s << shift[depth])], axis=0)
        return held

    def spread_planes(held, depth):
        for b in range(shift[depth] - 1, -1, -1):
            held = jnp.concatenate([held, move(held, plane_mask=1 << b)], axis=0)
        return held

    gate = lower_pieces[1]
    for depth in range(last - 1, -1, -1):
        for kind in (0, 1):
            if kind and depth == 0:
                continue
            blocks = []
            for s in range(2**depth):
                node = first[depth] + ((plane >> shift[depth]) ^ s)
                if kind:
                    body = pick(lower_blocks, node)
                    names = pick(update_rows, node).astype(jnp.float32)
                    owner = ((plane >> shift[depth]) ^ s) << shift[depth]
                    body = jnp.concatenate(spread_rows(body, names, depth, owner), axis=0)
                else:
                    body = pick(diag_inverse, node)
                blocks.append(after(body, gate))
            held = spread_planes(gather(blocks, depth), depth)
            if kind == 0:
                diag[depth] = pair_core(held)
            else:
                wide = pair_core(held).reshape(planes, depth, panel, 2 * piece)
                lower[depth] = [
                    wide[:, up].reshape(planes * panel, 2 * piece) for up in range(depth)
                ]
            gate = held

    forward = [None] * levels
    pending = [None] * levels
    work = right[last]
    for depth in range(last, -1, -1):
        forward[depth] = inner_sum(dot(work, diag[depth], ((1,), (0,))))
        if depth == 0:
            break
        keep = work.shape[0] // 2
        mask = 1 << shift[depth]
        for up in range(depth - 1, -1, -1):
            update = dot(forward[depth], lower[depth][up], ((1,), (1,)))
            if pending[up] is not None:
                update = update + pending[up]
            mine, theirs = update[:keep], reorder(update[keep:], mask)
            if up == depth - 1:
                work = right[up] - (cross_sum(mine) + cross_sum(theirs, mask))
            else:
                pending[up] = mine + move(theirs, plane_mask=mask)

    answer = [None] * levels
    for depth in range(levels):
        residual = forward[depth]
        if depth > 0:
            known = sum(dot(answer[up], lower[depth][up], ((1,), (0,))) for up in range(depth))
            residual = residual - inner_sum(known)
        partial_value = dot(residual, diag[depth], ((1,), (1,)))
        if depth < last:
            mask = 1 << shift[depth + 1]
            for up in range(depth):
                answer[up] = jnp.concatenate(
                    [answer[up], move(reorder(answer[up], mask), plane_mask=mask)], axis=0
                )
            answer[depth] = jnp.concatenate(
                [cross_sum(partial_value), cross_sum(reorder(partial_value, mask), mask)], axis=0
            )
        else:
            answer[depth] = cross_sum(partial_value)

    collected = []
    for depth in range(levels):
        for s in range(2**depth):
            o = s << shift[depth]
            p = reverse(o, bits)
            block = answer[depth][:, p * panel : (p + 1) * panel]
            collected.append(move(regroup(block, o), plane_mask=o) if o else block)
    upper = move(jnp.stack(collected[: planes - 1]), core_mask=1)
    lowest = move(jnp.stack(collected[planes - 1 :]), core_mask=1)
    return pl.pallas_call(
        functools.partial(finish_kernel, levels, first),
        out_shape=jax.ShapeDtypeStruct(rhs_blocks.shape, jnp.float32),
        in_specs=[pl.BlockSpec(memory_space=pltpu.SMEM)] + [vmem] * (node_total + 2),
        out_specs=vmem,
        scratch_shapes=[pltpu.VMEM((2 * node_total, half, panel), jnp.float32)],
        name="finish",
    )(spots, *collected, upper, lowest)


def solution(mesh):
    placed = (
        P(None, "leaf", None),
        P(None, "leaf", "row"),
        P(None, "leaf", "row"),
        P(None, "leaf"),
    )
    return jax.shard_map(
        local, mesh=mesh, in_specs=placed, out_specs=P(None, "leaf", None), check_vma=False
    )
```

time: 186 us -> 161 us (0.87)
  local copies, waits for them, and re-layouts: 20.1 us -> 4.82 us
  starting transfers between devices: 74.5 us -> 60.8 us
  waiting for transfers between devices: 69.5 us -> 75.1 us
  Pallas kernels: 0 us -> 4.63 us
  other arithmetic: 4.91 us -> 1.17 us
  matrix products: 15.3 us -> 13.2 us
    ppermute x48 -> x47, starting transfers between devices: 74.5 us -> 60.8 us  [move(): return lax.ppermute(x, AXES, pairs)]
    unnamed x49 -> x28, local copies, waits for them, and re-layouts: 8.48 us -> 2.67 us
    ppermute x48 -> x47, waiting for transfers between devices: 69.5 us -> 75.1 us  [move(): return lax.ppermute(x, AXES, pairs)]
    pallas_call x0 -> x2, Pallas kernels: none -> 4.63 us  [the longest x1 2.53 us: local(): pl.pallas_call(functools.partial(finish_kernel, levels, first), out_shape...]
    concatenate x12 -> x6, other arithmetic: 4.44 us -> 0.12 us  [the longest x2 0.04 us: gather(): jnp.concatenate([held, move(blocks[s], plane_mask=s << shift[depth])], ax...]
    slice x26 -> x11, local copies, waits for them, and re-layouts: 4.13 us -> 0.07 us  [the longest x5 0.04 us: reorder(): parts = [x[:, (p ^ g) * panel:((p ^ g) + 1) * panel] for p in range(planes)]]
    dynamic_slice x36 -> x0, local copies, waits for them, and re-layouts: 3.61 us -> none  [the longest x32 3.38 us: local(): lax.dynamic_index_in_dim(mine, own_group ^ g, 1, keepdims=False)]
  transfers between devices with their start and end apart: 48 -> 47, of which waited for: 26 -> 23; matrix products, arithmetic and copies ran while one was open for 8% -> 6% of each run, Pallas kernels for 0% -> 1%
where the time goes in v2:
time: 161 us; the launch traced here: 160 us
  waiting for transfers between devices  75.1 us (47%)
  starting transfers between devices  60.8 us (38%)
  matrix products  13.2 us (8%)
  local copies, waits for them, and re-layouts  4.82 us (3%)
  Pallas kernels  4.63 us (3%)
    ppermute x47, waiting for transfers between devices, move(): return lax.ppermute(x, AXES, pairs)  75.1 us
    ppermute x47, starting transfers between devices, move(): return lax.ppermute(x, AXES, pairs)  60.8 us
    dot_general x12, matrix products, dot(): lax.dot_general(left, right, (dims, ((), ())), precision=PRECISION, prefe...  11.3 us
  transfers between devices with their start and end apart: 47, of which 23 were waited for; matrix products, arithmetic and copies ran while one was open for 6% of the time, Pallas kernels for 1%

profile of v2, /device:TPU:0, one launch (start us, length us, event | category | flops | bytes accessed | tf_op | source)
XLA Modules:
  0.0 160.4 jit_solution(15985671887245907208)
XLA Ops:
  1.3 3.1 %collective-permute-start.5 = (f32[128,256]{1,0:T(8,128)S(1)}, f32[128,256]{1,0:T(8,128)S(1)}, u32[]{:S(2)}, u32[]{:S(2)}) collective-permute-start(f32[128,256]{1,0:T(8,128)S(1)} %get-tuple-element.32), channel_id=1, source_target_pairs={{0,8},{1,9},{2,10},{3,11},{4,12},{5,13},{6,14},{7,15},{8,0},{9,1},... | collective-permute-start | bytes 393224 | tf_op jit(solution)/shard_map/ppermute | solution.py:115
  5.0 2.1 %pack.1 = (f32[224,128]{1,0:T(8,128)}, f32[112,128]{1,0:T(8,128)}, f32[112,128]{1,0:T(8,128)}, f32[112,128]{1,0:T(8,128)}) custom-call(s32[4]{0:T(128)} %pad_add_fusion.spots, f32[7,128,256]{2,1,0:T(8,128)} %rhs.1), custom_call_target="tpu_custom_call" | custom-call | tf_op jit(solution)/shard_map/pack/pallas_call | solution.py:154
  7.2 3.0 %collective-permute-start.1 = (f32[112,128]{1,0:T(8,128)}, f32[112,128]{1,0:T(8,128)S(1)}, u32[]{:S(2)}, u32[]{:S(2)}) collective-permute-start(f32[112,128]{1,0:T(8,128)} %get-tuple-element.19), channel_id=1, source_target_pairs={{0,16},{1,17},{2,18},{3,19},{4,20},{5,21},{6,22},{7,23},{8,24},{9,... | collective-permute-start | bytes 172040 | tf_op jit(solution)/shard_map/ppermute | solution.py:115
  16.9 4.5 %collective-permute-start.3 = (f32[3,112,128]{2,1,0:T(8,128)S(1)}, f32[3,112,128]{2,1,0:T(8,128)S(1)}, u32[]{:S(2)}, u32[]{:S(2)}) collective-permute-start(f32[3,112,128]{2,1,0:T(8,128)S(1)} %pad_maximum_fusion.26), channel_id=1, source_target_pairs={{0,2},{1,3},{2,0},{3,1},{4,6},{5,7},{6,4},{7,5},{8,10},{9,11},{10,... | collective-permute-start | bytes 516104 | tf_op jit(solution)/shard_map/ppermute | solution.py:115
  21.4 4.2 %collective-permute-start.11 = (f32[136,256]{1,0:T(8,128)S(1)}, f32[136,256]{1,0:T(8,128)S(1)}, u32[]{:S(2)}, u32[]{:S(2)}) collective-permute-start(f32[136,256]{1,0:T(8,128)S(1)} %get-tuple-element.23), channel_id=1, source_target_pairs={{0,24},{1,25},{2,26},{3,27},{4,28},{5,29},{6,30},{7,31},{8,16},{9,... | collective-permute-start | bytes 417800 | tf_op jit(solution)/shard_map/ppermute | solution.py:115
  26.6 6.8 %collective-permute-done.10 = f32[136,256]{1,0:T(8,128)S(1)} collective-permute-done((f32[136,256]{1,0:T(8,128)S(1)}, f32[136,256]{1,0:T(8,128)S(1)}, u32[]{:S(2)}, u32[]{:S(2)}) %collective-permute-start.10) | collective-permute-done | bytes 139296 | tf_op jit(solution)/shard_map/ppermute | solution.py:115
  33.4 2.6 %collective-permute-start.16 = (f32[128,256]{1,0:T(8,128)S(1)}, f32[128,256]{1,0:T(8,128)S(1)}, u32[]{:S(2)}, u32[]{:S(2)}) collective-permute-start(f32[128,256]{1,0:T(8,128)S(1)} %get-tuple-element.25), channel_id=1, source_target_pairs={{0,16},{1,17},{2,18},{3,19},{4,20},{5,21},{6,22},{7,23},{8,24},{9,... | collective-permute-start | bytes 393224 | tf_op jit(solution)/shard_map/ppermute | solution.py:115
  36.1 8.9 %collective-permute-done.16 = f32[128,256]{1,0:T(8,128)S(1)} collective-permute-done((f32[128,256]{1,0:T(8,128)S(1)}, f32[128,256]{1,0:T(8,128)S(1)}, u32[]{:S(2)}, u32[]{:S(2)}) %collective-permute-start.16) | collective-permute-done | bytes 131104 | tf_op jit(solution)/shard_map/ppermute | solution.py:115
  45.3 7.6 %collective-permute-done.17 = f32[256,256]{1,0:T(8,128)S(1)} collective-permute-done((f32[256,256]{1,0:T(8,128)S(1)}, f32[256,256]{1,0:T(8,128)S(1)}, u32[]{:S(2)}, u32[]{:S(2)}) %collective-permute-start.17) | collective-permute-done | bytes 262176 | tf_op jit(solution)/shard_map/ppermute | solution.py:115
  56.8 3.8 %collective-permute-done.20 = f32[128,256]{1,0:T(8,128)S(1)} collective-permute-done((f32[128,256]{1,0:T(8,128)S(1)}, f32[128,256]{1,0:T(8,128)S(1)}, u32[]{:S(2)}, u32[]{:S(2)}) %collective-permute-start.20) | collective-permute-done | bytes 131104 | tf_op jit(solution)/shard_map/ppermute | solution.py:115
  72.9 5.5 %collective-permute-done.27 = f32[128,256]{1,0:T(8,128)S(1)} collective-permute-done((f32[128,256]{1,0:T(8,128)S(1)}, f32[128,256]{1,0:T(8,128)S(1)}, u32[]{:S(2)}, u32[]{:S(2)}) %collective-permute-start.27) | collective-permute-done | bytes 131104 | tf_op jit(solution)/shard_map/ppermute | solution.py:115
  83.3 3.8 %collective-permute-done.19 = f32[64,512]{1,0:T(8,128)S(1)} collective-permute-done((f32[64,512]{1,0:T(8,128)S(1)}, f32[64,512]{1,0:T(8,128)S(1)}, u32[]{:S(2)}, u32[]{:S(2)}) %collective-permute-start.19) | collective-permute-done | bytes 131104 | tf_op jit(solution)/shard_map/ppermute | solution.py:115
  90.9 3.5 %collective-permute-start.26 = (f32[32,512]{1,0:T(8,128)S(1)}, f32[32,512]{1,0:T(8,128)S(1)}, u32[]{:S(2)}, u32[]{:S(2)}) collective-permute-start(f32[32,512]{1,0:T(8,128)S(1)} %pad_maximum_fusion.35), channel_id=1, source_target_pairs={{0,18},{1,19},{2,16},{3,17},{4,22},{5,23},{6,20},{7,21},{8,26},{9,... | collective-permute-start | bytes 196616 | tf_op jit(solution)/shard_map/ppermute | solution.py:115
  94.6 2.2 %collective-permute-done.25 = f32[32,512]{1,0:T(8,128)S(1)} collective-permute-done((f32[32,512]{1,0:T(8,128)S(1)}, f32[32,512]{1,0:T(8,128)S(1)}, u32[]{:S(2)}, u32[]{:S(2)}) %collective-permute-start.25) | collective-permute-done | bytes 65568 | tf_op jit(solution)/shard_map/ppermute | solution.py:115
  96.8 4.0 %collective-permute-done.26 = f32[32,512]{1,0:T(8,128)S(1)} collective-permute-done((f32[32,512]{1,0:T(8,128)S(1)}, f32[32,512]{1,0:T(8,128)S(1)}, u32[]{:S(2)}, u32[]{:S(2)}) %collective-permute-start.26) | collective-permute-done | bytes 65568 | tf_op jit(solution)/shard_map/ppermute | solution.py:115
  103.2 2.7 %collective-permute-done.30 = f32[32,512]{1,0:T(8,128)S(1)} collective-permute-done((f32[32,512]{1,0:T(8,128)S(1)}, f32[32,512]{1,0:T(8,128)S(1)}, u32[]{:S(2)}, u32[]{:S(2)}) %collective-permute-start.30) | collective-permute-done | bytes 65568 | tf_op jit(solution)/shard_map/ppermute | solution.py:115
  107.3 4.1 %collective-permute-start.33 = (f32[32,512]{1,0:T(8,128)S(1)}, f32[32,512]{1,0:T(8,128)S(1)}, u32[]{:S(2)}, u32[]{:S(2)}) collective-permute-start(f32[32,512]{1,0:T(8,128)S(1)} %pad_maximum_fusion.36), channel_id=1, source_target_pairs={{0,18},{1,19},{2,16},{3,17},{4,22},{5,23},{6,20},{7,21},{8,26},{9,... | collective-permute-start | bytes 196616 | tf_op jit(solution)/shard_map/ppermute | solution.py:115
  111.5 2.2 %collective-permute-done.32 = f32[32,512]{1,0:T(8,128)S(1)} collective-permute-done((f32[32,512]{1,0:T(8,128)S(1)}, f32[32,512]{1,0:T(8,128)S(1)}, u32[]{:S(2)}, u32[]{:S(2)}) %collective-permute-start.32) | collective-permute-done | bytes 65568 | tf_op jit(solution)/shard_map/ppermute | solution.py:115
  113.7 2.1 %collective-permute-done.33 = f32[32,512]{1,0:T(8,128)S(1)} collective-permute-done((f32[32,512]{1,0:T(8,128)S(1)}, f32[32,512]{1,0:T(8,128)S(1)}, u32[]{:S(2)}, u32[]{:S(2)}) %collective-permute-start.33) | collective-permute-done | bytes 65568 | tf_op jit(solution)/shard_map/ppermute | solution.py:115
  117.4 4.2 %collective-permute-done.35 = f32[64,512]{1,0:T(8,128)S(1)} collective-permute-done((f32[64,512]{1,0:T(8,128)S(1)}, f32[64,512]{1,0:T(8,128)S(1)}, u32[]{:S(2)}, u32[]{:S(2)}) %collective-permute-start.35) | collective-permute-done | bytes 131104 | tf_op jit(solution)/shard_map/ppermute | solution.py:115
  128.7 2.3 %collective-permute-done.38 = f32[64,512]{1,0:T(8,128)S(1)} collective-permute-done((f32[64,512]{1,0:T(8,128)S(1)}, f32[64,512]{1,0:T(8,128)S(1)}, u32[]{:S(2)}, u32[]{:S(2)}) %collective-permute-start.38) | collective-permute-done | bytes 131104 | tf_op jit(solution)/shard_map/ppermute | solution.py:115
  134.1 4.8 %collective-permute-done.40 = f32[128,512]{1,0:T(8,128)S(1)} collective-permute-done((f32[128,512]{1,0:T(8,128)S(1)}, f32[128,512]{1,0:T(8,128)S(1)}, u32[]{:S(2)}, u32[]{:S(2)}) %collective-permute-start.40) | collective-permute-done | bytes 262176 | tf_op jit(solution)/shard_map/ppermute | solution.py:115
  142.6 3.8 %collective-permute-done.41 = f32[128,512]{1,0:T(8,128)S(1)} collective-permute-done((f32[128,512]{1,0:T(8,128)S(1)}, f32[128,512]{1,0:T(8,128)S(1)}, u32[]{:S(2)}, u32[]{:S(2)}) %collective-permute-start.41) | collective-permute-done | bytes 262176 | tf_op jit(solution)/shard_map/ppermute | solution.py:115
  157.9 2.5 %finish.1 = f32[7,128,256]{2,1,0:T(8,128)} custom-call(s32[4]{0:T(128)} %pad_add_fusion.spots, f32[128,128]{1,0:T(8,128)} %copy-done.1, f32[128,128]{1,0:T(8,128)} %copy-done.2, f32[128,128]{1,0:T(8,128)} %copy-done.3, f32[128,128]{1,0:T(8,128)} %get-tuple-element.46.refs_3_, f32[128,128]{1,0:T(8,128)} %copy-done.7, f32[128,128]{1,0:T(8,128)} %copy-done.6, ...), custom_call_target="tpu_custom_call" | custom-call | tf_op jit(solution)/shard_map/finish/pallas_call | solution.py:303
  (178 shorter events, 65.5 us)
Async XLA Ops:
  1.3 20.1 %collective-permute-start.5 = (f32[128,256]{1,0:T(8,128)S(1)}, f32[128,256]{1,0:T(8,128)S(1)}, u32[]{:S(2)}, u32[]{:S(2)}) collective-permute-start(f32[128,256]{1,0:T(8,128)S(1)} %get-tuple-element.32), channel_id=1, source_target_pairs={{0,8},{1,9},{2,10},{3,11},{4,12},{5,13},{6,14},{7,15},{8,0},{9,1},... | collective-permute-start | bytes 393224 | tf_op jit(solution)/shard_map/ppermute | solution.py:115
  7.2 8.3 %collective-permute-start.1 = (f32[112,128]{1,0:T(8,128)}, f32[112,128]{1,0:T(8,128)S(1)}, u32[]{:S(2)}, u32[]{:S(2)}) collective-permute-start(f32[112,128]{1,0:T(8,128)} %get-tuple-element.19), channel_id=1, source_target_pairs={{0,16},{1,17},{2,18},{3,19},{4,20},{5,21},{6,22},{7,23},{8,24},{9,... | collective-permute-start | bytes 172040 | tf_op jit(solution)/shard_map/ppermute | solution.py:115
  11.5 14.6 %collective-permute-start.4 = (f32[128,256]{1,0:T(8,128)S(1)}, f32[128,256]{1,0:T(8,128)S(1)}, u32[]{:S(2)}, u32[]{:S(2)}) collective-permute-start(f32[128,256]{1,0:T(8,128)S(1)} %get-tuple-element.33), channel_id=1, source_target_pairs={{0,16},{1,17},{2,18},{3,19},{4,20},{5,21},{6,22},{7,23},{8,24},{9,... | collective-permute-start | bytes 393224 | tf_op jit(solution)/shard_map/ppermute | solution.py:115
  14.5 11.9 %collective-permute-start.6 = (f32[128,256]{1,0:T(8,128)S(1)}, f32[128,256]{1,0:T(8,128)S(1)}, u32[]{:S(2)}, u32[]{:S(2)}) collective-permute-start(f32[128,256]{1,0:T(8,128)S(1)} %get-tuple-element.31), channel_id=1, source_target_pairs={{0,24},{1,25},{2,26},{3,27},{4,28},{5,29},{6,30},{7,31},{8,16},{9,... | collective-permute-start | bytes 393224 | tf_op jit(solution)/shard_map/ppermute | solution.py:115
  16.9 9.7 %collective-permute-start.3 = (f32[3,112,128]{2,1,0:T(8,128)S(1)}, f32[3,112,128]{2,1,0:T(8,128)S(1)}, u32[]{:S(2)}, u32[]{:S(2)}) collective-permute-start(f32[3,112,128]{2,1,0:T(8,128)S(1)} %pad_maximum_fusion.26), channel_id=1, source_target_pairs={{0,2},{1,3},{2,0},{3,1},{4,6},{5,7},{6,4},{7,5},{8,10},{9,11},{10,... | collective-permute-start | bytes 516104 | tf_op jit(solution)/shard_map/ppermute | solution.py:115
  21.4 23.7 %collective-permute-start.11 = (f32[136,256]{1,0:T(8,128)S(1)}, f32[136,256]{1,0:T(8,128)S(1)}, u32[]{:S(2)}, u32[]{:S(2)}) collective-permute-start(f32[136,256]{1,0:T(8,128)S(1)} %get-tuple-element.23), channel_id=1, source_target_pairs={{0,24},{1,25},{2,26},{3,27},{4,28},{5,29},{6,30},{7,31},{8,16},{9,... | collective-permute-start | bytes 417800 | tf_op jit(solution)/shard_map/ppermute | solution.py:115
  25.6 19.6 %collective-permute-start.9 = (f32[136,256]{1,0:T(8,128)S(1)}, f32[136,256]{1,0:T(8,128)S(1)}, u32[]{:S(2)}, u32[]{:S(2)}) collective-permute-start(f32[136,256]{1,0:T(8,128)S(1)} %select_maximum_fusion.2), channel_id=1, source_target_pairs={{0,16},{1,17},{2,18},{3,19},{4,20},{5,21},{6,22},{7,23},{8,24},{9,... | collective-permute-start | bytes 417800 | tf_op jit(solution)/shard_map/ppermute | solution.py:115
  26.5 28.0 %collective-permute-start.7 = (f32[512,256]{1,0:T(8,128)S(1)}, f32[512,256]{1,0:T(8,128)S(1)}, u32[]{:S(2)}, u32[]{:S(2)}) collective-permute-start(f32[512,256]{1,0:T(8,128)S(1)} %pad_maximum_fusion.15), channel_id=1, source_target_pairs={{0,1},{1,0},{2,3},{3,2},{4,5},{5,4},{6,7},{7,6},{8,9},{9,8},{10,11... | collective-permute-start | bytes 1572872 | tf_op jit(solution)/shard_map/ppermute | solution.py:115
  33.4 11.6 %collective-permute-start.16 = (f32[128,256]{1,0:T(8,128)S(1)}, f32[128,256]{1,0:T(8,128)S(1)}, u32[]{:S(2)}, u32[]{:S(2)}) collective-permute-start(f32[128,256]{1,0:T(8,128)S(1)} %get-tuple-element.25), channel_id=1, source_target_pairs={{0,16},{1,17},{2,18},{3,19},{4,20},{5,21},{6,22},{7,23},{8,24},{9,... | collective-permute-start | bytes 393224 | tf_op jit(solution)/shard_map/ppermute | solution.py:115
  45.0 7.8 %collective-permute-start.17 = (f32[256,256]{1,0:T(8,128)S(1)}, f32[256,256]{1,0:T(8,128)S(1)}, u32[]{:S(2)}, u32[]{:S(2)}) collective-permute-start(f32[256,256]{1,0:T(8,128)S(1)} %pad_maximum_fusion.20), channel_id=1, source_target_pairs={{0,8},{1,9},{2,10},{3,11},{4,12},{5,13},{6,14},{7,15},{8,0},{9,1},... | collective-permute-start | bytes 786440 | tf_op jit(solution)/shard_map/ppermute | solution.py:115
  45.2 15.6 %collective-permute-start.12 = (f32[4,136,256]{2,1,0:T(8,128)S(1)}, f32[4,136,256]{2,1,0:T(8,128)S(1)}, u32[]{:S(2)}, u32[]{:S(2)}) collective-permute-start(f32[4,136,256]{2,1,0:T(8,128)S(1)} %pad_maximum_fusion.14), channel_id=1, source_target_pairs={{0,1},{1,0},{2,3},{3,2},{4,5},{5,4},{6,7},{7,6},{8,9},{9,8},{10,11... | collective-permute-start | bytes 1671176 | tf_op jit(solution)/shard_map/ppermute | solution.py:115
  56.8 23.8 %collective-permute-start.18 = (f32[512,256]{1,0:T(8,128)S(1)}, f32[512,256]{1,0:T(8,128)S(1)}, u32[]{:S(2)}, u32[]{:S(2)}) collective-permute-start(f32[512,256]{1,0:T(8,128)S(1)} %constant_dynamic-update-slice_fusion), channel_id=1, source_target_pairs={{0,1},{1,0},{2,3},{3,2},{4,5},{5,4},{6,7},{7,6},{8,9},{9,8},{10,11... | collective-permute-start | bytes 1572872 | tf_op jit(solution)/shard_map/ppermute | solution.py:115
  60.7 9.3 %collective-permute-start.21 = (f32[256,256]{1,0:T(8,128)S(1)}, f32[256,256]{1,0:T(8,128)S(1)}, u32[]{:S(2)}, u32[]{:S(2)}) collective-permute-start(f32[256,256]{1,0:T(8,128)S(1)} %pad_maximum_fusion.21), channel_id=1, source_target_pairs={{0,8},{1,9},{2,10},{3,11},{4,12},{5,13},{6,14},{7,15},{8,0},{9,1},... | collective-permute-start | bytes 786440 | tf_op jit(solution)/shard_map/ppermute | solution.py:115
  63.5 14.9 %collective-permute-start.14 = (f32[64,512]{1,0:T(8,128)S(1)}, f32[64,512]{1,0:T(8,128)S(1)}, u32[]{:S(2)}, u32[]{:S(2)}) collective-permute-start(f32[64,512]{1,0:T(8,128)S(1)} %pad_maximum_fusion.28), channel_id=1, source_target_pairs={{0,8},{1,9},{2,10},{3,11},{4,12},{5,13},{6,14},{7,15},{8,0},{9,1},... | collective-permute-start | bytes 393224 | tf_op jit(solution)/shard_map/ppermute | solution.py:115
  65.6 13.0 %collective-permute-start.15 = (f32[64,512]{1,0:T(8,128)S(1)}, f32[64,512]{1,0:T(8,128)S(1)}, u32[]{:S(2)}, u32[]{:S(2)}) collective-permute-start(f32[64,512]{1,0:T(8,128)S(1)} %pad_maximum_fusion.28), channel_id=1, source_target_pairs={{0,10},{1,11},{2,8},{3,9},{4,14},{5,15},{6,12},{7,13},{8,2},{9,3},... | collective-permute-start | bytes 393224 | tf_op jit(solution)/shard_map/ppermute | solution.py:115
  70.0 8.3 %collective-permute-start.27 = (f32[128,256]{1,0:T(8,128)S(1)}, f32[128,256]{1,0:T(8,128)S(1)}, u32[]{:S(2)}, u32[]{:S(2)}) collective-permute-start(f32[128,256]{1,0:T(8,128)S(1)} %get-tuple-element.28), channel_id=1, source_target_pairs={{0,16},{1,17},{2,18},{3,19},{4,20},{5,21},{6,22},{7,23},{8,24},{9,... | collective-permute-start | bytes 393224 | tf_op jit(solution)/shard_map/ppermute | solution.py:115
  71.3 9.3 %collective-permute-start.13 = (f32[64,512]{1,0:T(8,128)S(1)}, f32[64,512]{1,0:T(8,128)S(1)}, u32[]{:S(2)}, u32[]{:S(2)}) collective-permute-start(f32[64,512]{1,0:T(8,128)S(1)} %slice.320), channel_id=1, source_target_pairs={{0,2},{1,3},{2,0},{3,1},{4,6},{5,7},{6,4},{7,5},{8,10},{9,11},{10,... | collective-permute-start | bytes 393224 | tf_op jit(solution)/shard_map/ppermute | solution.py:115
  78.4 10.6 %collective-permute-start.23 = (f32[64,512]{1,0:T(8,128)S(1)}, f32[64,512]{1,0:T(8,128)S(1)}, u32[]{:S(2)}, u32[]{:S(2)}) collective-permute-start(f32[64,512]{1,0:T(8,128)S(1)} %pad_maximum_fusion.29), channel_id=1, source_target_pairs={{0,8},{1,9},{2,10},{3,11},{4,12},{5,13},{6,14},{7,15},{8,0},{9,1},... | collective-permute-start | bytes 393224 | tf_op jit(solution)/shard_map/ppermute | solution.py:115
  78.5 10.5 %collective-permute-start.22 = (f32[512,256]{1,0:T(8,128)S(1)}, f32[512,256]{1,0:T(8,128)S(1)}, u32[]{:S(2)}, u32[]{:S(2)}) collective-permute-start(f32[512,256]{1,0:T(8,128)S(1)} %constant_dynamic-update-slice_fusion.3), channel_id=1, source_target_pairs={{0,1},{1,0},{2,3},{3,2},{4,5},{5,4},{6,7},{7,6},{8,9},{9,8},{10,11... | collective-permute-start | bytes 1572872 | tf_op jit(solution)/shard_map/ppermute | solution.py:115
  78.6 10.3 %collective-permute-start.28 = (f32[256,256]{1,0:T(8,128)S(1)}, f32[256,256]{1,0:T(8,128)S(1)}, u32[]{:S(2)}, u32[]{:S(2)}) collective-permute-start(f32[256,256]{1,0:T(8,128)S(1)} %pad_maximum_fusion.22), channel_id=1, source_target_pairs={{0,8},{1,9},{2,10},{3,11},{4,12},{5,13},{6,14},{7,15},{8,0},{9,1},... | collective-permute-start | bytes 786440 | tf_op jit(solution)/shard_map/ppermute | solution.py:115
  88.9 11.9 %collective-permute-start.29 = (f32[512,256]{1,0:T(8,128)S(1)}, f32[512,256]{1,0:T(8,128)S(1)}, u32[]{:S(2)}, u32[]{:S(2)}) collective-permute-start(f32[512,256]{1,0:T(8,128)S(1)} %constant_dynamic-update-slice_fusion.6), channel_id=1, source_target_pairs={{0,1},{1,0},{2,3},{3,2},{4,5},{5,4},{6,7},{7,6},{8,9},{9,8},{10,11... | collective-permute-start | bytes 1572872 | tf_op jit(solution)/shard_map/ppermute | solution.py:115
  90.9 9.9 %collective-permute-start.26 = (f32[32,512]{1,0:T(8,128)S(1)}, f32[32,512]{1,0:T(8,128)S(1)}, u32[]{:S(2)}, u32[]{:S(2)}) collective-permute-start(f32[32,512]{1,0:T(8,128)S(1)} %pad_maximum_fusion.35), channel_id=1, source_target_pairs={{0,18},{1,19},{2,16},{3,17},{4,22},{5,23},{6,20},{7,21},{8,26},{9,... | collective-permute-start | bytes 196616 | tf_op jit(solution)/shard_map/ppermute | solution.py:115
  107.3 8.4 %collective-permute-start.33 = (f32[32,512]{1,0:T(8,128)S(1)}, f32[32,512]{1,0:T(8,128)S(1)}, u32[]{:S(2)}, u32[]{:S(2)}) collective-permute-start(f32[32,512]{1,0:T(8,128)S(1)} %pad_maximum_fusion.36), channel_id=1, source_target_pairs={{0,18},{1,19},{2,16},{3,17},{4,22},{5,23},{6,20},{7,21},{8,26},{9,... | collective-permute-start | bytes 196616 | tf_op jit(solution)/shard_map/ppermute | solution.py:115
  141.3 13.6 %collective-permute-start.39 = (f32[128,128]{1,0:T(8,128)S(1)}, f32[128,128]{1,0:T(8,128)S(1)}, u32[]{:S(2)}, u32[]{:S(2)}) collective-permute-start(f32[128,128]{1,0:T(8,128)S(1)} %pad_maximum_fusion.37), channel_id=1, source_target_pairs={{0,16},{1,17},{2,18},{3,19},{4,20},{5,21},{6,22},{7,23},{8,24},{9,... | collective-permute-start | bytes 196616 | tf_op jit(solution)/shard_map/ppermute | solution.py:115
  (34 other events, 185.8 us)

commit v3 on v2

--- a/solution.py
+++ b/solution.py
@@ -21,10 +21,18 @@
     return sum(((mask >> b) & 1) << (bits - 1 - b) for b in range(bits))
 
 
-def pack_kernel(levels, first, cross, spots, rhs, own, *rest):
+def places(planes, inner):
+    plane = lax.axis_index("leaf") // inner
+    bits = planes.bit_length() - 1
+    own_group = sum(((plane >> b) & 1) << (bits - 1 - b) for b in range(bits))
+    row = lax.axis_index("row")
+    return plane, row % 2, row // 2, own_group
+
+
+def pack_kernel(levels, first, cross, inner, rhs, own, *rest):
     planes = 2 ** (levels - 1)
     messages, flat, lined = rest[: planes - 1], rest[-2], rest[-1]
-    plane, core, across, own_group = spots[0], spots[1], spots[2], spots[3]
+    plane, core, across, own_group = places(planes, inner)
     panel = rhs.shape[1]
     half = rhs.shape[2] // 2
     group = half // planes
@@ -51,11 +59,11 @@
         messages[o - 1][...] = lined[o, pl.ds(pl.multiple_of(across * part, 8), part), :]
 
 
-def finish_kernel(levels, first, spots, *refs):
+def finish_kernel(levels, first, inner, *refs):
     total = 2**levels - 1
     planes = 2 ** (levels - 1)
     mine, theirs_upper, theirs_last, out, flat = refs[:total], refs[-4], refs[-3], refs[-2], refs[-1]
-    plane, core, own_group = spots[0], spots[1], spots[3]
+    plane, core, _, own_group = places(planes, inner)
     half = out.shape[2] // 2
     group = half // planes
     slot = 0
@@ -100,10 +108,7 @@
     shift = [levels - 1 - d for d in range(levels)]
 
     plane = lax.axis_index("leaf") // inner
-    core = lax.axis_index("row") % 2
     across = lax.axis_index("row") // 2
-    own_group = sum(((plane >> b) & 1) << (bits - 1 - b) for b in range(bits))
-    spots = jnp.stack([plane, core, across, own_group]).astype(jnp.int32)
 
     def move(x, plane_mask=0, inner_mask=0, cross_mask=0, core_mask=0):
         pairs = []
@@ -152,17 +157,17 @@
     lines = sum(group * 2**d for d in range(levels))
     vmem = pl.BlockSpec(memory_space=pltpu.VMEM)
     packed = pl.pallas_call(
-        functools.partial(pack_kernel, levels, first, cross),
+        functools.partial(pack_kernel, levels, first, cross, inner),
         out_shape=[jax.ShapeDtypeStruct((lines, panel), jnp.float32)]
         + [jax.ShapeDtypeStruct((lines // cross, panel), jnp.float32)] * (planes - 1),
-        in_specs=[pl.BlockSpec(memory_space=pltpu.SMEM), vmem],
+        in_specs=[vmem],
         out_specs=[vmem] * planes,
         scratch_shapes=[
             pltpu.VMEM((node_total, half, panel), jnp.float32),
             pltpu.VMEM((planes, lines, panel), jnp.float32),
         ],
         name="pack",
-    )(spots, rhs_blocks)
+    )(rhs_blocks)
     arrived = jnp.stack([move(packed[o], plane_mask=o) for o in range(1, planes)])
     sides = [arrived] + [move(arrived, cross_mask=m) for m in range(1, cross)]
     part = lines // cross
@@ -183,8 +188,9 @@
     def in_order(parts):
         return jnp.concatenate([parts[reverse(p, bits)] for p in range(planes)], axis=0)
 
-    def pair_core(own):
-        return jnp.concatenate([own, move(own, core_mask=1)], axis=-1)
+    def pair_core(own, count=4):
+        parts = [move(part, core_mask=1) for part in jnp.split(own, count, axis=0)]
+        return jnp.concatenate([own, jnp.concatenate(parts, axis=0)], axis=-1)
 
     diag = [None] * levels
     lower = [None] * levels
@@ -227,31 +233,26 @@
             held = jnp.concatenate([held, move(held, plane_mask=1 << b)], axis=0)
         return held
 
-    gate = lower_pieces[1]
-    for depth in range(last - 1, -1, -1):
-        for kind in (0, 1):
-            if kind and depth == 0:
-                continue
-            blocks = []
-            for s in range(2**depth):
-                node = first[depth] + ((plane >> shift[depth]) ^ s)
-                if kind:
-                    body = pick(lower_blocks, node)
-                    names = pick(update_rows, node).astype(jnp.float32)
-                    owner = ((plane >> shift[depth]) ^ s) << shift[depth]
-                    body = jnp.concatenate(spread_rows(body, names, depth, owner), axis=0)
-                else:
-                    body = pick(diag_inverse, node)
-                blocks.append(after(body, gate))
-            held = spread_planes(gather(blocks, depth), depth)
-            if kind == 0:
-                diag[depth] = pair_core(held)
-            else:
-                wide = pair_core(held).reshape(planes, depth, panel, 2 * piece)
-                lower[depth] = [
-                    wide[:, up].reshape(planes * panel, 2 * piece) for up in range(depth)
-                ]
-            gate = held
+    def lower_block(depth, s):
+        node = first[depth] + ((plane >> shift[depth]) ^ s)
+        owner = ((plane >> shift[depth]) ^ s) << shift[depth]
+        names = pick(update_rows, node).astype(jnp.float32)
+        return jnp.concatenate(spread_rows(pick(lower_blocks, node), names, depth, owner), axis=0)
+
+    def diag_block(depth, s):
+        return pick(diag_inverse, first[depth] + ((plane >> shift[depth]) ^ s))
+
+    gate = lower_pieces[2]
+    far_diag = move(after(diag_block(1, 1), gate), plane_mask=2)
+    held_diag = jnp.concatenate([diag_block(1, 0), far_diag], axis=0)
+    near_diag = move(held_diag, plane_mask=1)
+    diag[1] = pair_core(jnp.concatenate([held_diag, near_diag], axis=0), 4)
+    far_mixed = move(after(jnp.concatenate([lower_block(1, 1), diag_block(0, 0)], axis=0), gate), plane_mask=2)
+    held_lower = jnp.concatenate([lower_block(1, 0), far_mixed[:panel]], axis=0)
+    held_zero = jnp.concatenate([diag_block(0, 0), far_mixed[panel:]], axis=0)
+    near_mixed = move(jnp.concatenate([held_lower, held_zero], axis=0), plane_mask=1)
+    lower[1] = [pair_core(jnp.concatenate([held_lower, near_mixed[: 2 * panel]], axis=0), 4)]
+    diag[0] = pair_core(jnp.concatenate([held_zero, near_mixed[2 * panel :]], axis=0), 4)
 
     forward = [None] * levels
     pending = [None] * levels
@@ -301,13 +302,13 @@
     upper = move(jnp.stack(collected[: planes - 1]), core_mask=1)
     lowest = move(jnp.stack(collected[planes - 1 :]), core_mask=1)
     return pl.pallas_call(
-        functools.partial(finish_kernel, levels, first),
+        functools.partial(finish_kernel, levels, first, inner),
         out_shape=jax.ShapeDtypeStruct(rhs_blocks.shape, jnp.float32),
-        in_specs=[pl.BlockSpec(memory_space=pltpu.SMEM)] + [vmem] * (node_total + 2),
+        in_specs=[vmem] * (node_total + 2),
         out_specs=vmem,
         scratch_shapes=[pltpu.VMEM((2 * node_total, half, panel), jnp.float32)],
         name="finish",
-    )(spots, *collected, upper, lowest)
+    )(*collected, upper, lowest)
 
 
 def solution(mesh):

time: 161 us -> 157 us (0.975)
  starting transfers between devices: 60.8 us -> 56.2 us
    ppermute x47 -> x60, starting transfers between devices: 60.8 us -> 56.2 us  [move(): return lax.ppermute(x, AXES, pairs)]
    ppermute x47 -> x60, waiting for transfers between devices: 75.1 us -> 76.5 us  [move(): return lax.ppermute(x, AXES, pairs)]
  transfers between devices with their start and end apart: 47 -> 60, of which waited for: 23 -> 29; matrix products, arithmetic and copies ran while one was open for 6% -> 6% of each run, Pallas kernels for 1% -> 1%
where the time goes in v3:
time: 157 us
  waiting for transfers between devices  76.5 us (49%)
  starting transfers between devices  56.2 us (36%)
  matrix products  13.3 us (8%)
  local copies, waits for them, and re-layouts  4.89 us (3%)
  Pallas kernels  4.63 us (3%)
    ppermute x60, waiting for transfers between devices, move(): return lax.ppermute(x, AXES, pairs)  76.5 us
    ppermute x60, starting transfers between devices, move(): return lax.ppermute(x, AXES, pairs)  56.2 us
    dot_general x12, matrix products, dot(): lax.dot_general(left, right, (dims, ((), ())), precision=PRECISION, prefe...  11.3 us
  transfers between devices with their start and end apart: 60, of which 29 were waited for; matrix products, arithmetic and copies ran while one was open for 6% of the time, Pallas kernels for 1%

profile of v3, /device:TPU:0, one launch (start us, length us, event | category | flops | bytes accessed | tf_op | source)
XLA Modules:
  0.0 156.6 jit_solution(11760709324900384296)
XLA Ops:
  1.3 3.1 %collective-permute-start.5 = (f32[128,256]{1,0:T(8,128)S(1)}, f32[128,256]{1,0:T(8,128)S(1)}, u32[]{:S(2)}, u32[]{:S(2)}) collective-permute-start(f32[128,256]{1,0:T(8,128)S(1)} %get-tuple-element.26), channel_id=1, source_target_pairs={{0,8},{1,9},{2,10},{3,11},{4,12},{5,13},{6,14},{7,15},{8,0},{9,1},... | collective-permute-start | bytes 393224 | tf_op jit(solution)/shard_map/ppermute | solution.py:120
  6.6 3.0 %collective-permute-start.1 = (f32[112,128]{1,0:T(8,128)}, f32[112,128]{1,0:T(8,128)S(1)}, u32[]{:S(2)}, u32[]{:S(2)}) collective-permute-start(f32[112,128]{1,0:T(8,128)} %get-tuple-element.16), channel_id=1, source_target_pairs={{0,16},{1,17},{2,18},{3,19},{4,20},{5,21},{6,22},{7,23},{8,24},{9,... | collective-permute-start | bytes 172040 | tf_op jit(solution)/shard_map/ppermute | solution.py:120
  10.9 2.5 %collective-permute-start.6 = (f32[128,256]{1,0:T(8,128)S(1)}, f32[128,256]{1,0:T(8,128)S(1)}, u32[]{:S(2)}, u32[]{:S(2)}) collective-permute-start(f32[128,256]{1,0:T(8,128)S(1)} %get-tuple-element.25), channel_id=1, source_target_pairs={{0,24},{1,25},{2,26},{3,27},{4,28},{5,29},{6,30},{7,31},{8,16},{9,... | collective-permute-start | bytes 393224 | tf_op jit(solution)/shard_map/ppermute | solution.py:120
  16.5 5.7 %collective-permute-start.3 = (f32[3,112,128]{2,1,0:T(8,128)S(1)}, f32[3,112,128]{2,1,0:T(8,128)S(1)}, u32[]{:S(2)}, u32[]{:S(2)}) collective-permute-start(f32[3,112,128]{2,1,0:T(8,128)S(1)} %pad_maximum_fusion.12), channel_id=1, source_target_pairs={{0,2},{1,3},{2,0},{3,1},{4,6},{5,7},{6,4},{7,5},{8,10},{9,11},{10,... | collective-permute-start | bytes 516104 | tf_op jit(solution)/shard_map/ppermute | solution.py:120
  22.3 3.1 %collective-permute-start.12 = (f32[136,256]{1,0:T(8,128)S(1)}, f32[136,256]{1,0:T(8,128)S(1)}, u32[]{:S(2)}, u32[]{:S(2)}) collective-permute-start(f32[136,256]{1,0:T(8,128)S(1)} %select_maximum_fusion.2), channel_id=1, source_target_pairs={{0,16},{1,17},{2,18},{3,19},{4,20},{5,21},{6,22},{7,23},{8,24},{9,... | collective-permute-start | bytes 417800 | tf_op jit(solution)/shard_map/ppermute | solution.py:120
  25.3 5.1 %collective-permute-done.4 = f32[128,256]{1,0:T(8,128)S(1)} collective-permute-done((f32[128,256]{1,0:T(8,128)S(1)}, f32[128,256]{1,0:T(8,128)S(1)}, u32[]{:S(2)}, u32[]{:S(2)}) %collective-permute-start.4) | collective-permute-done | bytes 131104 | tf_op jit(solution)/shard_map/ppermute | solution.py:120
  32.8 2.7 %collective-permute-start.14 = (f32[136,256]{1,0:T(8,128)S(1)}, f32[136,256]{1,0:T(8,128)S(1)}, u32[]{:S(2)}, u32[]{:S(2)}) collective-permute-start(f32[136,256]{1,0:T(8,128)S(1)} %get-tuple-element.20), channel_id=1, source_target_pairs={{0,24},{1,25},{2,26},{3,27},{4,28},{5,29},{6,30},{7,31},{8,16},{9,... | collective-permute-start | bytes 417800 | tf_op jit(solution)/shard_map/ppermute | solution.py:120
  37.0 4.3 %collective-permute-done.14 = f32[136,256]{1,0:T(8,128)S(1)} collective-permute-done((f32[136,256]{1,0:T(8,128)S(1)}, f32[136,256]{1,0:T(8,128)S(1)}, u32[]{:S(2)}, u32[]{:S(2)}) %collective-permute-start.14) | collective-permute-done | bytes 139296 | tf_op jit(solution)/shard_map/ppermute | solution.py:120
  41.9 4.6 %collective-permute-done.22 = f32[128,256]{1,0:T(8,128)S(1)} collective-permute-done((f32[128,256]{1,0:T(8,128)S(1)}, f32[128,256]{1,0:T(8,128)S(1)}, u32[]{:S(2)}, u32[]{:S(2)}) %collective-permute-start.22) | collective-permute-done | bytes 131104 | tf_op jit(solution)/shard_map/ppermute | solution.py:120
  48.5 2.9 %collective-permute-start.23 = (f32[256,256]{1,0:T(8,128)S(1)}, f32[256,256]{1,0:T(8,128)S(1)}, u32[]{:S(2)}, u32[]{:S(2)}) collective-permute-start(f32[256,256]{1,0:T(8,128)S(1)} %pad_maximum_fusion.7), channel_id=1, source_target_pairs={{0,8},{1,9},{2,10},{3,11},{4,12},{5,13},{6,14},{7,15},{8,0},{9,1},... | collective-permute-start | bytes 786440 | tf_op jit(solution)/shard_map/ppermute | solution.py:120
  52.8 2.5 %collective-permute-done.11 = f32[128,512]{1,0:T(8,128)S(1)} collective-permute-done((f32[128,512]{1,0:T(8,128)S(1)}, f32[128,512]{1,0:T(8,128)S(1)}, u32[]{:S(2)}, u32[]{:S(2)}) %collective-permute-start.11) | collective-permute-done | bytes 262176 | tf_op jit(solution)/shard_map/ppermute | solution.py:120
  57.9 5.6 %collective-permute-done.23 = f32[256,256]{1,0:T(8,128)S(1)} collective-permute-done((f32[256,256]{1,0:T(8,128)S(1)}, f32[256,256]{1,0:T(8,128)S(1)}, u32[]{:S(2)}, u32[]{:S(2)}) %collective-permute-start.23) | collective-permute-done | bytes 262176 | tf_op jit(solution)/shard_map/ppermute | solution.py:120
  66.2 3.7 %collective-permute-done.21 = f32[64,512]{1,0:T(8,128)S(1)} collective-permute-done((f32[64,512]{1,0:T(8,128)S(1)}, f32[64,512]{1,0:T(8,128)S(1)}, u32[]{:S(2)}, u32[]{:S(2)}) %collective-permute-start.21) | collective-permute-done | bytes 131104 | tf_op jit(solution)/shard_map/ppermute | solution.py:120
  73.5 3.6 %collective-permute-done.28 = f32[64,512]{1,0:T(8,128)S(1)} collective-permute-done((f32[64,512]{1,0:T(8,128)S(1)}, f32[64,512]{1,0:T(8,128)S(1)}, u32[]{:S(2)}, u32[]{:S(2)}) %collective-permute-start.28) | collective-permute-done | bytes 131104 | tf_op jit(solution)/shard_map/ppermute | solution.py:120
  77.1 7.2 %collective-permute-done.30 = f32[512,256]{1,0:T(8,128)S(1)} collective-permute-done((f32[512,256]{1,0:T(8,128)S(1)}, f32[512,256]{1,0:T(8,128)S(1)}, u32[]{:S(2)}, u32[]{:S(2)}) %collective-permute-start.30) | collective-permute-done | bytes 524320 | tf_op jit(solution)/shard_map/ppermute | solution.py:120
  89.7 2.3 %collective-permute-start.36 = (f32[32,512]{1,0:T(8,128)S(1)}, f32[32,512]{1,0:T(8,128)S(1)}, u32[]{:S(2)}, u32[]{:S(2)}) collective-permute-start(f32[32,512]{1,0:T(8,128)S(1)} %slice.348), channel_id=1, source_target_pairs={{0,2},{1,3},{2,0},{3,1},{4,6},{5,7},{6,4},{7,5},{8,10},{9,11},{10,... | collective-permute-start | bytes 196616 | tf_op jit(solution)/shard_map/ppermute | solution.py:120
  92.0 3.5 %collective-permute-done.37 = f32[32,512]{1,0:T(8,128)S(1)} collective-permute-done((f32[32,512]{1,0:T(8,128)S(1)}, f32[32,512]{1,0:T(8,128)S(1)}, u32[]{:S(2)}, u32[]{:S(2)}) %collective-permute-start.37) | collective-permute-done | bytes 65568 | tf_op jit(solution)/shard_map/ppermute | solution.py:120
  97.6 3.8 %collective-permute-done.43 = f32[32,512]{1,0:T(8,128)S(1)} collective-permute-done((f32[32,512]{1,0:T(8,128)S(1)}, f32[32,512]{1,0:T(8,128)S(1)}, u32[]{:S(2)}, u32[]{:S(2)}) %collective-permute-start.43) | collective-permute-done | bytes 65568 | tf_op jit(solution)/shard_map/ppermute | solution.py:120
  104.5 2.4 %collective-permute-start.46 = (f32[32,512]{1,0:T(8,128)S(1)}, f32[32,512]{1,0:T(8,128)S(1)}, u32[]{:S(2)}, u32[]{:S(2)}) collective-permute-start(f32[32,512]{1,0:T(8,128)S(1)} %pad_maximum_fusion.22), channel_id=1, source_target_pairs={{0,18},{1,19},{2,16},{3,17},{4,22},{5,23},{6,20},{7,21},{8,26},{9,... | collective-permute-start | bytes 196616 | tf_op jit(solution)/shard_map/ppermute | solution.py:120
  107.0 3.2 %collective-permute-done.45 = f32[32,512]{1,0:T(8,128)S(1)} collective-permute-done((f32[32,512]{1,0:T(8,128)S(1)}, f32[32,512]{1,0:T(8,128)S(1)}, u32[]{:S(2)}, u32[]{:S(2)}) %collective-permute-start.45) | collective-permute-done | bytes 65568 | tf_op jit(solution)/shard_map/ppermute | solution.py:120
  112.6 4.5 %collective-permute-done.48 = f32[64,512]{1,0:T(8,128)S(1)} collective-permute-done((f32[64,512]{1,0:T(8,128)S(1)}, f32[64,512]{1,0:T(8,128)S(1)}, u32[]{:S(2)}, u32[]{:S(2)}) %collective-permute-start.48) | collective-permute-done | bytes 131104 | tf_op jit(solution)/shard_map/ppermute | solution.py:120
  129.4 5.8 %collective-permute-done.53 = f32[128,512]{1,0:T(8,128)S(1)} collective-permute-done((f32[128,512]{1,0:T(8,128)S(1)}, f32[128,512]{1,0:T(8,128)S(1)}, u32[]{:S(2)}, u32[]{:S(2)}) %collective-permute-start.53) | collective-permute-done | bytes 262176 | tf_op jit(solution)/shard_map/ppermute | solution.py:120
  139.0 3.8 %collective-permute-done.54 = f32[128,512]{1,0:T(8,128)S(1)} collective-permute-done((f32[128,512]{1,0:T(8,128)S(1)}, f32[128,512]{1,0:T(8,128)S(1)}, u32[]{:S(2)}, u32[]{:S(2)}) %collective-permute-start.54) | collective-permute-done | bytes 262176 | tf_op jit(solution)/shard_map/ppermute | solution.py:120
  154.1 2.5 %finish.1 = f32[7,128,256]{2,1,0:T(8,128)} custom-call(f32[128,128]{1,0:T(8,128)} %copy-done.1, f32[128,128]{1,0:T(8,128)} %copy-done.2, f32[128,128]{1,0:T(8,128)} %copy-done.4, f32[128,128]{1,0:T(8,128)} %get-tuple-element.46.refs_3_, f32[128,128]{1,0:T(8,128)} %copy-done.7, f32[128,128]{1,0:T(8,128)} %copy-done.6, f32[128,128]{1,0:T(8,128)} %copy-done.5, ...), custom_call_target="tpu_custom_call" | custom-call | tf_op jit(solution)/shard_map/finish/pallas_call | solution.py:304
  (196 shorter events, 64.6 us)
Async XLA Ops:
  1.3 20.9 %collective-permute-start.5 = (f32[128,256]{1,0:T(8,128)S(1)}, f32[128,256]{1,0:T(8,128)S(1)}, u32[]{:S(2)}, u32[]{:S(2)}) collective-permute-start(f32[128,256]{1,0:T(8,128)S(1)} %get-tuple-element.26), channel_id=1, source_target_pairs={{0,8},{1,9},{2,10},{3,11},{4,12},{5,13},{6,14},{7,15},{8,0},{9,1},... | collective-permute-start | bytes 393224 | tf_op jit(solution)/shard_map/ppermute | solution.py:120
  10.9 14.4 %collective-permute-start.6 = (f32[128,256]{1,0:T(8,128)S(1)}, f32[128,256]{1,0:T(8,128)S(1)}, u32[]{:S(2)}, u32[]{:S(2)}) collective-permute-start(f32[128,256]{1,0:T(8,128)S(1)} %get-tuple-element.25), channel_id=1, source_target_pairs={{0,24},{1,25},{2,26},{3,27},{4,28},{5,29},{6,30},{7,31},{8,16},{9,... | collective-permute-start | bytes 393224 | tf_op jit(solution)/shard_map/ppermute | solution.py:120
  14.7 15.7 %collective-permute-start.4 = (f32[128,256]{1,0:T(8,128)S(1)}, f32[128,256]{1,0:T(8,128)S(1)}, u32[]{:S(2)}, u32[]{:S(2)}) collective-permute-start(f32[128,256]{1,0:T(8,128)S(1)} %get-tuple-element.27), channel_id=1, source_target_pairs={{0,16},{1,17},{2,18},{3,19},{4,20},{5,21},{6,22},{7,23},{8,24},{9,... | collective-permute-start | bytes 393224 | tf_op jit(solution)/shard_map/ppermute | solution.py:120
  14.8 16.2 %collective-permute-start.7 = (f32[128,256]{1,0:T(8,128)S(1)}, f32[128,256]{1,0:T(8,128)S(1)}, u32[]{:S(2)}, u32[]{:S(2)}) collective-permute-start(f32[128,256]{1,0:T(8,128)S(1)} %get-tuple-element.23), channel_id=1, source_target_pairs={{0,1},{1,0},{2,3},{3,2},{4,5},{5,4},{6,7},{7,6},{8,9},{9,8},{10,11... | collective-permute-start | bytes 393224 | tf_op jit(solution)/shard_map/ppermute | solution.py:120
  16.5 13.9 %collective-permute-start.3 = (f32[3,112,128]{2,1,0:T(8,128)S(1)}, f32[3,112,128]{2,1,0:T(8,128)S(1)}, u32[]{:S(2)}, u32[]{:S(2)}) collective-permute-start(f32[3,112,128]{2,1,0:T(8,128)S(1)} %pad_maximum_fusion.12), channel_id=1, source_target_pairs={{0,2},{1,3},{2,0},{3,1},{4,6},{5,7},{6,4},{7,5},{8,10},{9,11},{10,... | collective-permute-start | bytes 516104 | tf_op jit(solution)/shard_map/ppermute | solution.py:120
  22.3 10.6 %collective-permute-start.12 = (f32[136,256]{1,0:T(8,128)S(1)}, f32[136,256]{1,0:T(8,128)S(1)}, u32[]{:S(2)}, u32[]{:S(2)}) collective-permute-start(f32[136,256]{1,0:T(8,128)S(1)} %select_maximum_fusion.2), channel_id=1, source_target_pairs={{0,16},{1,17},{2,18},{3,19},{4,20},{5,21},{6,22},{7,23},{8,24},{9,... | collective-permute-start | bytes 417800 | tf_op jit(solution)/shard_map/ppermute | solution.py:120
  25.3 10.4 %collective-permute-start.9 = (f32[128,256]{1,0:T(8,128)S(1)}, f32[128,256]{1,0:T(8,128)S(1)}, u32[]{:S(2)}, u32[]{:S(2)}) collective-permute-start(f32[128,256]{1,0:T(8,128)S(1)} %collective-permute-done.5), channel_id=1, source_target_pairs={{0,1},{1,0},{2,3},{3,2},{4,5},{5,4},{6,7},{7,6},{8,9},{9,8},{10,11... | collective-permute-start | bytes 393224 | tf_op jit(solution)/shard_map/ppermute | solution.py:120
  32.8 8.5 %collective-permute-start.14 = (f32[136,256]{1,0:T(8,128)S(1)}, f32[136,256]{1,0:T(8,128)S(1)}, u32[]{:S(2)}, u32[]{:S(2)}) collective-permute-start(f32[136,256]{1,0:T(8,128)S(1)} %get-tuple-element.20), channel_id=1, source_target_pairs={{0,24},{1,25},{2,26},{3,27},{4,28},{5,29},{6,30},{7,31},{8,16},{9,... | collective-permute-start | bytes 417800 | tf_op jit(solution)/shard_map/ppermute | solution.py:120
  35.6 10.9 %collective-permute-start.15 = (f32[1,136,256]{2,1,0:T(8,128)S(1)}, f32[1,136,256]{2,1,0:T(8,128)S(1)}, u32[]{:S(2)}, u32[]{:S(2)}) collective-permute-start(f32[1,136,256]{2,1,0:T(8,128)S(1)} %fusion.30), channel_id=1, source_target_pairs={{0,1},{1,0},{2,3},{3,2},{4,5},{5,4},{6,7},{7,6},{8,9},{9,8},{10,11... | collective-permute-start | bytes 417800 | tf_op jit(solution)/shard_map/ppermute | solution.py:120
  35.7 10.8 %collective-permute-start.22 = (f32[128,256]{1,0:T(8,128)S(1)}, f32[128,256]{1,0:T(8,128)S(1)}, u32[]{:S(2)}, u32[]{:S(2)}) collective-permute-start(f32[128,256]{1,0:T(8,128)S(1)} %get-tuple-element.21), channel_id=1, source_target_pairs={{0,16},{1,17},{2,18},{3,19},{4,20},{5,21},{6,22},{7,23},{8,24},{9,... | collective-permute-start | bytes 393224 | tf_op jit(solution)/shard_map/ppermute | solution.py:120
  36.6 11.5 %collective-permute-start.17 = (f32[1,136,256]{2,1,0:T(8,128)S(1)}, f32[1,136,256]{2,1,0:T(8,128)S(1)}, u32[]{:S(2)}, u32[]{:S(2)}) collective-permute-start(f32[1,136,256]{2,1,0:T(8,128)S(1)} %bitcast.96), channel_id=1, source_target_pairs={{0,1},{1,0},{2,3},{3,2},{4,5},{5,4},{6,7},{7,6},{8,9},{9,8},{10,11... | collective-permute-start | bytes 417800 | tf_op jit(solution)/shard_map/ppermute | solution.py:120
  41.3 10.0 %collective-permute-start.16 = (f32[1,136,256]{2,1,0:T(8,128)S(1)}, f32[1,136,256]{2,1,0:T(8,128)S(1)}, u32[]{:S(2)}, u32[]{:S(2)}) collective-permute-start(f32[1,136,256]{2,1,0:T(8,128)S(1)} %bitcast.92), channel_id=1, source_target_pairs={{0,1},{1,0},{2,3},{3,2},{4,5},{5,4},{6,7},{7,6},{8,9},{9,8},{10,11... | collective-permute-start | bytes 417800 | tf_op jit(solution)/shard_map/ppermute | solution.py:120
  46.5 17.7 %collective-permute-start.24 = (f32[128,256]{1,0:T(8,128)S(1)}, f32[128,256]{1,0:T(8,128)S(1)}, u32[]{:S(2)}, u32[]{:S(2)}) collective-permute-start(f32[128,256]{1,0:T(8,128)S(1)} %get-tuple-element.24), channel_id=1, source_target_pairs={{0,1},{1,0},{2,3},{3,2},{4,5},{5,4},{6,7},{7,6},{8,9},{9,8},{10,11... | collective-permute-start | bytes 393224 | tf_op jit(solution)/shard_map/ppermute | solution.py:120
  46.5 8.8 %collective-permute-start.11 = (f32[128,512]{1,0:T(8,128)S(1)}, f32[128,512]{1,0:T(8,128)S(1)}, u32[]{:S(2)}, u32[]{:S(2)}) collective-permute-start(f32[128,512]{1,0:T(8,128)S(1)} %fusion.1), channel_id=1, source_target_pairs={{0,4},{1,5},{2,6},{3,7},{4,0},{5,1},{6,2},{7,3},{8,12},{9,13},{10,... | collective-permute-start | bytes 786440 | tf_op jit(solution)/shard_map/ppermute | solution.py:120
  48.1 16.9 %collective-permute-start.29 = (f32[256,256]{1,0:T(8,128)S(1)}, f32[256,256]{1,0:T(8,128)S(1)}, u32[]{:S(2)}, u32[]{:S(2)}) collective-permute-start(f32[256,256]{1,0:T(8,128)S(1)} %pad_maximum_fusion.8), channel_id=1, source_target_pairs={{0,16},{1,17},{2,18},{3,19},{4,20},{5,21},{6,22},{7,23},{8,24},{9,... | collective-permute-start | bytes 786440 | tf_op jit(solution)/shard_map/ppermute | solution.py:120
  48.5 15.0 %collective-permute-start.23 = (f32[256,256]{1,0:T(8,128)S(1)}, f32[256,256]{1,0:T(8,128)S(1)}, u32[]{:S(2)}, u32[]{:S(2)}) collective-permute-start(f32[256,256]{1,0:T(8,128)S(1)} %pad_maximum_fusion.7), channel_id=1, source_target_pairs={{0,8},{1,9},{2,10},{3,11},{4,12},{5,13},{6,14},{7,15},{8,0},{9,1},... | collective-permute-start | bytes 786440 | tf_op jit(solution)/shard_map/ppermute | solution.py:120
  51.3 13.7 %collective-permute-start.25 = (f32[128,256]{1,0:T(8,128)S(1)}, f32[128,256]{1,0:T(8,128)S(1)}, u32[]{:S(2)}, u32[]{:S(2)}) collective-permute-start(f32[128,256]{1,0:T(8,128)S(1)} %collective-permute-done.22), channel_id=1, source_target_pairs={{0,1},{1,0},{2,3},{3,2},{4,5},{5,4},{6,7},{7,6},{8,9},{9,8},{10,11... | collective-permute-start | bytes 393224 | tf_op jit(solution)/shard_map/ppermute | solution.py:120
  57.8 8.5 %collective-permute-start.20 = (f32[64,512]{1,0:T(8,128)S(1)}, f32[64,512]{1,0:T(8,128)S(1)}, u32[]{:S(2)}, u32[]{:S(2)}) collective-permute-start(f32[64,512]{1,0:T(8,128)S(1)} %pad_maximum_fusion.14), channel_id=1, source_target_pairs={{0,8},{1,9},{2,10},{3,11},{4,12},{5,13},{6,14},{7,15},{8,0},{9,1},... | collective-permute-start | bytes 393224 | tf_op jit(solution)/shard_map/ppermute | solution.py:120
  66.2 18.8 %collective-permute-start.31 = (f32[128,256]{1,0:T(8,128)S(1)}, f32[128,256]{1,0:T(8,128)S(1)}, u32[]{:S(2)}, u32[]{:S(2)}) collective-permute-start(f32[128,256]{1,0:T(8,128)S(1)} %fusion.39), channel_id=1, source_target_pairs={{0,1},{1,0},{2,3},{3,2},{4,5},{5,4},{6,7},{7,6},{8,9},{9,8},{10,11... | collective-permute-start | bytes 393224 | tf_op jit(solution)/shard_map/ppermute | solution.py:120
  70.0 14.4 %collective-permute-start.30 = (f32[512,256]{1,0:T(8,128)S(1)}, f32[512,256]{1,0:T(8,128)S(1)}, u32[]{:S(2)}, u32[]{:S(2)}) collective-permute-start(f32[512,256]{1,0:T(8,128)S(1)} %pad_maximum_fusion.6), channel_id=1, source_target_pairs={{0,8},{1,9},{2,10},{3,11},{4,12},{5,13},{6,14},{7,15},{8,0},{9,1},... | collective-permute-start | bytes 1572872 | tf_op jit(solution)/shard_map/ppermute | solution.py:120
  72.7 13.1 %collective-permute-start.35 = (f32[64,512]{1,0:T(8,128)S(1)}, f32[64,512]{1,0:T(8,128)S(1)}, u32[]{:S(2)}, u32[]{:S(2)}) collective-permute-start(f32[64,512]{1,0:T(8,128)S(1)} %pad_maximum_fusion.15), channel_id=1, source_target_pairs={{0,8},{1,9},{2,10},{3,11},{4,12},{5,13},{6,14},{7,15},{8,0},{9,1},... | collective-permute-start | bytes 393224 | tf_op jit(solution)/shard_map/ppermute | solution.py:120
  73.5 12.3 %collective-permute-start.32 = (f32[128,256]{1,0:T(8,128)S(1)}, f32[128,256]{1,0:T(8,128)S(1)}, u32[]{:S(2)}, u32[]{:S(2)}) collective-permute-start(f32[128,256]{1,0:T(8,128)S(1)} %get-tuple-element.63), channel_id=1, source_target_pairs={{0,1},{1,0},{2,3},{3,2},{4,5},{5,4},{6,7},{7,6},{8,9},{9,8},{10,11... | collective-permute-start | bytes 393224 | tf_op jit(solution)/shard_map/ppermute | solution.py:120
  87.7 8.6 %collective-permute-start.38 = (f32[32,512]{1,0:T(8,128)S(1)}, f32[32,512]{1,0:T(8,128)S(1)}, u32[]{:S(2)}, u32[]{:S(2)}) collective-permute-start(f32[32,512]{1,0:T(8,128)S(1)} %pad_maximum_fusion.21), channel_id=1, source_target_pairs={{0,18},{1,19},{2,16},{3,17},{4,22},{5,23},{6,20},{7,21},{8,26},{9,... | collective-permute-start | bytes 196616 | tf_op jit(solution)/shard_map/ppermute | solution.py:120
  137.3 13.8 %collective-permute-start.52 = (f32[128,128]{1,0:T(8,128)S(1)}, f32[128,128]{1,0:T(8,128)S(1)}, u32[]{:S(2)}, u32[]{:S(2)}) collective-permute-start(f32[128,128]{1,0:T(8,128)S(1)} %pad_maximum_fusion.23), channel_id=1, source_target_pairs={{0,16},{1,17},{2,18},{3,19},{4,20},{5,21},{6,22},{7,23},{8,24},{9,... | collective-permute-start | bytes 196616 | tf_op jit(solution)/shard_map/ppermute | solution.py:120
  (47 other events, 255.0 us)

commit v4 on v3

--- a/solution.py
+++ b/solution.py
@@ -194,7 +194,7 @@
 
     diag = [None] * levels
     lower = [None] * levels
-    diag[last] = pair_core(in_order(diag_pieces))
+    diag[last] = pair_core(in_order(diag_pieces), 4)
 
     def tagged(index):
         names = pick(update_rows, index).astype(jnp.float32)[None, :]
@@ -216,7 +216,7 @@
             result.append(jnp.matmul(chosen, body, precision=lax.Precision.HIGHEST))
         return result
 
-    both = pair_core(jnp.stack([lower_pieces[reverse(p, bits)] for p in range(planes)]))
+    both = pair_core(jnp.stack([lower_pieces[reverse(p, bits)] for p in range(planes)]), 4)
     lower[last] = [
         block.reshape(planes * panel, 2 * piece)
         for block in spread_rows(both[:, :panel], both[:, panel, :panel], last, plane)
@@ -246,13 +246,13 @@
     far_diag = move(after(diag_block(1, 1), gate), plane_mask=2)
     held_diag = jnp.concatenate([diag_block(1, 0), far_diag], axis=0)
     near_diag = move(held_diag, plane_mask=1)
-    diag[1] = pair_core(jnp.concatenate([held_diag, near_diag], axis=0), 4)
+    diag[1] = pair_core(jnp.concatenate([held_diag, near_diag], axis=0), 1)
     far_mixed = move(after(jnp.concatenate([lower_block(1, 1), diag_block(0, 0)], axis=0), gate), plane_mask=2)
     held_lower = jnp.concatenate([lower_block(1, 0), far_mixed[:panel]], axis=0)
     held_zero = jnp.concatenate([diag_block(0, 0), far_mixed[panel:]], axis=0)
     near_mixed = move(jnp.concatenate([held_lower, held_zero], axis=0), plane_mask=1)
     lower[1] = [pair_core(jnp.concatenate([held_lower, near_mixed[: 2 * panel]], axis=0), 4)]
-    diag[0] = pair_core(jnp.concatenate([held_zero, near_mixed[2 * panel :]], axis=0), 4)
+    diag[0] = pair_core(jnp.concatenate([held_zero, near_mixed[2 * panel :]], axis=0), 1)
 
     forward = [None] * levels
     pending = [None] * levels

time: 157 us -> 152 us (0.968)
  waiting for transfers between devices: 76.5 us -> 71.6 us
    ppermute x60 -> x54, waiting for transfers between devices: 76.5 us -> 71.6 us  [move(): return lax.ppermute(x, AXES, pairs)]
    ppermute x60 -> x54, starting transfers between devices: 56.2 us -> 56.2 us  [move(): return lax.ppermute(x, AXES, pairs)]
  transfers between devices with their start and end apart: 60 -> 54, of which waited for: 29 -> 26; matrix products, arithmetic and copies ran while one was open for 6% -> 6% of each run, Pallas kernels for 1% -> 1%
where the time goes in v4:
time: 152 us
  waiting for transfers between devices  71.6 us (47%)
  starting transfers between devices  56.2 us (37%)
  matrix products  13.3 us (9%)
  local copies, waits for them, and re-layouts  4.79 us (3%)
  Pallas kernels  4.63 us (3%)
    ppermute x54, waiting for transfers between devices, move(): return lax.ppermute(x, AXES, pairs)  71.6 us
    ppermute x54, starting transfers between devices, move(): return lax.ppermute(x, AXES, pairs)  56.2 us
    dot_general x12, matrix products, dot(): lax.dot_general(left, right, (dims, ((), ())), precision=PRECISION, prefe...  11.3 us
  transfers between devices with their start and end apart: 54, of which 26 were waited for; matrix products, arithmetic and copies ran while one was open for 6% of the time, Pallas kernels for 1%

profile of v4, /device:TPU:0, one launch (start us, length us, event | category | flops | bytes accessed | tf_op | source)
XLA Modules:
  0.0 151.8 jit_solution(8412447364892036921)
XLA Ops:
  1.3 3.1 %collective-permute-start.5 = (f32[128,256]{1,0:T(8,128)S(1)}, f32[128,256]{1,0:T(8,128)S(1)}, u32[]{:S(2)}, u32[]{:S(2)}) collective-permute-start(f32[128,256]{1,0:T(8,128)S(1)} %get-tuple-element.26), channel_id=1, source_target_pairs={{0,8},{1,9},{2,10},{3,11},{4,12},{5,13},{6,14},{7,15},{8,0},{9,1},... | collective-permute-start | bytes 393224 | tf_op jit(solution)/shard_map/ppermute | solution.py:120
  6.6 3.0 %collective-permute-start.1 = (f32[112,128]{1,0:T(8,128)}, f32[112,128]{1,0:T(8,128)S(1)}, u32[]{:S(2)}, u32[]{:S(2)}) collective-permute-start(f32[112,128]{1,0:T(8,128)} %get-tuple-element.16), channel_id=1, source_target_pairs={{0,16},{1,17},{2,18},{3,19},{4,20},{5,21},{6,22},{7,23},{8,24},{9,... | collective-permute-start | bytes 172040 | tf_op jit(solution)/shard_map/ppermute | solution.py:120
  10.9 2.5 %collective-permute-start.6 = (f32[128,256]{1,0:T(8,128)S(1)}, f32[128,256]{1,0:T(8,128)S(1)}, u32[]{:S(2)}, u32[]{:S(2)}) collective-permute-start(f32[128,256]{1,0:T(8,128)S(1)} %get-tuple-element.25), channel_id=1, source_target_pairs={{0,24},{1,25},{2,26},{3,27},{4,28},{5,29},{6,30},{7,31},{8,16},{9,... | collective-permute-start | bytes 393224 | tf_op jit(solution)/shard_map/ppermute | solution.py:120
  16.5 5.7 %collective-permute-start.3 = (f32[3,112,128]{2,1,0:T(8,128)S(1)}, f32[3,112,128]{2,1,0:T(8,128)S(1)}, u32[]{:S(2)}, u32[]{:S(2)}) collective-permute-start(f32[3,112,128]{2,1,0:T(8,128)S(1)} %pad_maximum_fusion.20), channel_id=1, source_target_pairs={{0,2},{1,3},{2,0},{3,1},{4,6},{5,7},{6,4},{7,5},{8,10},{9,11},{10,... | collective-permute-start | bytes 516104 | tf_op jit(solution)/shard_map/ppermute | solution.py:120
  22.3 3.1 %collective-permute-start.12 = (f32[136,256]{1,0:T(8,128)S(1)}, f32[136,256]{1,0:T(8,128)S(1)}, u32[]{:S(2)}, u32[]{:S(2)}) collective-permute-start(f32[136,256]{1,0:T(8,128)S(1)} %select_maximum_fusion.2), channel_id=1, source_target_pairs={{0,16},{1,17},{2,18},{3,19},{4,20},{5,21},{6,22},{7,23},{8,24},{9,... | collective-permute-start | bytes 417800 | tf_op jit(solution)/shard_map/ppermute | solution.py:120
  25.3 5.1 %collective-permute-done.4 = f32[128,256]{1,0:T(8,128)S(1)} collective-permute-done((f32[128,256]{1,0:T(8,128)S(1)}, f32[128,256]{1,0:T(8,128)S(1)}, u32[]{:S(2)}, u32[]{:S(2)}) %collective-permute-start.4) | collective-permute-done | bytes 131104 | tf_op jit(solution)/shard_map/ppermute | solution.py:120
  32.8 2.7 %collective-permute-start.14 = (f32[136,256]{1,0:T(8,128)S(1)}, f32[136,256]{1,0:T(8,128)S(1)}, u32[]{:S(2)}, u32[]{:S(2)}) collective-permute-start(f32[136,256]{1,0:T(8,128)S(1)} %get-tuple-element.20), channel_id=1, source_target_pairs={{0,24},{1,25},{2,26},{3,27},{4,28},{5,29},{6,30},{7,31},{8,16},{9,... | collective-permute-start | bytes 417800 | tf_op jit(solution)/shard_map/ppermute | solution.py:120
  37.0 4.3 %collective-permute-done.14 = f32[136,256]{1,0:T(8,128)S(1)} collective-permute-done((f32[136,256]{1,0:T(8,128)S(1)}, f32[136,256]{1,0:T(8,128)S(1)}, u32[]{:S(2)}, u32[]{:S(2)}) %collective-permute-start.14) | collective-permute-done | bytes 139296 | tf_op jit(solution)/shard_map/ppermute | solution.py:120
  41.9 4.6 %collective-permute-done.22 = f32[128,256]{1,0:T(8,128)S(1)} collective-permute-done((f32[128,256]{1,0:T(8,128)S(1)}, f32[128,256]{1,0:T(8,128)S(1)}, u32[]{:S(2)}, u32[]{:S(2)}) %collective-permute-start.22) | collective-permute-done | bytes 131104 | tf_op jit(solution)/shard_map/ppermute | solution.py:120
  48.4 2.9 %collective-permute-start.23 = (f32[256,256]{1,0:T(8,128)S(1)}, f32[256,256]{1,0:T(8,128)S(1)}, u32[]{:S(2)}, u32[]{:S(2)}) collective-permute-start(f32[256,256]{1,0:T(8,128)S(1)} %pad_maximum_fusion.15), channel_id=1, source_target_pairs={{0,8},{1,9},{2,10},{3,11},{4,12},{5,13},{6,14},{7,15},{8,0},{9,1},... | collective-permute-start | bytes 786440 | tf_op jit(solution)/shard_map/ppermute | solution.py:120
  56.0 2.9 %collective-permute-start.21 = (f32[64,512]{1,0:T(8,128)S(1)}, f32[64,512]{1,0:T(8,128)S(1)}, u32[]{:S(2)}, u32[]{:S(2)}) collective-permute-start(f32[64,512]{1,0:T(8,128)S(1)} %pad_maximum_fusion.22), channel_id=1, source_target_pairs={{0,10},{1,11},{2,8},{3,9},{4,14},{5,15},{6,12},{7,13},{8,2},{9,3},... | collective-permute-start | bytes 393224 | tf_op jit(solution)/shard_map/ppermute | solution.py:120
  65.3 3.7 %collective-permute-done.21 = f32[64,512]{1,0:T(8,128)S(1)} collective-permute-done((f32[64,512]{1,0:T(8,128)S(1)}, f32[64,512]{1,0:T(8,128)S(1)}, u32[]{:S(2)}, u32[]{:S(2)}) %collective-permute-start.21) | collective-permute-done | bytes 131104 | tf_op jit(solution)/shard_map/ppermute | solution.py:120
  71.0 8.3 %collective-permute-done.27 = f32[512,256]{1,0:T(8,128)S(1)} collective-permute-done((f32[512,256]{1,0:T(8,128)S(1)}, f32[512,256]{1,0:T(8,128)S(1)}, u32[]{:S(2)}, u32[]{:S(2)}) %collective-permute-start.27) | collective-permute-done | bytes 524320 | tf_op jit(solution)/shard_map/ppermute | solution.py:120
  83.3 3.5 %collective-permute-start.35 = (f32[32,512]{1,0:T(8,128)S(1)}, f32[32,512]{1,0:T(8,128)S(1)}, u32[]{:S(2)}, u32[]{:S(2)}) collective-permute-start(f32[32,512]{1,0:T(8,128)S(1)} %pad_maximum_fusion.29), channel_id=1, source_target_pairs={{0,18},{1,19},{2,16},{3,17},{4,22},{5,23},{6,20},{7,21},{8,26},{9,... | collective-permute-start | bytes 196616 | tf_op jit(solution)/shard_map/ppermute | solution.py:120
  87.4 2.2 %collective-permute-done.34 = f32[32,512]{1,0:T(8,128)S(1)} collective-permute-done((f32[32,512]{1,0:T(8,128)S(1)}, f32[32,512]{1,0:T(8,128)S(1)}, u32[]{:S(2)}, u32[]{:S(2)}) %collective-permute-start.34) | collective-permute-done | bytes 65568 | tf_op jit(solution)/shard_map/ppermute | solution.py:120
  89.7 2.9 %collective-permute-done.35 = f32[32,512]{1,0:T(8,128)S(1)} collective-permute-done((f32[32,512]{1,0:T(8,128)S(1)}, f32[32,512]{1,0:T(8,128)S(1)}, u32[]{:S(2)}, u32[]{:S(2)}) %collective-permute-start.35) | collective-permute-done | bytes 65568 | tf_op jit(solution)/shard_map/ppermute | solution.py:120
  93.9 3.8 %collective-permute-done.37 = f32[32,512]{1,0:T(8,128)S(1)} collective-permute-done((f32[32,512]{1,0:T(8,128)S(1)}, f32[32,512]{1,0:T(8,128)S(1)}, u32[]{:S(2)}, u32[]{:S(2)}) %collective-permute-start.37) | collective-permute-done | bytes 65568 | tf_op jit(solution)/shard_map/ppermute | solution.py:120
  99.8 3.3 %collective-permute-start.40 = (f32[32,512]{1,0:T(8,128)S(1)}, f32[32,512]{1,0:T(8,128)S(1)}, u32[]{:S(2)}, u32[]{:S(2)}) collective-permute-start(f32[32,512]{1,0:T(8,128)S(1)} %pad_maximum_fusion.30), channel_id=1, source_target_pairs={{0,18},{1,19},{2,16},{3,17},{4,22},{5,23},{6,20},{7,21},{8,26},{9,... | collective-permute-start | bytes 196616 | tf_op jit(solution)/shard_map/ppermute | solution.py:120
  108.0 5.0 %collective-permute-done.42 = f32[64,512]{1,0:T(8,128)S(1)} collective-permute-done((f32[64,512]{1,0:T(8,128)S(1)}, f32[64,512]{1,0:T(8,128)S(1)}, u32[]{:S(2)}, u32[]{:S(2)}) %collective-permute-start.42) | collective-permute-done | bytes 131104 | tf_op jit(solution)/shard_map/ppermute | solution.py:120
  119.8 2.5 %collective-permute-done.45 = f32[64,512]{1,0:T(8,128)S(1)} collective-permute-done((f32[64,512]{1,0:T(8,128)S(1)}, f32[64,512]{1,0:T(8,128)S(1)}, u32[]{:S(2)}, u32[]{:S(2)}) %collective-permute-start.45) | collective-permute-done | bytes 131104 | tf_op jit(solution)/shard_map/ppermute | solution.py:120
  124.4 5.8 %collective-permute-done.47 = f32[128,512]{1,0:T(8,128)S(1)} collective-permute-done((f32[128,512]{1,0:T(8,128)S(1)}, f32[128,512]{1,0:T(8,128)S(1)}, u32[]{:S(2)}, u32[]{:S(2)}) %collective-permute-start.47) | collective-permute-done | bytes 262176 | tf_op jit(solution)/shard_map/ppermute | solution.py:120
  134.1 3.6 %collective-permute-done.48 = f32[128,512]{1,0:T(8,128)S(1)} collective-permute-done((f32[128,512]{1,0:T(8,128)S(1)}, f32[128,512]{1,0:T(8,128)S(1)}, u32[]{:S(2)}, u32[]{:S(2)}) %collective-permute-start.48) | collective-permute-done | bytes 262176 | tf_op jit(solution)/shard_map/ppermute | solution.py:120
  137.8 2.2 %collective-permute-start.51 = (f32[128,128]{1,0:T(8,128)S(1)}, f32[128,128]{1,0:T(8,128)S(1)}, u32[]{:S(2)}, u32[]{:S(2)}) collective-permute-start(f32[128,128]{1,0:T(8,128)S(1)} %pad_maximum_fusion.34), channel_id=1, source_target_pairs={{0,24},{1,25},{2,26},{3,27},{4,28},{5,29},{6,30},{7,31},{8,16},{9,... | collective-permute-start | bytes 196616 | tf_op jit(solution)/shard_map/ppermute | solution.py:120
  149.3 2.5 %finish.1 = f32[7,128,256]{2,1,0:T(8,128)} custom-call(f32[128,128]{1,0:T(8,128)} %copy-done.1, f32[128,128]{1,0:T(8,128)} %copy-done.2, f32[128,128]{1,0:T(8,128)} %copy-done.4, f32[128,128]{1,0:T(8,128)} %get-tuple-element.44.refs_3_, f32[128,128]{1,0:T(8,128)} %copy-done.7, f32[128,128]{1,0:T(8,128)} %copy-done.6, f32[128,128]{1,0:T(8,128)} %copy-done.5, ...), custom_call_target="tpu_custom_call" | custom-call | tf_op jit(solution)/shard_map/finish/pallas_call | solution.py:304
  (185 shorter events, 61.8 us)
Async XLA Ops:
  1.3 20.9 %collective-permute-start.5 = (f32[128,256]{1,0:T(8,128)S(1)}, f32[128,256]{1,0:T(8,128)S(1)}, u32[]{:S(2)}, u32[]{:S(2)}) collective-permute-start(f32[128,256]{1,0:T(8,128)S(1)} %get-tuple-element.26), channel_id=1, source_target_pairs={{0,8},{1,9},{2,10},{3,11},{4,12},{5,13},{6,14},{7,15},{8,0},{9,1},... | collective-permute-start | bytes 393224 | tf_op jit(solution)/shard_map/ppermute | solution.py:120
  10.9 14.4 %collective-permute-start.6 = (f32[128,256]{1,0:T(8,128)S(1)}, f32[128,256]{1,0:T(8,128)S(1)}, u32[]{:S(2)}, u32[]{:S(2)}) collective-permute-start(f32[128,256]{1,0:T(8,128)S(1)} %get-tuple-element.25), channel_id=1, source_target_pairs={{0,24},{1,25},{2,26},{3,27},{4,28},{5,29},{6,30},{7,31},{8,16},{9,... | collective-permute-start | bytes 393224 | tf_op jit(solution)/shard_map/ppermute | solution.py:120
  14.7 15.7 %collective-permute-start.4 = (f32[128,256]{1,0:T(8,128)S(1)}, f32[128,256]{1,0:T(8,128)S(1)}, u32[]{:S(2)}, u32[]{:S(2)}) collective-permute-start(f32[128,256]{1,0:T(8,128)S(1)} %get-tuple-element.27), channel_id=1, source_target_pairs={{0,16},{1,17},{2,18},{3,19},{4,20},{5,21},{6,22},{7,23},{8,24},{9,... | collective-permute-start | bytes 393224 | tf_op jit(solution)/shard_map/ppermute | solution.py:120
  14.8 16.2 %collective-permute-start.7 = (f32[128,256]{1,0:T(8,128)S(1)}, f32[128,256]{1,0:T(8,128)S(1)}, u32[]{:S(2)}, u32[]{:S(2)}) collective-permute-start(f32[128,256]{1,0:T(8,128)S(1)} %get-tuple-element.23), channel_id=1, source_target_pairs={{0,1},{1,0},{2,3},{3,2},{4,5},{5,4},{6,7},{7,6},{8,9},{9,8},{10,11... | collective-permute-start | bytes 393224 | tf_op jit(solution)/shard_map/ppermute | solution.py:120
  16.5 13.9 %collective-permute-start.3 = (f32[3,112,128]{2,1,0:T(8,128)S(1)}, f32[3,112,128]{2,1,0:T(8,128)S(1)}, u32[]{:S(2)}, u32[]{:S(2)}) collective-permute-start(f32[3,112,128]{2,1,0:T(8,128)S(1)} %pad_maximum_fusion.20), channel_id=1, source_target_pairs={{0,2},{1,3},{2,0},{3,1},{4,6},{5,7},{6,4},{7,5},{8,10},{9,11},{10,... | collective-permute-start | bytes 516104 | tf_op jit(solution)/shard_map/ppermute | solution.py:120
  22.3 10.6 %collective-permute-start.12 = (f32[136,256]{1,0:T(8,128)S(1)}, f32[136,256]{1,0:T(8,128)S(1)}, u32[]{:S(2)}, u32[]{:S(2)}) collective-permute-start(f32[136,256]{1,0:T(8,128)S(1)} %select_maximum_fusion.2), channel_id=1, source_target_pairs={{0,16},{1,17},{2,18},{3,19},{4,20},{5,21},{6,22},{7,23},{8,24},{9,... | collective-permute-start | bytes 417800 | tf_op jit(solution)/shard_map/ppermute | solution.py:120
  25.3 10.4 %collective-permute-start.9 = (f32[128,256]{1,0:T(8,128)S(1)}, f32[128,256]{1,0:T(8,128)S(1)}, u32[]{:S(2)}, u32[]{:S(2)}) collective-permute-start(f32[128,256]{1,0:T(8,128)S(1)} %collective-permute-done.5), channel_id=1, source_target_pairs={{0,1},{1,0},{2,3},{3,2},{4,5},{5,4},{6,7},{7,6},{8,9},{9,8},{10,11... | collective-permute-start | bytes 393224 | tf_op jit(solution)/shard_map/ppermute | solution.py:120
  35.6 12.4 %collective-permute-start.15 = (f32[1,136,256]{2,1,0:T(8,128)S(1)}, f32[1,136,256]{2,1,0:T(8,128)S(1)}, u32[]{:S(2)}, u32[]{:S(2)}) collective-permute-start(f32[1,136,256]{2,1,0:T(8,128)S(1)} %fusion.30), channel_id=1, source_target_pairs={{0,1},{1,0},{2,3},{3,2},{4,5},{5,4},{6,7},{7,6},{8,9},{9,8},{10,11... | collective-permute-start | bytes 417800 | tf_op jit(solution)/shard_map/ppermute | solution.py:120
  35.7 10.8 %collective-permute-start.22 = (f32[128,256]{1,0:T(8,128)S(1)}, f32[128,256]{1,0:T(8,128)S(1)}, u32[]{:S(2)}, u32[]{:S(2)}) collective-permute-start(f32[128,256]{1,0:T(8,128)S(1)} %get-tuple-element.21), channel_id=1, source_target_pairs={{0,16},{1,17},{2,18},{3,19},{4,20},{5,21},{6,22},{7,23},{8,24},{9,... | collective-permute-start | bytes 393224 | tf_op jit(solution)/shard_map/ppermute | solution.py:120
  36.6 11.8 %collective-permute-start.17 = (f32[1,136,256]{2,1,0:T(8,128)S(1)}, f32[1,136,256]{2,1,0:T(8,128)S(1)}, u32[]{:S(2)}, u32[]{:S(2)}) collective-permute-start(f32[1,136,256]{2,1,0:T(8,128)S(1)} %bitcast.96), channel_id=1, source_target_pairs={{0,1},{1,0},{2,3},{3,2},{4,5},{5,4},{6,7},{7,6},{8,9},{9,8},{10,11... | collective-permute-start | bytes 417800 | tf_op jit(solution)/shard_map/ppermute | solution.py:120
  41.3 10.0 %collective-permute-start.18 = (f32[1,136,256]{2,1,0:T(8,128)S(1)}, f32[1,136,256]{2,1,0:T(8,128)S(1)}, u32[]{:S(2)}, u32[]{:S(2)}) collective-permute-start(f32[1,136,256]{2,1,0:T(8,128)S(1)} %bitcast.100), channel_id=1, source_target_pairs={{0,1},{1,0},{2,3},{3,2},{4,5},{5,4},{6,7},{7,6},{8,9},{9,8},{10,11... | collective-permute-start | bytes 417800 | tf_op jit(solution)/shard_map/ppermute | solution.py:120
  41.3 10.0 %collective-permute-start.16 = (f32[1,136,256]{2,1,0:T(8,128)S(1)}, f32[1,136,256]{2,1,0:T(8,128)S(1)}, u32[]{:S(2)}, u32[]{:S(2)}) collective-permute-start(f32[1,136,256]{2,1,0:T(8,128)S(1)} %bitcast.92), channel_id=1, source_target_pairs={{0,1},{1,0},{2,3},{3,2},{4,5},{5,4},{6,7},{7,6},{8,9},{9,8},{10,11... | collective-permute-start | bytes 417800 | tf_op jit(solution)/shard_map/ppermute | solution.py:120
  48.0 14.5 %collective-permute-start.26 = (f32[256,256]{1,0:T(8,128)S(1)}, f32[256,256]{1,0:T(8,128)S(1)}, u32[]{:S(2)}, u32[]{:S(2)}) collective-permute-start(f32[256,256]{1,0:T(8,128)S(1)} %pad_maximum_fusion.16), channel_id=1, source_target_pairs={{0,16},{1,17},{2,18},{3,19},{4,20},{5,21},{6,22},{7,23},{8,24},{9,... | collective-permute-start | bytes 786440 | tf_op jit(solution)/shard_map/ppermute | solution.py:120
  48.4 14.1 %collective-permute-start.23 = (f32[256,256]{1,0:T(8,128)S(1)}, f32[256,256]{1,0:T(8,128)S(1)}, u32[]{:S(2)}, u32[]{:S(2)}) collective-permute-start(f32[256,256]{1,0:T(8,128)S(1)} %pad_maximum_fusion.15), channel_id=1, source_target_pairs={{0,8},{1,9},{2,10},{3,11},{4,12},{5,13},{6,14},{7,15},{8,0},{9,1},... | collective-permute-start | bytes 786440 | tf_op jit(solution)/shard_map/ppermute | solution.py:120
  56.0 9.3 %collective-permute-start.20 = (f32[64,512]{1,0:T(8,128)S(1)}, f32[64,512]{1,0:T(8,128)S(1)}, u32[]{:S(2)}, u32[]{:S(2)}) collective-permute-start(f32[64,512]{1,0:T(8,128)S(1)} %pad_maximum_fusion.22), channel_id=1, source_target_pairs={{0,8},{1,9},{2,10},{3,11},{4,12},{5,13},{6,14},{7,15},{8,0},{9,1},... | collective-permute-start | bytes 393224 | tf_op jit(solution)/shard_map/ppermute | solution.py:120
  56.0 13.0 %collective-permute-start.21 = (f32[64,512]{1,0:T(8,128)S(1)}, f32[64,512]{1,0:T(8,128)S(1)}, u32[]{:S(2)}, u32[]{:S(2)}) collective-permute-start(f32[64,512]{1,0:T(8,128)S(1)} %pad_maximum_fusion.22), channel_id=1, source_target_pairs={{0,10},{1,11},{2,8},{3,9},{4,14},{5,15},{6,12},{7,13},{8,2},{9,3},... | collective-permute-start | bytes 393224 | tf_op jit(solution)/shard_map/ppermute | solution.py:120
  59.0 10.6 %collective-permute-start.19 = (f32[64,512]{1,0:T(8,128)S(1)}, f32[64,512]{1,0:T(8,128)S(1)}, u32[]{:S(2)}, u32[]{:S(2)}) collective-permute-start(f32[64,512]{1,0:T(8,128)S(1)} %slice.337), channel_id=1, source_target_pairs={{0,2},{1,3},{2,0},{3,1},{4,6},{5,7},{6,4},{7,5},{8,10},{9,11},{10,... | collective-permute-start | bytes 393224 | tf_op jit(solution)/shard_map/ppermute | solution.py:120
  62.7 16.7 %collective-permute-start.27 = (f32[512,256]{1,0:T(8,128)S(1)}, f32[512,256]{1,0:T(8,128)S(1)}, u32[]{:S(2)}, u32[]{:S(2)}) collective-permute-start(f32[512,256]{1,0:T(8,128)S(1)} %pad_maximum_fusion.13), channel_id=1, source_target_pairs={{0,8},{1,9},{2,10},{3,11},{4,12},{5,13},{6,14},{7,15},{8,0},{9,1},... | collective-permute-start | bytes 1572872 | tf_op jit(solution)/shard_map/ppermute | solution.py:120
  65.3 14.8 %collective-permute-start.28 = (f32[128,256]{1,0:T(8,128)S(1)}, f32[128,256]{1,0:T(8,128)S(1)}, u32[]{:S(2)}, u32[]{:S(2)}) collective-permute-start(f32[128,256]{1,0:T(8,128)S(1)} %fusion.39), channel_id=1, source_target_pairs={{0,1},{1,0},{2,3},{3,2},{4,5},{5,4},{6,7},{7,6},{8,9},{9,8},{10,11... | collective-permute-start | bytes 393224 | tf_op jit(solution)/shard_map/ppermute | solution.py:120
  69.0 12.8 %collective-permute-start.32 = (f32[64,512]{1,0:T(8,128)S(1)}, f32[64,512]{1,0:T(8,128)S(1)}, u32[]{:S(2)}, u32[]{:S(2)}) collective-permute-start(f32[64,512]{1,0:T(8,128)S(1)} %pad_maximum_fusion.23), channel_id=1, source_target_pairs={{0,8},{1,9},{2,10},{3,11},{4,12},{5,13},{6,14},{7,15},{8,0},{9,1},... | collective-permute-start | bytes 393224 | tf_op jit(solution)/shard_map/ppermute | solution.py:120
  69.6 12.2 %collective-permute-start.29 = (f32[128,256]{1,0:T(8,128)S(1)}, f32[128,256]{1,0:T(8,128)S(1)}, u32[]{:S(2)}, u32[]{:S(2)}) collective-permute-start(f32[128,256]{1,0:T(8,128)S(1)} %get-tuple-element.59), channel_id=1, source_target_pairs={{0,1},{1,0},{2,3},{3,2},{4,5},{5,4},{6,7},{7,6},{8,9},{9,8},{10,11... | collective-permute-start | bytes 393224 | tf_op jit(solution)/shard_map/ppermute | solution.py:120
  80.0 12.5 %collective-permute-start.36 = (f32[512,256]{1,0:T(8,128)S(1)}, f32[512,256]{1,0:T(8,128)S(1)}, u32[]{:S(2)}, u32[]{:S(2)}) collective-permute-start(f32[512,256]{1,0:T(8,128)S(1)} %pad_maximum_fusion.14), channel_id=1, source_target_pairs={{0,1},{1,0},{2,3},{3,2},{4,5},{5,4},{6,7},{7,6},{8,9},{9,8},{10,11... | collective-permute-start | bytes 1572872 | tf_op jit(solution)/shard_map/ppermute | solution.py:120
  83.3 9.2 %collective-permute-start.35 = (f32[32,512]{1,0:T(8,128)S(1)}, f32[32,512]{1,0:T(8,128)S(1)}, u32[]{:S(2)}, u32[]{:S(2)}) collective-permute-start(f32[32,512]{1,0:T(8,128)S(1)} %pad_maximum_fusion.29), channel_id=1, source_target_pairs={{0,18},{1,19},{2,16},{3,17},{4,22},{5,23},{6,20},{7,21},{8,26},{9,... | collective-permute-start | bytes 196616 | tf_op jit(solution)/shard_map/ppermute | solution.py:120
  132.6 13.7 %collective-permute-start.46 = (f32[128,128]{1,0:T(8,128)S(1)}, f32[128,128]{1,0:T(8,128)S(1)}, u32[]{:S(2)}, u32[]{:S(2)}) collective-permute-start(f32[128,128]{1,0:T(8,128)S(1)} %pad_maximum_fusion.31), channel_id=1, source_target_pairs={{0,16},{1,17},{2,18},{3,19},{4,20},{5,21},{6,22},{7,23},{8,24},{9,... | collective-permute-start | bytes 196616 | tf_op jit(solution)/shard_map/ppermute | solution.py:120
  (41 other events, 229.0 us)

commit v5 on v4

--- a/solution.py
+++ b/solution.py
@@ -202,7 +202,7 @@
             [pick(lower_blocks, index), jnp.pad(names, ((0, 7), (0, piece - panel)))], axis=0
         )
 
-    gate = diag_pieces[1]
+    gate = diag_pieces[3]
     lower_pieces = {0: tagged(first[last] + plane)}
     for o in range(1, planes):
         lower_pieces[o] = move(after(tagged(first[last] + (plane ^ o)), gate), plane_mask=o)
@@ -242,7 +242,7 @@
     def diag_block(depth, s):
         return pick(diag_inverse, first[depth] + ((plane >> shift[depth]) ^ s))
 
-    gate = lower_pieces[2]
+    gate = lower_pieces[3]
     far_diag = move(after(diag_block(1, 1), gate), plane_mask=2)
     held_diag = jnp.concatenate([diag_block(1, 0), far_diag], axis=0)
     near_diag = move(held_diag, plane_mask=1)

time: 152 us -> 147 us (0.967)
  starting transfers between devices: 56.2 us -> 47.9 us
  waiting for transfers between devices: 71.6 us -> 75.4 us
    ppermute x54, starting transfers between devices: 56.2 us -> 47.9 us  [move(): return lax.ppermute(x, AXES, pairs)]
    ppermute x54, waiting for transfers between devices: 71.6 us -> 75.4 us  [move(): return lax.ppermute(x, AXES, pairs)]
  transfers between devices with their start and end apart: 54 -> 54, of which waited for: 26 -> 29; matrix products, arithmetic and copies ran while one was open for 6% -> 6% of each run, Pallas kernels for 1% -> 1%
where the time goes in v5:
time: 147 us
  waiting for transfers between devices  75.4 us (51%)
  starting transfers between devices  47.9 us (33%)
  matrix products  13.3 us (9%)
  local copies, waits for them, and re-layouts  4.79 us (3%)
  Pallas kernels  4.63 us (3%)
    ppermute x54, waiting for transfers between devices, move(): return lax.ppermute(x, AXES, pairs)  75.4 us
    ppermute x54, starting transfers between devices, move(): return lax.ppermute(x, AXES, pairs)  47.9 us
    dot_general x12, matrix products, dot(): lax.dot_general(left, right, (dims, ((), ())), precision=PRECISION, prefe...  11.4 us
  transfers between devices with their start and end apart: 54, of which 29 were waited for; matrix products, arithmetic and copies ran while one was open for 6% of the time, Pallas kernels for 1%

profile of v5, /device:TPU:0, one launch (start us, length us, event | category | flops | bytes accessed | tf_op | source)
XLA Modules:
  0.0 147.3 jit_solution(11433233765746565276)
XLA Ops:
  1.3 5.1 %collective-permute-start.6 = (f32[128,256]{1,0:T(8,128)S(1)}, f32[128,256]{1,0:T(8,128)S(1)}, u32[]{:S(2)}, u32[]{:S(2)}) collective-permute-start(f32[128,256]{1,0:T(8,128)S(1)} %get-tuple-element.25), channel_id=1, source_target_pairs={{0,24},{1,25},{2,26},{3,27},{4,28},{5,29},{6,30},{7,31},{8,16},{9,... | collective-permute-start | bytes 393224 | tf_op jit(solution)/shard_map/ppermute | solution.py:120
  6.5 2.1 %pack.1 = (f32[224,128]{1,0:T(8,128)}, f32[112,128]{1,0:T(8,128)}, f32[112,128]{1,0:T(8,128)}, f32[112,128]{1,0:T(8,128)}) custom-call(f32[7,128,256]{2,1,0:T(8,128)} %rhs.1), custom_call_target="tpu_custom_call" | custom-call | tf_op jit(solution)/shard_map/pack/pallas_call | solution.py:159
  9.2 3.7 %collective-permute-start.2 = (f32[112,128]{1,0:T(8,128)}, f32[112,128]{1,0:T(8,128)S(1)}, u32[]{:S(2)}, u32[]{:S(2)}) collective-permute-start(f32[112,128]{1,0:T(8,128)} %get-tuple-element.17), channel_id=1, source_target_pairs={{0,24},{1,25},{2,26},{3,27},{4,28},{5,29},{6,30},{7,31},{8,16},{9,... | collective-permute-start | bytes 172040 | tf_op jit(solution)/shard_map/ppermute | solution.py:120
  15.0 4.8 %collective-permute-done.1 = f32[112,128]{1,0:T(8,128)S(1)} collective-permute-done((f32[112,128]{1,0:T(8,128)}, f32[112,128]{1,0:T(8,128)S(1)}, u32[]{:S(2)}, u32[]{:S(2)}) %collective-permute-start.1) | collective-permute-done | bytes 57376 | tf_op jit(solution)/shard_map/ppermute | solution.py:120
  23.2 3.4 %collective-permute-done.3 = f32[3,112,128]{2,1,0:T(8,128)S(1)} collective-permute-done((f32[3,112,128]{2,1,0:T(8,128)S(1)}, f32[3,112,128]{2,1,0:T(8,128)S(1)}, u32[]{:S(2)}, u32[]{:S(2)}) %collective-permute-start.3) | collective-permute-done | bytes 172064 | tf_op jit(solution)/shard_map/ppermute | solution.py:120
  32.1 4.9 %collective-permute-done.12 = f32[136,256]{1,0:T(8,128)S(1)} collective-permute-done((f32[136,256]{1,0:T(8,128)S(1)}, f32[136,256]{1,0:T(8,128)S(1)}, u32[]{:S(2)}, u32[]{:S(2)}) %collective-permute-start.12) | collective-permute-done | bytes 139296 | tf_op jit(solution)/shard_map/ppermute | solution.py:120
  37.7 4.5 %collective-permute-done.22 = f32[128,256]{1,0:T(8,128)S(1)} collective-permute-done((f32[128,256]{1,0:T(8,128)S(1)}, f32[128,256]{1,0:T(8,128)S(1)}, u32[]{:S(2)}, u32[]{:S(2)}) %collective-permute-start.22) | collective-permute-done | bytes 131104 | tf_op jit(solution)/shard_map/ppermute | solution.py:120
  46.7 3.8 %collective-permute-done.11 = f32[128,512]{1,0:T(8,128)S(1)} collective-permute-done((f32[128,512]{1,0:T(8,128)S(1)}, f32[128,512]{1,0:T(8,128)S(1)}, u32[]{:S(2)}, u32[]{:S(2)}) %collective-permute-start.11) | collective-permute-done | bytes 262176 | tf_op jit(solution)/shard_map/ppermute | solution.py:120
  51.8 2.9 %collective-permute-start.21 = (f32[64,512]{1,0:T(8,128)S(1)}, f32[64,512]{1,0:T(8,128)S(1)}, u32[]{:S(2)}, u32[]{:S(2)}) collective-permute-start(f32[64,512]{1,0:T(8,128)S(1)} %pad_maximum_fusion.22), channel_id=1, source_target_pairs={{0,10},{1,11},{2,8},{3,9},{4,14},{5,15},{6,12},{7,13},{8,2},{9,3},... | collective-permute-start | bytes 393224 | tf_op jit(solution)/shard_map/ppermute | solution.py:120
  56.6 2.1 %collective-permute-done.23 = f32[256,256]{1,0:T(8,128)S(1)} collective-permute-done((f32[256,256]{1,0:T(8,128)S(1)}, f32[256,256]{1,0:T(8,128)S(1)}, u32[]{:S(2)}, u32[]{:S(2)}) %collective-permute-start.23) | collective-permute-done | bytes 262176 | tf_op jit(solution)/shard_map/ppermute | solution.py:120
  59.0 2.5 %collective-permute-done.20 = f32[64,512]{1,0:T(8,128)S(1)} collective-permute-done((f32[64,512]{1,0:T(8,128)S(1)}, f32[64,512]{1,0:T(8,128)S(1)}, u32[]{:S(2)}, u32[]{:S(2)}) %collective-permute-start.20) | collective-permute-done | bytes 131104 | tf_op jit(solution)/shard_map/ppermute | solution.py:120
  61.5 3.6 %collective-permute-done.21 = f32[64,512]{1,0:T(8,128)S(1)} collective-permute-done((f32[64,512]{1,0:T(8,128)S(1)}, f32[64,512]{1,0:T(8,128)S(1)}, u32[]{:S(2)}, u32[]{:S(2)}) %collective-permute-start.21) | collective-permute-done | bytes 131104 | tf_op jit(solution)/shard_map/ppermute | solution.py:120
  66.5 8.9 %collective-permute-done.27 = f32[512,256]{1,0:T(8,128)S(1)} collective-permute-done((f32[512,256]{1,0:T(8,128)S(1)}, f32[512,256]{1,0:T(8,128)S(1)}, u32[]{:S(2)}, u32[]{:S(2)}) %collective-permute-start.27) | collective-permute-done | bytes 524320 | tf_op jit(solution)/shard_map/ppermute | solution.py:120
  78.4 3.8 %collective-permute-start.35 = (f32[32,512]{1,0:T(8,128)S(1)}, f32[32,512]{1,0:T(8,128)S(1)}, u32[]{:S(2)}, u32[]{:S(2)}) collective-permute-start(f32[32,512]{1,0:T(8,128)S(1)} %pad_maximum_fusion.29), channel_id=1, source_target_pairs={{0,18},{1,19},{2,16},{3,17},{4,22},{5,23},{6,20},{7,21},{8,26},{9,... | collective-permute-start | bytes 196616 | tf_op jit(solution)/shard_map/ppermute | solution.py:120
  82.8 2.6 %collective-permute-done.34 = f32[32,512]{1,0:T(8,128)S(1)} collective-permute-done((f32[32,512]{1,0:T(8,128)S(1)}, f32[32,512]{1,0:T(8,128)S(1)}, u32[]{:S(2)}, u32[]{:S(2)}) %collective-permute-start.34) | collective-permute-done | bytes 65568 | tf_op jit(solution)/shard_map/ppermute | solution.py:120
  85.4 2.7 %collective-permute-done.35 = f32[32,512]{1,0:T(8,128)S(1)} collective-permute-done((f32[32,512]{1,0:T(8,128)S(1)}, f32[32,512]{1,0:T(8,128)S(1)}, u32[]{:S(2)}, u32[]{:S(2)}) %collective-permute-start.35) | collective-permute-done | bytes 65568 | tf_op jit(solution)/shard_map/ppermute | solution.py:120
  89.4 3.8 %collective-permute-done.37 = f32[32,512]{1,0:T(8,128)S(1)} collective-permute-done((f32[32,512]{1,0:T(8,128)S(1)}, f32[32,512]{1,0:T(8,128)S(1)}, u32[]{:S(2)}, u32[]{:S(2)}) %collective-permute-start.37) | collective-permute-done | bytes 65568 | tf_op jit(solution)/shard_map/ppermute | solution.py:120
  95.0 3.6 %collective-permute-start.40 = (f32[32,512]{1,0:T(8,128)S(1)}, f32[32,512]{1,0:T(8,128)S(1)}, u32[]{:S(2)}, u32[]{:S(2)}) collective-permute-start(f32[32,512]{1,0:T(8,128)S(1)} %pad_maximum_fusion.30), channel_id=1, source_target_pairs={{0,18},{1,19},{2,16},{3,17},{4,22},{5,23},{6,20},{7,21},{8,26},{9,... | collective-permute-start | bytes 196616 | tf_op jit(solution)/shard_map/ppermute | solution.py:120
  103.2 4.5 %collective-permute-done.42 = f32[64,512]{1,0:T(8,128)S(1)} collective-permute-done((f32[64,512]{1,0:T(8,128)S(1)}, f32[64,512]{1,0:T(8,128)S(1)}, u32[]{:S(2)}, u32[]{:S(2)}) %collective-permute-start.42) | collective-permute-done | bytes 131104 | tf_op jit(solution)/shard_map/ppermute | solution.py:120
  115.2 2.5 %collective-permute-done.45 = f32[64,512]{1,0:T(8,128)S(1)} collective-permute-done((f32[64,512]{1,0:T(8,128)S(1)}, f32[64,512]{1,0:T(8,128)S(1)}, u32[]{:S(2)}, u32[]{:S(2)}) %collective-permute-start.45) | collective-permute-done | bytes 131104 | tf_op jit(solution)/shard_map/ppermute | solution.py:120
  119.9 5.8 %collective-permute-done.47 = f32[128,512]{1,0:T(8,128)S(1)} collective-permute-done((f32[128,512]{1,0:T(8,128)S(1)}, f32[128,512]{1,0:T(8,128)S(1)}, u32[]{:S(2)}, u32[]{:S(2)}) %collective-permute-start.47) | collective-permute-done | bytes 262176 | tf_op jit(solution)/shard_map/ppermute | solution.py:120
  129.6 3.6 %collective-permute-done.48 = f32[128,512]{1,0:T(8,128)S(1)} collective-permute-done((f32[128,512]{1,0:T(8,128)S(1)}, f32[128,512]{1,0:T(8,128)S(1)}, u32[]{:S(2)}, u32[]{:S(2)}) %collective-permute-start.48) | collective-permute-done | bytes 262176 | tf_op jit(solution)/shard_map/ppermute | solution.py:120
  133.3 2.3 %collective-permute-start.51 = (f32[128,128]{1,0:T(8,128)S(1)}, f32[128,128]{1,0:T(8,128)S(1)}, u32[]{:S(2)}, u32[]{:S(2)}) collective-permute-start(f32[128,128]{1,0:T(8,128)S(1)} %pad_maximum_fusion.34), channel_id=1, source_target_pairs={{0,24},{1,25},{2,26},{3,27},{4,28},{5,29},{6,30},{7,31},{8,16},{9,... | collective-permute-start | bytes 196616 | tf_op jit(solution)/shard_map/ppermute | solution.py:120
  144.7 2.5 %finish.1 = f32[7,128,256]{2,1,0:T(8,128)} custom-call(f32[128,128]{1,0:T(8,128)} %copy-done.1, f32[128,128]{1,0:T(8,128)} %copy-done.2, f32[128,128]{1,0:T(8,128)} %copy-done.4, f32[128,128]{1,0:T(8,128)} %get-tuple-element.44.refs_3_, f32[128,128]{1,0:T(8,128)} %copy-done.7, f32[128,128]{1,0:T(8,128)} %copy-done.6, f32[128,128]{1,0:T(8,128)} %copy-done.5, ...), custom_call_target="tpu_custom_call" | custom-call | tf_op jit(solution)/shard_map/finish/pallas_call | solution.py:304
  (185 shorter events, 56.7 us)
Async XLA Ops:
  1.3 20.1 %collective-permute-start.6 = (f32[128,256]{1,0:T(8,128)S(1)}, f32[128,256]{1,0:T(8,128)S(1)}, u32[]{:S(2)}, u32[]{:S(2)}) collective-permute-start(f32[128,256]{1,0:T(8,128)S(1)} %get-tuple-element.25), channel_id=1, source_target_pairs={{0,24},{1,25},{2,26},{3,27},{4,28},{5,29},{6,30},{7,31},{8,16},{9,... | collective-permute-start | bytes 393224 | tf_op jit(solution)/shard_map/ppermute | solution.py:120
  8.6 11.2 %collective-permute-start.1 = (f32[112,128]{1,0:T(8,128)}, f32[112,128]{1,0:T(8,128)S(1)}, u32[]{:S(2)}, u32[]{:S(2)}) collective-permute-start(f32[112,128]{1,0:T(8,128)} %get-tuple-element.16), channel_id=1, source_target_pairs={{0,16},{1,17},{2,18},{3,19},{4,20},{5,21},{6,22},{7,23},{8,24},{9,... | collective-permute-start | bytes 172040 | tf_op jit(solution)/shard_map/ppermute | solution.py:120
  9.2 10.6 %collective-permute-start.2 = (f32[112,128]{1,0:T(8,128)}, f32[112,128]{1,0:T(8,128)S(1)}, u32[]{:S(2)}, u32[]{:S(2)}) collective-permute-start(f32[112,128]{1,0:T(8,128)} %get-tuple-element.17), channel_id=1, source_target_pairs={{0,24},{1,25},{2,26},{3,27},{4,28},{5,29},{6,30},{7,31},{8,16},{9,... | collective-permute-start | bytes 172040 | tf_op jit(solution)/shard_map/ppermute | solution.py:120
  12.9 9.7 %collective-permute-start.4 = (f32[128,256]{1,0:T(8,128)S(1)}, f32[128,256]{1,0:T(8,128)S(1)}, u32[]{:S(2)}, u32[]{:S(2)}) collective-permute-start(f32[128,256]{1,0:T(8,128)S(1)} %get-tuple-element.27), channel_id=1, source_target_pairs={{0,16},{1,17},{2,18},{3,19},{4,20},{5,21},{6,22},{7,23},{8,24},{9,... | collective-permute-start | bytes 393224 | tf_op jit(solution)/shard_map/ppermute | solution.py:120
  14.3 8.5 %collective-permute-start.5 = (f32[128,256]{1,0:T(8,128)S(1)}, f32[128,256]{1,0:T(8,128)S(1)}, u32[]{:S(2)}, u32[]{:S(2)}) collective-permute-start(f32[128,256]{1,0:T(8,128)S(1)} %get-tuple-element.26), channel_id=1, source_target_pairs={{0,8},{1,9},{2,10},{3,11},{4,12},{5,13},{6,14},{7,15},{8,0},{9,1},... | collective-permute-start | bytes 393224 | tf_op jit(solution)/shard_map/ppermute | solution.py:120
  22.7 8.5 %collective-permute-start.10 = (f32[128,256]{1,0:T(8,128)S(1)}, f32[128,256]{1,0:T(8,128)S(1)}, u32[]{:S(2)}, u32[]{:S(2)}) collective-permute-start(f32[128,256]{1,0:T(8,128)S(1)} %collective-permute-done.6), channel_id=1, source_target_pairs={{0,1},{1,0},{2,3},{3,2},{4,5},{5,4},{6,7},{7,6},{8,9},{9,8},{10,11... | collective-permute-start | bytes 393224 | tf_op jit(solution)/shard_map/ppermute | solution.py:120
  22.7 8.5 %collective-permute-start.8 = (f32[128,256]{1,0:T(8,128)S(1)}, f32[128,256]{1,0:T(8,128)S(1)}, u32[]{:S(2)}, u32[]{:S(2)}) collective-permute-start(f32[128,256]{1,0:T(8,128)S(1)} %collective-permute-done.4), channel_id=1, source_target_pairs={{0,1},{1,0},{2,3},{3,2},{4,5},{5,4},{6,7},{7,6},{8,9},{9,8},{10,11... | collective-permute-start | bytes 393224 | tf_op jit(solution)/shard_map/ppermute | solution.py:120
  26.7 10.3 %collective-permute-start.12 = (f32[136,256]{1,0:T(8,128)S(1)}, f32[136,256]{1,0:T(8,128)S(1)}, u32[]{:S(2)}, u32[]{:S(2)}) collective-permute-start(f32[136,256]{1,0:T(8,128)S(1)} %get-tuple-element.18), channel_id=1, source_target_pairs={{0,16},{1,17},{2,18},{3,19},{4,20},{5,21},{6,22},{7,23},{8,24},{9,... | collective-permute-start | bytes 417800 | tf_op jit(solution)/shard_map/ppermute | solution.py:120
  31.2 12.6 %collective-permute-start.15 = (f32[1,136,256]{2,1,0:T(8,128)S(1)}, f32[1,136,256]{2,1,0:T(8,128)S(1)}, u32[]{:S(2)}, u32[]{:S(2)}) collective-permute-start(f32[1,136,256]{2,1,0:T(8,128)S(1)} %fusion.30), channel_id=1, source_target_pairs={{0,1},{1,0},{2,3},{3,2},{4,5},{5,4},{6,7},{7,6},{8,9},{9,8},{10,11... | collective-permute-start | bytes 417800 | tf_op jit(solution)/shard_map/ppermute | solution.py:120
  31.3 10.9 %collective-permute-start.22 = (f32[128,256]{1,0:T(8,128)S(1)}, f32[128,256]{1,0:T(8,128)S(1)}, u32[]{:S(2)}, u32[]{:S(2)}) collective-permute-start(f32[128,256]{1,0:T(8,128)S(1)} %get-tuple-element.21), channel_id=1, source_target_pairs={{0,16},{1,17},{2,18},{3,19},{4,20},{5,21},{6,22},{7,23},{8,24},{9,... | collective-permute-start | bytes 393224 | tf_op jit(solution)/shard_map/ppermute | solution.py:120
  42.2 8.3 %collective-permute-start.11 = (f32[128,512]{1,0:T(8,128)S(1)}, f32[128,512]{1,0:T(8,128)S(1)}, u32[]{:S(2)}, u32[]{:S(2)}) collective-permute-start(f32[128,512]{1,0:T(8,128)S(1)} %fusion.5), channel_id=1, source_target_pairs={{0,4},{1,5},{2,6},{3,7},{4,0},{5,1},{6,2},{7,3},{8,12},{9,13},{10,... | collective-permute-start | bytes 786440 | tf_op jit(solution)/shard_map/ppermute | solution.py:120
  43.7 15.1 %collective-permute-start.26 = (f32[256,256]{1,0:T(8,128)S(1)}, f32[256,256]{1,0:T(8,128)S(1)}, u32[]{:S(2)}, u32[]{:S(2)}) collective-permute-start(f32[256,256]{1,0:T(8,128)S(1)} %pad_maximum_fusion.16), channel_id=1, source_target_pairs={{0,16},{1,17},{2,18},{3,19},{4,20},{5,21},{6,22},{7,23},{8,24},{9,... | collective-permute-start | bytes 786440 | tf_op jit(solution)/shard_map/ppermute | solution.py:120
  43.8 14.8 %collective-permute-start.23 = (f32[256,256]{1,0:T(8,128)S(1)}, f32[256,256]{1,0:T(8,128)S(1)}, u32[]{:S(2)}, u32[]{:S(2)}) collective-permute-start(f32[256,256]{1,0:T(8,128)S(1)} %pad_maximum_fusion.15), channel_id=1, source_target_pairs={{0,8},{1,9},{2,10},{3,11},{4,12},{5,13},{6,14},{7,15},{8,0},{9,1},... | collective-permute-start | bytes 786440 | tf_op jit(solution)/shard_map/ppermute | solution.py:120
  51.7 9.8 %collective-permute-start.20 = (f32[64,512]{1,0:T(8,128)S(1)}, f32[64,512]{1,0:T(8,128)S(1)}, u32[]{:S(2)}, u32[]{:S(2)}) collective-permute-start(f32[64,512]{1,0:T(8,128)S(1)} %pad_maximum_fusion.22), channel_id=1, source_target_pairs={{0,8},{1,9},{2,10},{3,11},{4,12},{5,13},{6,14},{7,15},{8,0},{9,1},... | collective-permute-start | bytes 393224 | tf_op jit(solution)/shard_map/ppermute | solution.py:120
  51.8 13.3 %collective-permute-start.21 = (f32[64,512]{1,0:T(8,128)S(1)}, f32[64,512]{1,0:T(8,128)S(1)}, u32[]{:S(2)}, u32[]{:S(2)}) collective-permute-start(f32[64,512]{1,0:T(8,128)S(1)} %pad_maximum_fusion.22), channel_id=1, source_target_pairs={{0,10},{1,11},{2,8},{3,9},{4,14},{5,15},{6,12},{7,13},{8,2},{9,3},... | collective-permute-start | bytes 393224 | tf_op jit(solution)/shard_map/ppermute | solution.py:120
  54.7 10.4 %collective-permute-start.19 = (f32[64,512]{1,0:T(8,128)S(1)}, f32[64,512]{1,0:T(8,128)S(1)}, u32[]{:S(2)}, u32[]{:S(2)}) collective-permute-start(f32[64,512]{1,0:T(8,128)S(1)} %slice.337), channel_id=1, source_target_pairs={{0,2},{1,3},{2,0},{3,1},{4,6},{5,7},{6,4},{7,5},{8,10},{9,11},{10,... | collective-permute-start | bytes 393224 | tf_op jit(solution)/shard_map/ppermute | solution.py:120
  58.9 16.5 %collective-permute-start.27 = (f32[512,256]{1,0:T(8,128)S(1)}, f32[512,256]{1,0:T(8,128)S(1)}, u32[]{:S(2)}, u32[]{:S(2)}) collective-permute-start(f32[512,256]{1,0:T(8,128)S(1)} %pad_maximum_fusion.13), channel_id=1, source_target_pairs={{0,8},{1,9},{2,10},{3,11},{4,12},{5,13},{6,14},{7,15},{8,0},{9,1},... | collective-permute-start | bytes 1572872 | tf_op jit(solution)/shard_map/ppermute | solution.py:120
  61.5 14.6 %collective-permute-start.28 = (f32[128,256]{1,0:T(8,128)S(1)}, f32[128,256]{1,0:T(8,128)S(1)}, u32[]{:S(2)}, u32[]{:S(2)}) collective-permute-start(f32[128,256]{1,0:T(8,128)S(1)} %fusion.39), channel_id=1, source_target_pairs={{0,1},{1,0},{2,3},{3,2},{4,5},{5,4},{6,7},{7,6},{8,9},{9,8},{10,11... | collective-permute-start | bytes 393224 | tf_op jit(solution)/shard_map/ppermute | solution.py:120
  65.1 12.1 %collective-permute-start.32 = (f32[64,512]{1,0:T(8,128)S(1)}, f32[64,512]{1,0:T(8,128)S(1)}, u32[]{:S(2)}, u32[]{:S(2)}) collective-permute-start(f32[64,512]{1,0:T(8,128)S(1)} %pad_maximum_fusion.23), channel_id=1, source_target_pairs={{0,8},{1,9},{2,10},{3,11},{4,12},{5,13},{6,14},{7,15},{8,0},{9,1},... | collective-permute-start | bytes 393224 | tf_op jit(solution)/shard_map/ppermute | solution.py:120
  65.1 12.1 %collective-permute-start.29 = (f32[128,256]{1,0:T(8,128)S(1)}, f32[128,256]{1,0:T(8,128)S(1)}, u32[]{:S(2)}, u32[]{:S(2)}) collective-permute-start(f32[128,256]{1,0:T(8,128)S(1)} %get-tuple-element.59), channel_id=1, source_target_pairs={{0,1},{1,0},{2,3},{3,2},{4,5},{5,4},{6,7},{7,6},{8,9},{9,8},{10,11... | collective-permute-start | bytes 393224 | tf_op jit(solution)/shard_map/ppermute | solution.py:120
  65.9 9.6 %collective-permute-start.25 = (f32[64,512]{1,0:T(8,128)S(1)}, f32[64,512]{1,0:T(8,128)S(1)}, u32[]{:S(2)}, u32[]{:S(2)}) collective-permute-start(f32[64,512]{1,0:T(8,128)S(1)} %fusion.4), channel_id=1, source_target_pairs={{0,4},{1,5},{2,6},{3,7},{4,0},{5,1},{6,2},{7,3},{8,12},{9,13},{10,... | collective-permute-start | bytes 393224 | tf_op jit(solution)/shard_map/ppermute | solution.py:120
  76.1 11.9 %collective-permute-start.36 = (f32[512,256]{1,0:T(8,128)S(1)}, f32[512,256]{1,0:T(8,128)S(1)}, u32[]{:S(2)}, u32[]{:S(2)}) collective-permute-start(f32[512,256]{1,0:T(8,128)S(1)} %pad_maximum_fusion.14), channel_id=1, source_target_pairs={{0,1},{1,0},{2,3},{3,2},{4,5},{5,4},{6,7},{7,6},{8,9},{9,8},{10,11... | collective-permute-start | bytes 1572872 | tf_op jit(solution)/shard_map/ppermute | solution.py:120
  78.4 9.6 %collective-permute-start.35 = (f32[32,512]{1,0:T(8,128)S(1)}, f32[32,512]{1,0:T(8,128)S(1)}, u32[]{:S(2)}, u32[]{:S(2)}) collective-permute-start(f32[32,512]{1,0:T(8,128)S(1)} %pad_maximum_fusion.29), channel_id=1, source_target_pairs={{0,18},{1,19},{2,16},{3,17},{4,22},{5,23},{6,20},{7,21},{8,26},{9,... | collective-permute-start | bytes 196616 | tf_op jit(solution)/shard_map/ppermute | solution.py:120
  128.0 13.7 %collective-permute-start.46 = (f32[128,128]{1,0:T(8,128)S(1)}, f32[128,128]{1,0:T(8,128)S(1)}, u32[]{:S(2)}, u32[]{:S(2)}) collective-permute-start(f32[128,128]{1,0:T(8,128)S(1)} %pad_maximum_fusion.31), channel_id=1, source_target_pairs={{0,16},{1,17},{2,18},{3,19},{4,20},{5,21},{6,22},{7,23},{8,24},{9,... | collective-permute-start | bytes 196616 | tf_op jit(solution)/shard_map/ppermute | solution.py:120
  (41 other events, 221.0 us)

commit v6 on v5

--- a/solution.py
+++ b/solution.py
@@ -202,7 +202,7 @@
             [pick(lower_blocks, index), jnp.pad(names, ((0, 7), (0, piece - panel)))], axis=0
         )
 
-    gate = diag_pieces[3]
+    gate = diag_pieces[2]
     lower_pieces = {0: tagged(first[last] + plane)}
     for o in range(1, planes):
         lower_pieces[o] = move(after(tagged(first[last] + (plane ^ o)), gate), plane_mask=o)

time: 147 us -> 148 us (level)
  starting transfers between devices: 47.9 us -> 58.4 us
  waiting for transfers between devices: 75.4 us -> 65.7 us
    ppermute x54, starting transfers between devices: 47.9 us -> 58.4 us  [move(): return lax.ppermute(x, AXES, pairs)]
    ppermute x54, waiting for transfers between devices: 75.4 us -> 65.7 us  [move(): return lax.ppermute(x, AXES, pairs)]
  transfers between devices with their start and end apart: 54 -> 54, of which waited for: 29 -> 25; matrix products, arithmetic and copies ran while one was open for 6% -> 6% of each run, Pallas kernels for 1% -> 1%
where the time goes in v6:
time: 148 us
  waiting for transfers between devices  65.7 us (44%)
  starting transfers between devices  58.4 us (39%)
  matrix products  13.3 us (9%)
  local copies, waits for them, and re-layouts  4.79 us (3%)
  Pallas kernels  4.63 us (3%)
    ppermute x54, waiting for transfers between devices, move(): return lax.ppermute(x, AXES, pairs)  65.7 us
    ppermute x54, starting transfers between devices, move(): return lax.ppermute(x, AXES, pairs)  58.4 us
    dot_general x12, matrix products, dot(): lax.dot_general(left, right, (dims, ((), ())), precision=PRECISION, prefe...  11.4 us
  transfers between devices with their start and end apart: 54, of which 25 were waited for; matrix products, arithmetic and copies ran while one was open for 6% of the time, Pallas kernels for 1%

profile of v6, /device:TPU:0, one launch (start us, length us, event | category | flops | bytes accessed | tf_op | source)
XLA Modules:
  0.0 148.1 jit_solution(18319863249117324938)
XLA Ops:
  1.3 4.1 %collective-permute-start.4 = (f32[128,256]{1,0:T(8,128)S(1)}, f32[128,256]{1,0:T(8,128)S(1)}, u32[]{:S(2)}, u32[]{:S(2)}) collective-permute-start(f32[128,256]{1,0:T(8,128)S(1)} %get-tuple-element.27), channel_id=1, source_target_pairs={{0,16},{1,17},{2,18},{3,19},{4,20},{5,21},{6,22},{7,23},{8,24},{9,... | collective-permute-start | bytes 393224 | tf_op jit(solution)/shard_map/ppermute | solution.py:120
  5.4 2.1 %pack.1 = (f32[224,128]{1,0:T(8,128)}, f32[112,128]{1,0:T(8,128)}, f32[112,128]{1,0:T(8,128)}, f32[112,128]{1,0:T(8,128)}) custom-call(f32[7,128,256]{2,1,0:T(8,128)} %rhs.1), custom_call_target="tpu_custom_call" | custom-call | tf_op jit(solution)/shard_map/pack/pallas_call | solution.py:159
  9.5 2.5 %collective-permute-start.2 = (f32[112,128]{1,0:T(8,128)}, f32[112,128]{1,0:T(8,128)S(1)}, u32[]{:S(2)}, u32[]{:S(2)}) collective-permute-start(f32[112,128]{1,0:T(8,128)} %get-tuple-element.17), channel_id=1, source_target_pairs={{0,24},{1,25},{2,26},{3,27},{4,28},{5,29},{6,30},{7,31},{8,16},{9,... | collective-permute-start | bytes 172040 | tf_op jit(solution)/shard_map/ppermute | solution.py:120
  14.7 3.5 %collective-permute-done.1 = f32[112,128]{1,0:T(8,128)S(1)} collective-permute-done((f32[112,128]{1,0:T(8,128)}, f32[112,128]{1,0:T(8,128)S(1)}, u32[]{:S(2)}, u32[]{:S(2)}) %collective-permute-start.1) | collective-permute-done | bytes 57376 | tf_op jit(solution)/shard_map/ppermute | solution.py:120
  19.8 3.8 %collective-permute-start.14 = (f32[136,256]{1,0:T(8,128)S(1)}, f32[136,256]{1,0:T(8,128)S(1)}, u32[]{:S(2)}, u32[]{:S(2)}) collective-permute-start(f32[136,256]{1,0:T(8,128)S(1)} %select_maximum_fusion), channel_id=1, source_target_pairs={{0,24},{1,25},{2,26},{3,27},{4,28},{5,29},{6,30},{7,31},{8,16},{9,... | collective-permute-start | bytes 417800 | tf_op jit(solution)/shard_map/ppermute | solution.py:120
  25.1 3.6 %collective-permute-start.12 = (f32[136,256]{1,0:T(8,128)S(1)}, f32[136,256]{1,0:T(8,128)S(1)}, u32[]{:S(2)}, u32[]{:S(2)}) collective-permute-start(f32[136,256]{1,0:T(8,128)S(1)} %get-tuple-element.18), channel_id=1, source_target_pairs={{0,16},{1,17},{2,18},{3,19},{4,20},{5,21},{6,22},{7,23},{8,24},{9,... | collective-permute-start | bytes 417800 | tf_op jit(solution)/shard_map/ppermute | solution.py:120
  28.7 5.7 %collective-permute-start.13 = (f32[136,256]{1,0:T(8,128)S(1)}, f32[136,256]{1,0:T(8,128)S(1)}, u32[]{:S(2)}, u32[]{:S(2)}) collective-permute-start(f32[136,256]{1,0:T(8,128)S(1)} %get-tuple-element.19), channel_id=1, source_target_pairs={{0,8},{1,9},{2,10},{3,11},{4,12},{5,13},{6,14},{7,15},{8,0},{9,1},... | collective-permute-start | bytes 417800 | tf_op jit(solution)/shard_map/ppermute | solution.py:120
  38.8 4.8 %collective-permute-done.22 = f32[128,256]{1,0:T(8,128)S(1)} collective-permute-done((f32[128,256]{1,0:T(8,128)S(1)}, f32[128,256]{1,0:T(8,128)S(1)}, u32[]{:S(2)}, u32[]{:S(2)}) %collective-permute-start.22) | collective-permute-done | bytes 131104 | tf_op jit(solution)/shard_map/ppermute | solution.py:120
  48.3 3.5 %collective-permute-done.11 = f32[128,512]{1,0:T(8,128)S(1)} collective-permute-done((f32[128,512]{1,0:T(8,128)S(1)}, f32[128,512]{1,0:T(8,128)S(1)}, u32[]{:S(2)}, u32[]{:S(2)}) %collective-permute-start.11) | collective-permute-done | bytes 262176 | tf_op jit(solution)/shard_map/ppermute | solution.py:120
  54.1 2.6 %collective-permute-start.19 = (f32[64,512]{1,0:T(8,128)S(1)}, f32[64,512]{1,0:T(8,128)S(1)}, u32[]{:S(2)}, u32[]{:S(2)}) collective-permute-start(f32[64,512]{1,0:T(8,128)S(1)} %slice.337), channel_id=1, source_target_pairs={{0,2},{1,3},{2,0},{3,1},{4,6},{5,7},{6,4},{7,5},{8,10},{9,11},{10,... | collective-permute-start | bytes 393224 | tf_op jit(solution)/shard_map/ppermute | solution.py:120
  60.3 2.2 %collective-permute-done.20 = f32[64,512]{1,0:T(8,128)S(1)} collective-permute-done((f32[64,512]{1,0:T(8,128)S(1)}, f32[64,512]{1,0:T(8,128)S(1)}, u32[]{:S(2)}, u32[]{:S(2)}) %collective-permute-start.20) | collective-permute-done | bytes 131104 | tf_op jit(solution)/shard_map/ppermute | solution.py:120
  62.4 2.3 %collective-permute-done.21 = f32[64,512]{1,0:T(8,128)S(1)} collective-permute-done((f32[64,512]{1,0:T(8,128)S(1)}, f32[64,512]{1,0:T(8,128)S(1)}, u32[]{:S(2)}, u32[]{:S(2)}) %collective-permute-start.21) | collective-permute-done | bytes 131104 | tf_op jit(solution)/shard_map/ppermute | solution.py:120
  66.2 10.3 %collective-permute-done.27 = f32[512,256]{1,0:T(8,128)S(1)} collective-permute-done((f32[512,256]{1,0:T(8,128)S(1)}, f32[512,256]{1,0:T(8,128)S(1)}, u32[]{:S(2)}, u32[]{:S(2)}) %collective-permute-start.27) | collective-permute-done | bytes 524320 | tf_op jit(solution)/shard_map/ppermute | solution.py:120
  79.8 2.8 %collective-permute-start.35 = (f32[32,512]{1,0:T(8,128)S(1)}, f32[32,512]{1,0:T(8,128)S(1)}, u32[]{:S(2)}, u32[]{:S(2)}) collective-permute-start(f32[32,512]{1,0:T(8,128)S(1)} %pad_maximum_fusion.29), channel_id=1, source_target_pairs={{0,18},{1,19},{2,16},{3,17},{4,22},{5,23},{6,20},{7,21},{8,26},{9,... | collective-permute-start | bytes 196616 | tf_op jit(solution)/shard_map/ppermute | solution.py:120
  84.2 3.2 %collective-permute-done.34 = f32[32,512]{1,0:T(8,128)S(1)} collective-permute-done((f32[32,512]{1,0:T(8,128)S(1)}, f32[32,512]{1,0:T(8,128)S(1)}, u32[]{:S(2)}, u32[]{:S(2)}) %collective-permute-start.34) | collective-permute-done | bytes 65568 | tf_op jit(solution)/shard_map/ppermute | solution.py:120
  89.3 3.5 %collective-permute-done.37 = f32[32,512]{1,0:T(8,128)S(1)} collective-permute-done((f32[32,512]{1,0:T(8,128)S(1)}, f32[32,512]{1,0:T(8,128)S(1)}, u32[]{:S(2)}, u32[]{:S(2)}) %collective-permute-start.37) | collective-permute-done | bytes 65568 | tf_op jit(solution)/shard_map/ppermute | solution.py:120
  93.9 2.3 %collective-permute-start.38 = (f32[32,512]{1,0:T(8,128)S(1)}, f32[32,512]{1,0:T(8,128)S(1)}, u32[]{:S(2)}, u32[]{:S(2)}) collective-permute-start(f32[32,512]{1,0:T(8,128)S(1)} %fusion.1), channel_id=1, source_target_pairs={{0,2},{1,3},{2,0},{3,1},{4,6},{5,7},{6,4},{7,5},{8,10},{9,11},{10,... | collective-permute-start | bytes 196616 | tf_op jit(solution)/shard_map/ppermute | solution.py:120
  96.2 2.4 %collective-permute-start.40 = (f32[32,512]{1,0:T(8,128)S(1)}, f32[32,512]{1,0:T(8,128)S(1)}, u32[]{:S(2)}, u32[]{:S(2)}) collective-permute-start(f32[32,512]{1,0:T(8,128)S(1)} %pad_maximum_fusion.30), channel_id=1, source_target_pairs={{0,18},{1,19},{2,16},{3,17},{4,22},{5,23},{6,20},{7,21},{8,26},{9,... | collective-permute-start | bytes 196616 | tf_op jit(solution)/shard_map/ppermute | solution.py:120
  98.7 3.0 %collective-permute-done.39 = f32[32,512]{1,0:T(8,128)S(1)} collective-permute-done((f32[32,512]{1,0:T(8,128)S(1)}, f32[32,512]{1,0:T(8,128)S(1)}, u32[]{:S(2)}, u32[]{:S(2)}) %collective-permute-start.39) | collective-permute-done | bytes 65568 | tf_op jit(solution)/shard_map/ppermute | solution.py:120
  104.0 4.6 %collective-permute-done.42 = f32[64,512]{1,0:T(8,128)S(1)} collective-permute-done((f32[64,512]{1,0:T(8,128)S(1)}, f32[64,512]{1,0:T(8,128)S(1)}, u32[]{:S(2)}, u32[]{:S(2)}) %collective-permute-start.42) | collective-permute-done | bytes 131104 | tf_op jit(solution)/shard_map/ppermute | solution.py:120
  120.9 5.8 %collective-permute-done.47 = f32[128,512]{1,0:T(8,128)S(1)} collective-permute-done((f32[128,512]{1,0:T(8,128)S(1)}, f32[128,512]{1,0:T(8,128)S(1)}, u32[]{:S(2)}, u32[]{:S(2)}) %collective-permute-start.47) | collective-permute-done | bytes 262176 | tf_op jit(solution)/shard_map/ppermute | solution.py:120
  130.7 3.6 %collective-permute-done.48 = f32[128,512]{1,0:T(8,128)S(1)} collective-permute-done((f32[128,512]{1,0:T(8,128)S(1)}, f32[128,512]{1,0:T(8,128)S(1)}, u32[]{:S(2)}, u32[]{:S(2)}) %collective-permute-start.48) | collective-permute-done | bytes 262176 | tf_op jit(solution)/shard_map/ppermute | solution.py:120
  134.4 2.3 %collective-permute-start.51 = (f32[128,128]{1,0:T(8,128)S(1)}, f32[128,128]{1,0:T(8,128)S(1)}, u32[]{:S(2)}, u32[]{:S(2)}) collective-permute-start(f32[128,128]{1,0:T(8,128)S(1)} %pad_maximum_fusion.34), channel_id=1, source_target_pairs={{0,24},{1,25},{2,26},{3,27},{4,28},{5,29},{6,30},{7,31},{8,16},{9,... | collective-permute-start | bytes 196616 | tf_op jit(solution)/shard_map/ppermute | solution.py:120
  145.6 2.5 %finish.1 = f32[7,128,256]{2,1,0:T(8,128)} custom-call(f32[128,128]{1,0:T(8,128)} %copy-done.1, f32[128,128]{1,0:T(8,128)} %copy-done.2, f32[128,128]{1,0:T(8,128)} %copy-done.4, f32[128,128]{1,0:T(8,128)} %get-tuple-element.44.refs_3_, f32[128,128]{1,0:T(8,128)} %copy-done.7, f32[128,128]{1,0:T(8,128)} %copy-done.6, f32[128,128]{1,0:T(8,128)} %copy-done.5, ...), custom_call_target="tpu_custom_call" | custom-call | tf_op jit(solution)/shard_map/finish/pallas_call | solution.py:304
  (185 shorter events, 60.5 us)
Async XLA Ops:
  1.3 18.5 %collective-permute-start.4 = (f32[128,256]{1,0:T(8,128)S(1)}, f32[128,256]{1,0:T(8,128)S(1)}, u32[]{:S(2)}, u32[]{:S(2)}) collective-permute-start(f32[128,256]{1,0:T(8,128)S(1)} %get-tuple-element.27), channel_id=1, source_target_pairs={{0,16},{1,17},{2,18},{3,19},{4,20},{5,21},{6,22},{7,23},{8,24},{9,... | collective-permute-start | bytes 393224 | tf_op jit(solution)/shard_map/ppermute | solution.py:120
  9.1 9.0 %collective-permute-start.1 = (f32[112,128]{1,0:T(8,128)}, f32[112,128]{1,0:T(8,128)S(1)}, u32[]{:S(2)}, u32[]{:S(2)}) collective-permute-start(f32[112,128]{1,0:T(8,128)} %get-tuple-element.16), channel_id=1, source_target_pairs={{0,16},{1,17},{2,18},{3,19},{4,20},{5,21},{6,22},{7,23},{8,24},{9,... | collective-permute-start | bytes 172040 | tf_op jit(solution)/shard_map/ppermute | solution.py:120
  11.9 11.7 %collective-permute-start.6 = (f32[128,256]{1,0:T(8,128)S(1)}, f32[128,256]{1,0:T(8,128)S(1)}, u32[]{:S(2)}, u32[]{:S(2)}) collective-permute-start(f32[128,256]{1,0:T(8,128)S(1)} %get-tuple-element.25), channel_id=1, source_target_pairs={{0,24},{1,25},{2,26},{3,27},{4,28},{5,29},{6,30},{7,31},{8,16},{9,... | collective-permute-start | bytes 393224 | tf_op jit(solution)/shard_map/ppermute | solution.py:120
  14.6 9.0 %collective-permute-start.5 = (f32[128,256]{1,0:T(8,128)S(1)}, f32[128,256]{1,0:T(8,128)S(1)}, u32[]{:S(2)}, u32[]{:S(2)}) collective-permute-start(f32[128,256]{1,0:T(8,128)S(1)} %get-tuple-element.26), channel_id=1, source_target_pairs={{0,8},{1,9},{2,10},{3,11},{4,12},{5,13},{6,14},{7,15},{8,0},{9,1},... | collective-permute-start | bytes 393224 | tf_op jit(solution)/shard_map/ppermute | solution.py:120
  19.8 8.9 %collective-permute-start.14 = (f32[136,256]{1,0:T(8,128)S(1)}, f32[136,256]{1,0:T(8,128)S(1)}, u32[]{:S(2)}, u32[]{:S(2)}) collective-permute-start(f32[136,256]{1,0:T(8,128)S(1)} %select_maximum_fusion), channel_id=1, source_target_pairs={{0,24},{1,25},{2,26},{3,27},{4,28},{5,29},{6,30},{7,31},{8,16},{9,... | collective-permute-start | bytes 417800 | tf_op jit(solution)/shard_map/ppermute | solution.py:120
  23.7 10.8 %collective-permute-start.8 = (f32[128,256]{1,0:T(8,128)S(1)}, f32[128,256]{1,0:T(8,128)S(1)}, u32[]{:S(2)}, u32[]{:S(2)}) collective-permute-start(f32[128,256]{1,0:T(8,128)S(1)} %collective-permute-done.4), channel_id=1, source_target_pairs={{0,1},{1,0},{2,3},{3,2},{4,5},{5,4},{6,7},{7,6},{8,9},{9,8},{10,11... | collective-permute-start | bytes 393224 | tf_op jit(solution)/shard_map/ppermute | solution.py:120
  23.7 10.7 %collective-permute-start.10 = (f32[128,256]{1,0:T(8,128)S(1)}, f32[128,256]{1,0:T(8,128)S(1)}, u32[]{:S(2)}, u32[]{:S(2)}) collective-permute-start(f32[128,256]{1,0:T(8,128)S(1)} %collective-permute-done.6), channel_id=1, source_target_pairs={{0,1},{1,0},{2,3},{3,2},{4,5},{5,4},{6,7},{7,6},{8,9},{9,8},{10,11... | collective-permute-start | bytes 393224 | tf_op jit(solution)/shard_map/ppermute | solution.py:120
  25.0 9.5 %collective-permute-start.9 = (f32[128,256]{1,0:T(8,128)S(1)}, f32[128,256]{1,0:T(8,128)S(1)}, u32[]{:S(2)}, u32[]{:S(2)}) collective-permute-start(f32[128,256]{1,0:T(8,128)S(1)} %collective-permute-done.5), channel_id=1, source_target_pairs={{0,1},{1,0},{2,3},{3,2},{4,5},{5,4},{6,7},{7,6},{8,9},{9,8},{10,11... | collective-permute-start | bytes 393224 | tf_op jit(solution)/shard_map/ppermute | solution.py:120
  25.1 11.3 %collective-permute-start.12 = (f32[136,256]{1,0:T(8,128)S(1)}, f32[136,256]{1,0:T(8,128)S(1)}, u32[]{:S(2)}, u32[]{:S(2)}) collective-permute-start(f32[136,256]{1,0:T(8,128)S(1)} %get-tuple-element.18), channel_id=1, source_target_pairs={{0,16},{1,17},{2,18},{3,19},{4,20},{5,21},{6,22},{7,23},{8,24},{9,... | collective-permute-start | bytes 417800 | tf_op jit(solution)/shard_map/ppermute | solution.py:120
  28.7 9.6 %collective-permute-start.13 = (f32[136,256]{1,0:T(8,128)S(1)}, f32[136,256]{1,0:T(8,128)S(1)}, u32[]{:S(2)}, u32[]{:S(2)}) collective-permute-start(f32[136,256]{1,0:T(8,128)S(1)} %get-tuple-element.19), channel_id=1, source_target_pairs={{0,8},{1,9},{2,10},{3,11},{4,12},{5,13},{6,14},{7,15},{8,0},{9,1},... | collective-permute-start | bytes 417800 | tf_op jit(solution)/shard_map/ppermute | solution.py:120
  34.4 10.7 %collective-permute-start.15 = (f32[1,136,256]{2,1,0:T(8,128)S(1)}, f32[1,136,256]{2,1,0:T(8,128)S(1)}, u32[]{:S(2)}, u32[]{:S(2)}) collective-permute-start(f32[1,136,256]{2,1,0:T(8,128)S(1)} %fusion.30), channel_id=1, source_target_pairs={{0,1},{1,0},{2,3},{3,2},{4,5},{5,4},{6,7},{7,6},{8,9},{9,8},{10,11... | collective-permute-start | bytes 417800 | tf_op jit(solution)/shard_map/ppermute | solution.py:120
  34.5 9.1 %collective-permute-start.22 = (f32[128,256]{1,0:T(8,128)S(1)}, f32[128,256]{1,0:T(8,128)S(1)}, u32[]{:S(2)}, u32[]{:S(2)}) collective-permute-start(f32[128,256]{1,0:T(8,128)S(1)} %get-tuple-element.21), channel_id=1, source_target_pairs={{0,16},{1,17},{2,18},{3,19},{4,20},{5,21},{6,22},{7,23},{8,24},{9,... | collective-permute-start | bytes 393224 | tf_op jit(solution)/shard_map/ppermute | solution.py:120
  45.1 14.7 %collective-permute-start.26 = (f32[256,256]{1,0:T(8,128)S(1)}, f32[256,256]{1,0:T(8,128)S(1)}, u32[]{:S(2)}, u32[]{:S(2)}) collective-permute-start(f32[256,256]{1,0:T(8,128)S(1)} %pad_maximum_fusion.16), channel_id=1, source_target_pairs={{0,16},{1,17},{2,18},{3,19},{4,20},{5,21},{6,22},{7,23},{8,24},{9,... | collective-permute-start | bytes 786440 | tf_op jit(solution)/shard_map/ppermute | solution.py:120
  45.2 14.5 %collective-permute-start.23 = (f32[256,256]{1,0:T(8,128)S(1)}, f32[256,256]{1,0:T(8,128)S(1)}, u32[]{:S(2)}, u32[]{:S(2)}) collective-permute-start(f32[256,256]{1,0:T(8,128)S(1)} %pad_maximum_fusion.15), channel_id=1, source_target_pairs={{0,8},{1,9},{2,10},{3,11},{4,12},{5,13},{6,14},{7,15},{8,0},{9,1},... | collective-permute-start | bytes 786440 | tf_op jit(solution)/shard_map/ppermute | solution.py:120
  53.1 9.4 %collective-permute-start.20 = (f32[64,512]{1,0:T(8,128)S(1)}, f32[64,512]{1,0:T(8,128)S(1)}, u32[]{:S(2)}, u32[]{:S(2)}) collective-permute-start(f32[64,512]{1,0:T(8,128)S(1)} %pad_maximum_fusion.22), channel_id=1, source_target_pairs={{0,8},{1,9},{2,10},{3,11},{4,12},{5,13},{6,14},{7,15},{8,0},{9,1},... | collective-permute-start | bytes 393224 | tf_op jit(solution)/shard_map/ppermute | solution.py:120
  53.1 11.6 %collective-permute-start.21 = (f32[64,512]{1,0:T(8,128)S(1)}, f32[64,512]{1,0:T(8,128)S(1)}, u32[]{:S(2)}, u32[]{:S(2)}) collective-permute-start(f32[64,512]{1,0:T(8,128)S(1)} %pad_maximum_fusion.22), channel_id=1, source_target_pairs={{0,10},{1,11},{2,8},{3,9},{4,14},{5,15},{6,12},{7,13},{8,2},{9,3},... | collective-permute-start | bytes 393224 | tf_op jit(solution)/shard_map/ppermute | solution.py:120
  54.1 10.7 %collective-permute-start.19 = (f32[64,512]{1,0:T(8,128)S(1)}, f32[64,512]{1,0:T(8,128)S(1)}, u32[]{:S(2)}, u32[]{:S(2)}) collective-permute-start(f32[64,512]{1,0:T(8,128)S(1)} %slice.337), channel_id=1, source_target_pairs={{0,2},{1,3},{2,0},{3,1},{4,6},{5,7},{6,4},{7,5},{8,10},{9,11},{10,... | collective-permute-start | bytes 393224 | tf_op jit(solution)/shard_map/ppermute | solution.py:120
  59.8 16.7 %collective-permute-start.27 = (f32[512,256]{1,0:T(8,128)S(1)}, f32[512,256]{1,0:T(8,128)S(1)}, u32[]{:S(2)}, u32[]{:S(2)}) collective-permute-start(f32[512,256]{1,0:T(8,128)S(1)} %pad_maximum_fusion.13), channel_id=1, source_target_pairs={{0,8},{1,9},{2,10},{3,11},{4,12},{5,13},{6,14},{7,15},{8,0},{9,1},... | collective-permute-start | bytes 1572872 | tf_op jit(solution)/shard_map/ppermute | solution.py:120
  62.4 14.8 %collective-permute-start.28 = (f32[128,256]{1,0:T(8,128)S(1)}, f32[128,256]{1,0:T(8,128)S(1)}, u32[]{:S(2)}, u32[]{:S(2)}) collective-permute-start(f32[128,256]{1,0:T(8,128)S(1)} %fusion.39), channel_id=1, source_target_pairs={{0,1},{1,0},{2,3},{3,2},{4,5},{5,4},{6,7},{7,6},{8,9},{9,8},{10,11... | collective-permute-start | bytes 393224 | tf_op jit(solution)/shard_map/ppermute | solution.py:120
  64.8 13.7 %collective-permute-start.32 = (f32[64,512]{1,0:T(8,128)S(1)}, f32[64,512]{1,0:T(8,128)S(1)}, u32[]{:S(2)}, u32[]{:S(2)}) collective-permute-start(f32[64,512]{1,0:T(8,128)S(1)} %pad_maximum_fusion.23), channel_id=1, source_target_pairs={{0,8},{1,9},{2,10},{3,11},{4,12},{5,13},{6,14},{7,15},{8,0},{9,1},... | collective-permute-start | bytes 393224 | tf_op jit(solution)/shard_map/ppermute | solution.py:120
  64.8 13.7 %collective-permute-start.29 = (f32[128,256]{1,0:T(8,128)S(1)}, f32[128,256]{1,0:T(8,128)S(1)}, u32[]{:S(2)}, u32[]{:S(2)}) collective-permute-start(f32[128,256]{1,0:T(8,128)S(1)} %get-tuple-element.59), channel_id=1, source_target_pairs={{0,1},{1,0},{2,3},{3,2},{4,5},{5,4},{6,7},{7,6},{8,9},{9,8},{10,11... | collective-permute-start | bytes 393224 | tf_op jit(solution)/shard_map/ppermute | solution.py:120
  65.6 11.0 %collective-permute-start.25 = (f32[64,512]{1,0:T(8,128)S(1)}, f32[64,512]{1,0:T(8,128)S(1)}, u32[]{:S(2)}, u32[]{:S(2)}) collective-permute-start(f32[64,512]{1,0:T(8,128)S(1)} %fusion.4), channel_id=1, source_target_pairs={{0,4},{1,5},{2,6},{3,7},{4,0},{5,1},{6,2},{7,3},{8,12},{9,13},{10,... | collective-permute-start | bytes 393224 | tf_op jit(solution)/shard_map/ppermute | solution.py:120
  77.2 10.6 %collective-permute-start.36 = (f32[512,256]{1,0:T(8,128)S(1)}, f32[512,256]{1,0:T(8,128)S(1)}, u32[]{:S(2)}, u32[]{:S(2)}) collective-permute-start(f32[512,256]{1,0:T(8,128)S(1)} %pad_maximum_fusion.14), channel_id=1, source_target_pairs={{0,1},{1,0},{2,3},{3,2},{4,5},{5,4},{6,7},{7,6},{8,9},{9,8},{10,11... | collective-permute-start | bytes 1572872 | tf_op jit(solution)/shard_map/ppermute | solution.py:120
  128.8 13.8 %collective-permute-start.46 = (f32[128,128]{1,0:T(8,128)S(1)}, f32[128,128]{1,0:T(8,128)S(1)}, u32[]{:S(2)}, u32[]{:S(2)}) collective-permute-start(f32[128,128]{1,0:T(8,128)S(1)} %pad_maximum_fusion.31), channel_id=1, source_target_pairs={{0,16},{1,17},{2,18},{3,19},{4,20},{5,21},{6,22},{7,23},{8,24},{9,... | collective-permute-start | bytes 196616 | tf_op jit(solution)/shard_map/ppermute | solution.py:120
  (41 other events, 227.9 us)
